TPU v7x, 32 devices: a whole 2x2x4 slice. The times are simulated.
32 devices in a mesh: dp: 8 (over y, x, core), ctx: 4 (over z).
Axes of the slice: x: 2, y: 2, z: 4, core: 2. Of those that a mesh axis runs over, the one named last changes fastest.
Arguments:
- frames: bfloat16 [8192, 1024], P(('dp', 'ctx')), parts along dimension 0, may hold values from -20 to 20
- tile_source: int32 [512], P('dp'), parts along dimension 0, may hold values from 0 to 63, as said below
- tile_utt: int32 [512], P('dp'), parts along dimension 0, may hold values from 0 to 3, never falling along the last dimension, each value on 1 to 33 neighbouring positions
- query_weight: bfloat16 [1024, 512], replicated, may hold values from -1.625 to 1.625
- key_weight: bfloat16 [1024, 512], replicated, may hold values from -0.1875 to 0.1875
- value_weight: bfloat16 [1024, 512], replicated, may hold values from -0.1875 to 0.1875
- output_weight: bfloat16 [512, 1024], replicated, may hold values from -1.5 to 1.5
- depth_weight: float32 [31, 1024], replicated, may hold values from -1 to 1
- bn_scale: float32 [1024], replicated, may hold values from 0.5 to 2
- bn_shift: float32 [1024], replicated, may hold values from -3 to 3
Outputs:
- encoded: bfloat16 [8192, 1024], P(('dp', 'ctx')), parts along dimension 0
There are 8 independent parts, one for each index of `dp`. A program takes and returns all parts, laid end to end along the dimension named above; an argument that names none is the same for every part. Nothing has to cross between parts.
Inputs may be any that keep to these rules, and one draw needn't show every extreme that they name: `tile_source`: A permutation of the tiles of a part. The tiles that one shard receives come at most 4 from any one shard, and exactly 4 from some shard; for one tile position within a shard, the sources over all shards lie on distinct shards. `tile_utt`: never falls along the tiles; each of the 4 utterances holds 1 to 33 tiles, one exactly 33.
All inputs are finite; a program needn't handle non-finite values.
Results may differ from a plain program's by a relative error of at most 0.0068.
Values may be sent and summed in bfloat16 or wider, within the bound.
No kernel may reach another device: no remote copies, remote signals or barrier semaphores. Data moves between devices by JAX's collectives and lax.ppermute only.
A program may use at most 64 MiB of HBM per device.

v0:
```python
import functools
import math

import jax
import jax.numpy as jnp
from jax import lax
from jax.experimental import pallas as pl
from jax.experimental.pallas import tpu as pltpu
from jax.sharding import PartitionSpec as P


HEADS = 4
HEAD_DIM = 128
KERNEL = 31
TILE = 16
UTTS = 4
ALONE = 56
NEGATIVE = -1e30

VMEM = pl.BlockSpec(memory_space=pltpu.VMEM)
SMEM = pl.BlockSpec(memory_space=pltpu.SMEM)
HBM = pl.BlockSpec(memory_space=pltpu.HBM)


def params(mib):
    return pltpu.CompilerParams(vmem_limit_bytes=mib << 20)


def layer_norm(rows):
    values = rows.astype(jnp.float32)
    center = values - jnp.mean(values, axis=-1, keepdims=True)
    spread = jnp.mean(center * center, axis=-1, keepdims=True)
    return center * lax.rsqrt(spread + 1e-05)


def project(rows, weight_ref):
    return jnp.dot(rows, weight_ref[...], preferred_element_type=jnp.float32).astype(jnp.bfloat16)


def attend(
    grouped, query_utt, key_utt, key_parts, value_parts, query_weight, output_weight
):
    queries = project(layer_norm(grouped[...]).astype(jnp.bfloat16), query_weight)
    allowed = query_utt[:, :1] == key_utt
    exponent_scale = math.log2(math.e) / math.sqrt(HEAD_DIM)
    heads = []
    for head in range(HEADS):
        columns = slice(head * HEAD_DIM, (head + 1) * HEAD_DIM)
        key_head = jnp.concatenate([part[:, columns] for part in key_parts], axis=0)
        value_head = jnp.concatenate([part[:, columns] for part in value_parts], axis=0)
        scores = lax.dot_general(
            queries[:, columns],
            key_head,
            (((1,), (1,)), ((), ())),
            preferred_element_type=jnp.float32,
        )
        scores = jnp.where(allowed, scores, NEGATIVE)
        top = jnp.max(scores, axis=-1, keepdims=True)
        weights = jnp.exp2((scores - top) * exponent_scale)
        row_sum = jnp.sum(weights, axis=-1, keepdims=True)
        summed = jnp.dot(
            weights.astype(jnp.bfloat16), value_head, preferred_element_type=jnp.float32
        )
        heads.append((summed / row_sum).astype(jnp.bfloat16))
    attended = jnp.concatenate(heads, axis=1)
    return (
        grouped[...].astype(jnp.float32)
        + jnp.dot(attended, output_weight[...], preferred_element_type=jnp.float32)
    ).astype(jnp.bfloat16)


def convolve(residual, plan, at, half_taps, half_shift, out_hbm, padded, residual_rows, out, sems):
    rows_dev, width = out.shape
    tiles_dev = rows_dev // TILE
    held = tiles_dev + 2
    residual_rows[...] = residual[TILE : TILE + rows_dev]
    shaped = layer_norm(residual).astype(jnp.bfloat16).astype(jnp.float32)
    for i in range(held):
        row = pl.multiple_of(plan[at + i] * TILE, TILE)
        for block in range(width // 128):
            padded[block, pl.ds(row, TILE), :] = shaped[
                i * TILE : (i + 1) * TILE, block * 128 : (block + 1) * 128
            ]
    group = math.gcd(tiles_dev, 4)

    def write(step):
        rows = pl.ds(pl.multiple_of(step * group * TILE, TILE), group * TILE)
        return pltpu.make_async_copy(out.at[rows, :], out_hbm.at[rows, :], sems.at[step])

    def some_tiles(step, carried):
        starts = [
            pl.multiple_of(plan[at + held + step * group + k] * TILE, TILE) for k in range(group)
        ]
        for block in range(width // 128):
            columns = slice(block * 128, (block + 1) * 128)
            shift = jnp.broadcast_to(half_shift[:, columns], (8, 128))
            sums = [[shift, shift] for _ in range(group)]
            windows = [{} for _ in range(group)]
            for tap in range(KERNEL):
                weight = half_taps[tap : tap + 1, columns]
                for k in range(group):
                    for part in range(2):
                        offset = tap + 8 * part
                        if offset not in windows[k]:
                            windows[k][offset] = padded[
                                block, pl.ds(starts[k] + (offset - KERNEL // 2), 8), :
                            ]
                        sums[k][part] = sums[k][part] + windows[k][offset] * weight
            for k in range(group):
                half = jnp.concatenate(sums[k], axis=0)
                rows = pl.ds(pl.multiple_of((step * group + k) * TILE, TILE), TILE)
                kept = residual_rows[rows, columns].astype(jnp.float32)
                out[rows, columns] = (kept + (half + half * jnp.tanh(half))).astype(jnp.bfloat16)
        write(step).start()
        return carried

    steps = tiles_dev // group
    lax.fori_loop(0, steps, some_tiles, 0)
    for step in range(steps):
        write(step).wait()


def plan_places(me, utt_ref, tiles_dev, total, plan, at):
    first = me * tiles_dev - 1
    held = tiles_dev + 2
    place = jnp.int32(1)
    before = utt_ref[jnp.clip(first, 0, total - 1)]
    for i in range(held):
        here = utt_ref[jnp.clip(first + i, 0, total - 1)]
        if i:
            place = place + 1 + (here != before).astype(jnp.int32)
        before = here
        inside = (first + i >= 0) & (first + i < total)
        plan[at + i] = jnp.where(inside, place, padded_rows(tiles_dev) // TILE - 1)
        if 1 <= i <= tiles_dev:
            plan[at + held + i - 1] = place


def padded_rows(tiles_dev):
    return (1 + tiles_dev + 2 + (UTTS - 1) + 2) * TILE


def block_scratch(rows_dev, width):
    tiles_dev = rows_dev // TILE
    return [
        pltpu.VMEM((width // 128, padded_rows(tiles_dev), 128), jnp.float32),
        pltpu.VMEM((rows_dev, width), jnp.bfloat16),
        pltpu.VMEM((rows_dev, width), jnp.bfloat16),
        pltpu.SemaphoreType.DMA((tiles_dev // math.gcd(tiles_dev, 4),)),
    ]


def key_value_kernel(rows_ref, key_weight_ref, value_weight_ref, key_ref, value_ref):
    normed = layer_norm(rows_ref[...]).astype(jnp.bfloat16)
    key_ref[...] = project(normed, key_weight_ref)
    value_ref[...] = project(normed, value_weight_ref)


def key_value(rows, key_weight, value_weight):
    shape = jax.ShapeDtypeStruct((rows.shape[0], key_weight.shape[1]), jnp.bfloat16)
    flops = 4 * rows.shape[0] * rows.shape[1] * key_weight.shape[1]
    return pl.pallas_call(
        key_value_kernel,
        out_shape=(shape, shape),
        in_specs=[VMEM] * 3,
        out_specs=(VMEM, VMEM),
        cost_estimate=pl.CostEstimate(flops=flops, bytes_accessed=3 << 20, transcendentals=0),
        name="key_value",
    )(rows, key_weight, value_weight)


def ring_kernel(count, me_ref, source_ref, utt_ref, key_utt_ref, *refs):
    chunks = refs[:count]
    keys = refs[count : 2 * count]
    values = refs[2 * count : 3 * count]
    query_weight, output_weight, taps, scale, shift, out_hbm = refs[3 * count : 3 * count + 6]
    padded, residual_rows, out, write_sems = refs[3 * count + 6 : 3 * count + 10]
    grouped, query_utt, half_taps, plan, sems = refs[3 * count + 10 :]
    me = me_ref[0]
    tiles_dev = out.shape[0] // TILE
    held = tiles_dev + 2
    total = tiles_dev * count
    first = me * tiles_dev - 1
    padded[...] = jnp.zeros_like(padded)
    half_taps[...] = taps[...] * (0.5 * scale[...])
    for i in range(held):
        position = jnp.clip(first + i, 0, total - 1)
        source = source_ref[position]
        row = pl.multiple_of((source % tiles_dev) * TILE, TILE)
        behind = lax.rem(me - source // tiles_dev + count, count)
        for step in range(count):

            @pl.when(behind == step)
            def _(step=step, row=row, i=i):
                pltpu.make_async_copy(
                    chunks[step].at[pl.ds(row, TILE), :],
                    grouped.at[pl.ds(i * TILE, TILE), :],
                    sems.at[i],
                ).start()

        query_utt[pl.ds(i * TILE, TILE), :] = jnp.full((TILE, 128), utt_ref[position], jnp.int32)
    plan_places(me, utt_ref, tiles_dev, total, plan, 0)
    for i in range(held):
        pltpu.make_async_copy(
            chunks[0].at[pl.ds(0, TILE), :], grouped.at[pl.ds(i * TILE, TILE), :], sems.at[i]
        ).wait()
    residual = attend(
        grouped, query_utt, key_utt_ref[...], keys, values, query_weight, output_weight
    )
    convolve(
        residual, plan, 0, half_taps, 0.5 * shift[...], out_hbm, padded, residual_rows, out,
        write_sems,
    )


def ring_block(
    frames, tile_source, tile_utt, query_weight, key_weight, value_weight, output_weight,
    depth_weight, bn_scale, bn_shift,
):
    count = lax.axis_size("ctx")
    me = lax.axis_index("ctx")
    rows_dev, width = frames.shape
    tiles_dev = rows_dev // TILE
    ring = [(i, (i + 1) % count) for i in range(count)]
    chunks = [frames]
    for _ in range(count - 1):
        chunks.append(lax.ppermute(chunks[-1], "ctx", ring))
    pairs = [key_value(chunk, key_weight, value_weight) for chunk in chunks]
    shards = lax.rem(me - jnp.arange(count, dtype=jnp.int32) + count, count)
    arrived = (shards[:, None] * tiles_dev + jnp.arange(tiles_dev, dtype=jnp.int32)).reshape(-1)
    key_utt = jnp.sum(
        jnp.where(arrived[:, None] == tile_source[None, :], tile_utt[None, :], 0), axis=1
    )
    key_utt = jnp.repeat(key_utt, TILE).reshape(1, -1)
    return pl.pallas_call(
        functools.partial(ring_kernel, count),
        out_shape=jax.ShapeDtypeStruct((rows_dev, width), jnp.bfloat16),
        in_specs=[SMEM] * 3
        + [VMEM]
        + [pl.BlockSpec(memory_space=pl.ANY)] * count
        + [VMEM] * (2 * count + 5),
        out_specs=HBM,
        scratch_shapes=block_scratch(rows_dev, width)
        + [
            pltpu.VMEM((rows_dev + 2 * TILE, width), jnp.bfloat16),
            pltpu.VMEM((rows_dev + 2 * TILE, 128), jnp.int32),
            pltpu.VMEM(depth_weight.shape, jnp.float32),
            pltpu.SMEM((2 * tiles_dev + 2,), jnp.int32),
            pltpu.SemaphoreType.DMA((tiles_dev + 2,)),
        ],
        cost_estimate=pl.CostEstimate(
            flops=2 << 30, bytes_accessed=8 << 20, transcendentals=1 << 20
        ),
        name="ring_block",
    )(
        me.reshape(1), tile_source, tile_utt, key_utt, *chunks,
        *[pair[0] for pair in pairs], *[pair[1] for pair in pairs],
        query_weight, output_weight, depth_weight, bn_scale.reshape(1, -1), bn_shift.reshape(1, -1),
    )


COUNT = 4
SWAP_OUTER = [(0, 1), (1, 0), (2, 3), (3, 2)]
SWAP_INNER = [(1, 2), (2, 1)]
TO_ENDS = [(1, 0), (2, 3)]
FROM_ENDS = [(0, 1), (3, 2)]
OVER_TWO = [(0, 2), (3, 1)]


def quarter_of(source_shard, target):
    return jnp.where(source_shard % 2 == 1, target, COUNT - 1 - target)


def divide(value, by):
    if by & (by - 1) == 0:
        return value >> (by.bit_length() - 1)
    return lax.div(value, by)


def arrange_kernel(
    me_ref, source_hbm, rows_hbm, low_ref, last_ref, high_ref, start_ref, source_ref, rows, slots, sems
):
    me = me_ref[0]
    rows_dev, quarter_rows = rows.shape[0], last_ref.shape[0]
    tiles_dev = rows_dev // TILE
    per_pair = tiles_dev // COUNT
    rows_copy = pltpu.make_async_copy(rows_hbm, rows, sems.at[0])
    source_copy = pltpu.make_async_copy(source_hbm, source_ref, sems.at[1])
    source_copy.start()
    rows_copy.start()
    source_copy.wait()
    for target in range(COUNT):
        place = quarter_of(me, target) * per_pair
        for position in range(target * tiles_dev, (target + 1) * tiles_dev):
            source = source_ref[position]
            shard = divide(source, tiles_dev)
            mine = shard == me
            slots[jnp.where(mine, place, tiles_dev)] = source - shard * tiles_dev
            place = place + mine.astype(jnp.int32)
    rows_copy.wait()
    for place in range(tiles_dev):
        tile = rows[pl.ds(pl.multiple_of(slots[place] * TILE, TILE), TILE), :]
        row = place * TILE
        if row < rows_dev - quarter_rows:
            low_ref[row : row + TILE] = tile
        else:
            row_here = row - (rows_dev - quarter_rows)
            last_ref[row_here : row_here + TILE] = tile
        if row >= quarter_rows:
            high_ref[row - quarter_rows : row - quarter_rows + TILE] = tile
        else:
            start_ref[row : row + TILE] = tile


def hold_kernel(*refs):
    count = (len(refs) - 3) // 2
    arrays, kept = refs[:count], refs[count : 2 * count - 1]
    taps, scale, shift, sems = refs[2 * count - 1 :]
    targets = (*kept[:-2], taps, scale, shift)
    copies = [
        pltpu.make_async_copy(array, target, sems.at[i])
        for i, (array, target) in enumerate(zip(arrays, targets))
    ]
    for copy in copies:
        copy.start()
    for copy in copies:
        copy.wait()
    kept[-2][...] = taps[...] * (0.5 * scale[...])
    kept[-1][...] = 0.5 * shift[...]


def hold(*arrays):
    taps, scale, shift = arrays[-3:]
    kept = (*arrays[:-2], shift)
    return pl.pallas_call(
        hold_kernel,
        out_shape=tuple(pltpu.VMEM(a.shape, a.dtype) for a in kept),
        in_specs=[HBM] * len(arrays),
        out_specs=(VMEM,) * len(kept),
        scratch_shapes=[pltpu.VMEM(a.shape, a.dtype) for a in (taps, scale, shift)]
        + [pltpu.SemaphoreType.DMA((len(arrays),))],
        compiler_params=params(ALONE),
        cost_estimate=pl.CostEstimate(flops=0, bytes_accessed=8 << 20, transcendentals=0),
        name="hold_call",
    )(*arrays)


def plan_sizes(tiles_dev):
    held = tiles_dev + 2
    return held, 2 * held, 3 * held + tiles_dev


def tables_kernel(
    me_ref, source_ref, utt_ref, plan_ref, key_utt_ref, query_utt_ref, filled, ranks, key_utts
):
    me = me_ref[0]
    total = source_ref.shape[0]
    tiles_dev = total // COUNT
    per_pair = tiles_dev // COUNT
    quarter_tiles = per_pair
    for pair in range(COUNT * COUNT):
        filled[pair] = 0

    def one(position, carried):
        pair = divide(source_ref[position], tiles_dev) * COUNT + divide(position, tiles_dev)
        rank = filled[pair]
        filled[pair] = rank + 1
        ranks[position] = rank
        key_utts[pair * per_pair + rank] = utt_ref[position]
        return carried

    lax.fori_loop(0, total, one, 0, unroll=4)
    is_end = (me == 0) | (me == COUNT - 1)
    second = jnp.where(is_end, 2, 3)
    third = jnp.where(is_end, 3, 2)
    held, places_at, _ = plan_sizes(tiles_dev)
    for i in range(held):
        position = jnp.clip(me * tiles_dev - 1 + i, 0, total - 1)
        source = divide(source_ref[position], tiles_dev)
        apart = me ^ source
        quarter = quarter_of(source, divide(position, tiles_dev))
        row = quarter * quarter_tiles + ranks[position]
        early = jnp.where(apart == 0, row, -1)
        near = tiles_dev + row + jnp.where(quarter == COUNT - 1, 3 * quarter_tiles, 0)
        early = jnp.where(apart == 1, near, early)
        early = jnp.where(apart == second, tiles_dev + 2 * quarter_tiles + row, early)
        plan_ref[i] = early
        plan_ref[held + i] = jnp.where(apart == third, row, -1)
        query_utt_ref[i * TILE : (i + 1) * TILE] = jnp.full(
            (TILE, 128), utt_ref[position], jnp.int32
        )
    plan_places(me, utt_ref, tiles_dev, total, plan_ref, places_at)

    near, second, far = me ^ 1, me ^ second, me ^ third
    order = [(me, quarter, False) for quarter in (0, 1, 2, 3)]
    order += [(near, quarter, False) for quarter in (0, 1, 2)]
    order += [(second, quarter, False) for quarter in (1, 2, 3)]
    order += [(near, 3, True), (second, 0, True), (far, 3, True)]
    order += [(far, quarter, False) for quarter in (0, 1, 2)]
    lane_tile = lax.broadcasted_iota(jnp.int32, (1, 128), 1) // TILE
    tile_values = []
    for shard, quarter, inner_only in order:
        target = quarter_of(shard, quarter)
        for rank in range(per_pair):
            utt = key_utts[(shard * COUNT + target) * per_pair + rank]
            if inner_only:
                utt = jnp.where(is_end, -1, utt)
            tile_values.append(utt)
    per_vector = 128 // TILE
    for start in range(0, len(tile_values), per_vector):
        vector = jnp.full((1, 128), tile_values[start], jnp.int32)
        for k in range(1, per_vector):
            vector = jnp.where(lane_tile == k, tile_values[start + k], vector)
        key_utt_ref[:, start * TILE : start * TILE + 128] = vector


def early_kernel(
    me_ref, plan, low, last, near, near_last, inner, inner_end,
    key_weight, value_weight, key_ref, value_ref, grouped, rows,
):
    me = me_ref[0]
    is_end = (me == 0) | (me == COUNT - 1)
    piece, quarter_rows = low.shape[0], last.shape[0]
    base = piece + quarter_rows
    rows[0:piece] = low[...]
    rows[piece:base] = last[...]
    rows[base : base + piece] = near[...]

    @pl.when(is_end)
    def _():
        rows[base + piece : base + 2 * piece] = inner_end[...]

    @pl.when(jnp.logical_not(is_end))
    def _():
        rows[base + piece : base + 2 * piece] = inner[...]

    rows[base + 2 * piece :] = near_last[...]
    for i in range(grouped.shape[0] // TILE):
        place = jnp.maximum(plan[i], 0)
        grouped[i * TILE : (i + 1) * TILE] = rows[
            pl.ds(pl.multiple_of(place * TILE, TILE), TILE), :
        ]
    normed = layer_norm(rows[...]).astype(jnp.bfloat16)
    key_ref[...] = project(normed, key_weight)
    value_ref[...] = project(normed, value_weight)


def lay_kernel(first_ref, second_ref, out_ref):
    rows = first_ref.shape[0]
    out_ref[:rows] = first_ref[...]
    out_ref[rows:] = second_ref[...]


def final_kernel(
    me_ref, plan, query_utt, key_utt, early_grouped, far, far_end,
    early_key, early_value, middle_key, middle_value,
    key_weight, value_weight, query_weight, output_weight, half_taps, half_shift,
    out_hbm, grouped, padded, residual_rows, out, write_sems, late,
):
    me = me_ref[0]
    is_end = (me == 0) | (me == COUNT - 1)
    held, places_at, _ = plan_sizes(out.shape[0] // TILE)

    @pl.when(is_end)
    def _():
        late[...] = far_end[...]

    @pl.when(jnp.logical_not(is_end))
    def _():
        late[...] = far[...]

    for i in range(held):
        row = plan[held + i]

        @pl.when(row >= 0)
        def _(row=row, i=i):
            grouped[i * TILE : (i + 1) * TILE] = late[
                pl.ds(pl.multiple_of(row * TILE, TILE), TILE), :
            ]

    padded[...] = jnp.zeros_like(padded)
    normed = layer_norm(late[...]).astype(jnp.bfloat16)
    late_key = project(normed, key_weight)
    late_value = project(normed, value_weight)
    residual = attend(
        grouped, query_utt, key_utt[...],
        [early_key, middle_key, late_key], [early_value, middle_value, late_value],
        query_weight, output_weight,
    )
    convolve(
        residual, plan, places_at, half_taps, half_shift[...], out_hbm, padded, residual_rows,
        out, write_sems,
    )


def after(value, other):
    return lax.optimization_barrier((value, other))[0]


def line_block(
    frames, tile_source, tile_utt, query_weight, key_weight, value_weight, output_weight,
    depth_weight, bn_scale, bn_shift,
):
    me = lax.axis_index("ctx").reshape(1)
    rows_dev, width = frames.shape
    quarter = rows_dev // COUNT
    piece = rows_dev - quarter
    total = tile_source.shape[0]
    wide = key_weight.shape[1]

    def shape(rows, columns=width, kind=jnp.bfloat16):
        return jax.ShapeDtypeStruct((rows, columns), kind)

    def cost(rows):
        return pl.CostEstimate(
            flops=4 * rows * width * wide, bytes_accessed=rows * width * 4, transcendentals=rows
        )

    low, last, high, start = pl.pallas_call(
        arrange_kernel,
        out_shape=tuple(pltpu.VMEM((n, width), frames.dtype) for n in (piece, quarter, piece, quarter)),
        in_specs=[SMEM] + [HBM] * 2,
        out_specs=(VMEM,) * 4,
        scratch_shapes=[
            pltpu.SMEM((total,), jnp.int32),
            pltpu.VMEM((rows_dev, width), jnp.bfloat16),
            pltpu.SMEM((rows_dev // TILE + 1,), jnp.int32),
            pltpu.SemaphoreType.DMA((2,)),
        ],
        compiler_params=params(ALONE),
        name="arrange",
    )(me, tile_source, frames)

    def swap(value, perm):
        return lax.ppermute(value, "ctx", perm)

    near = swap(low, SWAP_OUTER)
    inner = swap(high, SWAP_INNER)
    held_rows = rows_dev + 2 * TILE
    plan, key_utt, query_utt = pl.pallas_call(
        tables_kernel,
        out_shape=(
            jax.ShapeDtypeStruct((plan_sizes(rows_dev // TILE)[2],), jnp.int32),
            shape(1, total * TILE, jnp.int32),
            shape(held_rows, 128, jnp.int32),
        ),
        in_specs=[SMEM] * 3,
        out_specs=(SMEM, VMEM, VMEM),
        scratch_shapes=[pltpu.SMEM((n,), jnp.int32) for n in (COUNT * COUNT, total, total)],
        compiler_params=params(4),
        name="tables_call",
    )(me, tile_source, tile_utt)
    key_weight, value_weight, query_weight, output_weight, half_taps, half_shift = hold(
        key_weight, value_weight, query_weight, output_weight, depth_weight,
        bn_scale.reshape(1, -1), bn_shift.reshape(1, -1),
    )
    far = swap(low, OVER_TWO)
    inner_end = swap(inner, TO_ENDS)
    near_last = swap(after(last, near), FROM_ENDS)
    far_end = swap(far, TO_ENDS)
    rest = pl.pallas_call(
        lay_kernel,
        out_shape=shape(2 * quarter),
        in_specs=[VMEM] * 2,
        out_specs=VMEM,
        compiler_params=params(4),
        name="lay_call",
    )(start, near_last)
    rest = swap(after(rest, far), SWAP_INNER)

    early_rows = rows_dev + 2 * piece + quarter
    early_key, early_value, grouped = pl.pallas_call(
        early_kernel,
        out_shape=(shape(early_rows, wide), shape(early_rows, wide), shape(held_rows)),
        in_specs=[SMEM] * 2 + [VMEM] * 8,
        out_specs=(VMEM,) * 3,
        scratch_shapes=[pltpu.VMEM((early_rows, width), jnp.bfloat16)],
        compiler_params=params(16),
        cost_estimate=cost(early_rows),
        name="early_call",
    )(me, plan, low, last, near, near_last, inner, inner_end, key_weight, value_weight)
    middle_key, middle_value = pl.pallas_call(
        key_value_kernel,
        out_shape=(shape(2 * quarter, wide),) * 2,
        in_specs=[VMEM] * 3,
        out_specs=(VMEM,) * 2,
        compiler_params=params(8),
        cost_estimate=cost(2 * quarter),
        name="middle_call",
    )(rest, key_weight, value_weight)
    return pl.pallas_call(
        final_kernel,
        out_shape=(shape(rows_dev), shape(held_rows)),
        in_specs=[SMEM] * 2 + [VMEM] * 15,
        out_specs=(HBM, VMEM),
        input_output_aliases={4: 1},
        scratch_shapes=block_scratch(rows_dev, width) + [pltpu.VMEM((piece, width), jnp.bfloat16)],
        compiler_params=params(28),
        cost_estimate=pl.CostEstimate(
            flops=2 << 30, bytes_accessed=8 << 20, transcendentals=1 << 20
        ),
        name="final",
    )(
        me, plan, query_utt, key_utt, grouped, far, far_end,
        early_key, early_value, middle_key, middle_value,
        key_weight, value_weight, query_weight, output_weight, half_taps, half_shift,
    )[0]


def per_device(*arrays):
    tiles_dev = arrays[0].shape[0] // TILE
    if lax.axis_size("ctx") == COUNT and tiles_dev % COUNT == 0:
        return line_block(*arrays)
    return ring_block(*arrays)


def solution(mesh):
    return jax.shard_map(
        per_device,
        mesh=mesh,
        in_specs=(P(("dp", "ctx"), None), P("dp"), P("dp"), P(), P(), P(), P(), P(), P(), P()),
        out_specs=P(("dp", "ctx"), None),
        check_vma=False,
    )
```

profile of v0, /device:TPU:0, one launch (start us, length us, event | category | flops | bytes accessed | tf_op | source)
XLA Modules:
  0.0 52.7 jit_solution(4110638107487826020)
XLA Ops:
  0.0 1.1 %arrange.1 = (bf16[192,1024]{1,0:T(8,128)(2,1)S(1)}, bf16[64,1024]{1,0:T(8,128)(2,1)S(1)}, bf16[192,1024]{1,0:T(8,128)(2,1)S(1)}, bf16[64,1024]{1,0:T(8,128)(2,1)S(1)}) custom-call(s32[1]{0:T(128)} %bitcast.me_ref, s32[64]{0:T(128)} %source_hbm.1, bf16[256,1024]{1,0:T(8,128)(2,1)} %rows_hbm.1), custom_call_target="tpu_custom_call" | custom-call | tf_op jit(solution)/shard_map/arrange/pallas_call | solution.py:519
  1.1 3.1 %collective-permute-start = (bf16[192,1024]{1,0:T(8,128)(2,1)S(1)}, bf16[192,1024]{1,0:T(8,128)(2,1)S(1)}, u32[]{:S(2)}, u32[]{:S(2)}) collective-permute-start(bf16[192,1024]{1,0:T(8,128)(2,1)S(1)} %get-tuple-element.29.low), channel_id=1, source_target_pairs={{0,1},{1,0},{2,3},{3,2},{4,5},{5,4},{6,7},{7,6},{8,9},{9,8},{10,11... | collective-permute-start | bytes 1179656 | tf_op jit(solution)/shard_map/ppermute | solution.py:535
  4.3 0.7 %collective-permute-start.2 = (bf16[192,1024]{1,0:T(8,128)(2,1)S(1)}, bf16[192,1024]{1,0:T(8,128)(2,1)S(1)}, u32[]{:S(2)}, u32[]{:S(2)}) collective-permute-start(bf16[192,1024]{1,0:T(8,128)(2,1)S(1)} %get-tuple-element.32), channel_id=1, source_target_pairs={{1,2},{2,1},{5,6},{6,5},{9,10},{10,9},{13,14},{14,13},{17,18},{18,... | collective-permute-start | bytes 1179656 | tf_op jit(solution)/shard_map/ppermute | solution.py:535
  4.9 5.8 %collective-permute-start.4 = (bf16[192,1024]{1,0:T(8,128)(2,1)S(1)}, bf16[192,1024]{1,0:T(8,128)(2,1)S(1)}, u32[]{:S(2)}, u32[]{:S(2)}) collective-permute-start(bf16[192,1024]{1,0:T(8,128)(2,1)S(1)} %get-tuple-element.29.low), channel_id=1, source_target_pairs={{0,2},{3,1},{4,6},{7,5},{8,10},{11,9},{12,14},{15,13},{16,18},{19,... | collective-permute-start | bytes 1179656 | tf_op jit(solution)/shard_map/ppermute | solution.py:535
  10.7 3.1 %collective-permute-done.near = bf16[192,1024]{1,0:T(8,128)(2,1)S(1)} collective-permute-done((bf16[192,1024]{1,0:T(8,128)(2,1)S(1)}, bf16[192,1024]{1,0:T(8,128)(2,1)S(1)}, u32[]{:S(2)}, u32[]{:S(2)}) %collective-permute-start) | collective-permute-done | bytes 393248 | tf_op jit(solution)/shard_map/ppermute | solution.py:535
  13.8 4.4 %collective-permute-start.1 = (bf16[64,1024]{1,0:T(8,128)(2,1)S(1)}, bf16[64,1024]{1,0:T(8,128)(2,1)S(1)}, u32[]{:S(2)}, u32[]{:S(2)}) collective-permute-start(bf16[64,1024]{1,0:T(8,128)(2,1)S(1)} %get-tuple-element.31.last), channel_id=1, source_target_pairs={{0,1},{3,2},{4,5},{7,6},{8,9},{11,10},{12,13},{15,14},{16,17},{19,... | collective-permute-start | bytes 393224 | tf_op jit(solution)/shard_map/ppermute | solution.py:535
  18.1 0.0 collective-permute-done.2.inner
  18.2 1.3 %collective-permute-start.3 = (bf16[192,1024]{1,0:T(8,128)(2,1)S(1)}, bf16[192,1024]{1,0:T(8,128)(2,1)S(1)}, u32[]{:S(2)}, u32[]{:S(2)}) collective-permute-start(bf16[192,1024]{1,0:T(8,128)(2,1)S(1)} %collective-permute-done.2.inner), channel_id=1, source_target_pairs={{1,0},{2,3},{5,4},{6,7},{9,8},{10,11},{13,12},{14,15},{17,16},{18,... | collective-permute-start | bytes 1179656 | tf_op jit(solution)/shard_map/ppermute | solution.py:535
  19.5 4.4 %collective-permute-done.1.near_last.second_ref = bf16[64,1024]{1,0:T(8,128)(2,1)S(1)} collective-permute-done((bf16[64,1024]{1,0:T(8,128)(2,1)S(1)}, bf16[64,1024]{1,0:T(8,128)(2,1)S(1)}, u32[]{:S(2)}, u32[]{:S(2)}) %collective-permute-start.1) | collective-permute-done | bytes 131104 | tf_op jit(solution)/shard_map/ppermute | solution.py:535
  23.9 0.0 copy-start
  23.9 0.0 copy-start.1
  23.9 0.0 collective-permute-done.4.far
  23.9 0.7 %collective-permute-start.6 = (bf16[128,1024]{1,0:T(8,128)(2,1)S(1)}, bf16[128,1024]{1,0:T(8,128)(2,1)S(1)}, u32[]{:S(2)}, u32[]{:S(2)}) collective-permute-start(bf16[128,1024]{1,0:T(8,128)(2,1)S(1)} %lay_call.1), channel_id=1, source_target_pairs={{1,2},{2,1},{5,6},{6,5},{9,10},{10,9},{13,14},{14,13},{17,18},{18,... | collective-permute-start | bytes 786440 | tf_op jit(solution)/shard_map/ppermute | solution.py:535
  24.6 1.3 %collective-permute-start.5 = (bf16[192,1024]{1,0:T(8,128)(2,1)S(1)}, bf16[192,1024]{1,0:T(8,128)(2,1)S(1)}, u32[]{:S(2)}, u32[]{:S(2)}) collective-permute-start(bf16[192,1024]{1,0:T(8,128)(2,1)S(1)} %collective-permute-done.4.far), channel_id=1, source_target_pairs={{1,0},{2,3},{5,4},{6,7},{9,8},{10,11},{13,12},{14,15},{17,16},{18,... | collective-permute-start | bytes 1179656 | tf_op jit(solution)/shard_map/ppermute | solution.py:535
  25.9 0.0 copy-done
  25.9 0.0 copy-done.1
  25.9 1.8 %tables_call.1 = (s32[70]{0:T(128)S(1)}, s32[1,1024]{1,0:T(1,128)S(1)}, s32[288,128]{1,0:T(8,128)S(1)}) custom-call(s32[1]{0:T(128)} %bitcast.me_ref, s32[64]{0:T(128)S(1)} %copy-done, s32[64]{0:T(128)S(1)} %copy-done.1), custom_call_target="tpu_custom_call" | custom-call | tf_op jit(solution)/shard_map/tables_call/pallas_call | solution.py:540
  27.8 2.3 %hold_call.1 = (bf16[1024,512]{1,0:T(8,128)(2,1)S(1)}, bf16[1024,512]{1,0:T(8,128)(2,1)S(1)}, bf16[1024,512]{1,0:T(8,128)(2,1)S(1)}, bf16[512,1024]{1,0:T(8,128)...) custom-call(bf16[1024,512]{1,0:T(8,128)(2,1)} %refs_0_.1, bf16[1024,512]{1,0:T(8,128)(2,1)} %refs_1_.1, ...), custom_call_target="tpu_custom_call" | custom-call | bytes 8388608 | tf_op jit(solution)/shard_map/hold_call/pallas_call | solution.py:335
  30.0 0.0 collective-permute-done.6.rows_ref
  30.1 0.6 %middle_call.1 = (bf16[128,512]{1,0:T(8,128)(2,1)S(1)}, bf16[128,512]{1,0:T(8,128)(2,1)S(1)}) custom-call(bf16[128,1024]{1,0:T(8,128)(2,1)S(1)} %collective-permute-done.6.rows_ref, bf16[1024,512]{1,0:T(8,128)(2,1)S(1)} %get-tuple-element.33.key_weight.key_weight_ref, bf16[1024,512]{1,0:T(8,128)(2,1)S(1)} %get-tuple-element.34.value_weight.value_weight_ref), custom_call_target="tpu_custom_call" | custom-call | flops 268435456 | bytes 524288 | tf_op jit(solution)/shard_map/middle_call/pallas_call | solution.py:582
  30.7 7.1 %collective-permute-done.3.inner_end = bf16[192,1024]{1,0:T(8,128)(2,1)S(1)} collective-permute-done((bf16[192,1024]{1,0:T(8,128)(2,1)S(1)}, bf16[192,1024]{1,0:T(8,128)(2,1)S(1)}, u32[]{:S(2)}, u32[]{:S(2)}) %collective-permute-start.3) | collective-permute-done | bytes 393248 | tf_op jit(solution)/shard_map/ppermute | solution.py:535
  37.8 2.8 %early_call.1 = (bf16[704,512]{1,0:T(8,128)(2,1)S(1)}, bf16[704,512]{1,0:T(8,128)(2,1)S(1)}, bf16[288,1024]{1,0:T(8,128)(2,1)S(1)}) custom-call(s32[1]{0:T(128)} %bitcast.me_ref, s32[70]{0:T(128)S(1)} %get-tuple-element.26.plan, bf16[192,1024]{1,0:T(8,128)(2,1)S(1)} %get-tuple-element.29.low, bf16[64,1024]{1,0:T(8,128)(2,1)S(1)} %get-tuple-element.31.last, ...), custom_call_target="tpu_custom_call" | custom-call | flops 1476395008 | bytes 2883584 | tf_op jit(solution)/shard_map/early_call/pallas_call | solution.py:572
  40.6 3.6 %collective-permute-done.5.far_end = bf16[192,1024]{1,0:T(8,128)(2,1)S(1)} collective-permute-done((bf16[192,1024]{1,0:T(8,128)(2,1)S(1)}, bf16[192,1024]{1,0:T(8,128)(2,1)S(1)}, u32[]{:S(2)}, u32[]{:S(2)}) %collective-permute-start.5) | collective-permute-done | bytes 393248 | tf_op jit(solution)/shard_map/ppermute | solution.py:535
  44.2 8.5 %final.1 = (bf16[256,1024]{1,0:T(8,128)(2,1)}, bf16[288,1024]{1,0:T(8,128)(2,1)S(1)}) custom-call(s32[1]{0:T(128)} %bitcast.me_ref, s32[70]{0:T(128)S(1)} %get-tuple-element.26.plan, s32[288,128]{1,0:T(8,128)S(1)} %get-tuple-element.27.query_utt, s32[1,1024]{1,0:T(1,128)S(1)} %get-tuple-element.28.key_utt, ...), custom_call_target="tpu_custom_call", output_to_operand_aliasing={{1}: (4, {})} | custom-call | flops 2147483648 | bytes 8388608 | tf_op jit(solution)/shard_map/final/pallas_call | solution.py:591
  (1 shorter events, 0.0 us)
Async XLA Ops:
  1.1 12.6 %collective-permute-start = (bf16[192,1024]{1,0:T(8,128)(2,1)S(1)}, bf16[192,1024]{1,0:T(8,128)(2,1)S(1)}, u32[]{:S(2)}, u32[]{:S(2)}) collective-permute-start(bf16[192,1024]{1,0:T(8,128)(2,1)S(1)} %get-tuple-element.29.low), channel_id=1, source_target_pairs={{0,1},{1,0},{2,3},{3,2},{4,5},{5,4},{6,7},{7,6},{8,9},{9,8},{10,11... | collective-permute-start | bytes 1179656 | tf_op jit(solution)/shard_map/ppermute | solution.py:535
  4.3 13.9 %collective-permute-start.2 = (bf16[192,1024]{1,0:T(8,128)(2,1)S(1)}, bf16[192,1024]{1,0:T(8,128)(2,1)S(1)}, u32[]{:S(2)}, u32[]{:S(2)}) collective-permute-start(bf16[192,1024]{1,0:T(8,128)(2,1)S(1)} %get-tuple-element.32), channel_id=1, source_target_pairs={{1,2},{2,1},{5,6},{6,5},{9,10},{10,9},{13,14},{14,13},{17,18},{18,... | collective-permute-start | bytes 1179656 | tf_op jit(solution)/shard_map/ppermute | solution.py:535
  4.9 19.0 %collective-permute-start.4 = (bf16[192,1024]{1,0:T(8,128)(2,1)S(1)}, bf16[192,1024]{1,0:T(8,128)(2,1)S(1)}, u32[]{:S(2)}, u32[]{:S(2)}) collective-permute-start(bf16[192,1024]{1,0:T(8,128)(2,1)S(1)} %get-tuple-element.29.low), channel_id=1, source_target_pairs={{0,2},{3,1},{4,6},{7,5},{8,10},{11,9},{12,14},{15,13},{16,18},{19,... | collective-permute-start | bytes 1179656 | tf_op jit(solution)/shard_map/ppermute | solution.py:535
  13.8 10.1 %collective-permute-start.1 = (bf16[64,1024]{1,0:T(8,128)(2,1)S(1)}, bf16[64,1024]{1,0:T(8,128)(2,1)S(1)}, u32[]{:S(2)}, u32[]{:S(2)}) collective-permute-start(bf16[64,1024]{1,0:T(8,128)(2,1)S(1)} %get-tuple-element.31.last), channel_id=1, source_target_pairs={{0,1},{3,2},{4,5},{7,6},{8,9},{11,10},{12,13},{15,14},{16,17},{19,... | collective-permute-start | bytes 393224 | tf_op jit(solution)/shard_map/ppermute | solution.py:535
  18.2 19.6 %collective-permute-start.3 = (bf16[192,1024]{1,0:T(8,128)(2,1)S(1)}, bf16[192,1024]{1,0:T(8,128)(2,1)S(1)}, u32[]{:S(2)}, u32[]{:S(2)}) collective-permute-start(bf16[192,1024]{1,0:T(8,128)(2,1)S(1)} %collective-permute-done.2.inner), channel_id=1, source_target_pairs={{1,0},{2,3},{5,4},{6,7},{9,8},{10,11},{13,12},{14,15},{17,16},{18,... | collective-permute-start | bytes 1179656 | tf_op jit(solution)/shard_map/ppermute | solution.py:535
  23.9 2.0 %copy-start = (s32[64]{0:T(128)S(1)}, s32[64]{0:T(128)}, u32[]{:S(2)}) copy-start(s32[64]{0:T(128)} %source_hbm.1) | copy-start | bytes 772
  23.9 2.0 %copy-start.1 = (s32[64]{0:T(128)S(1)}, s32[64]{0:T(128)}, u32[]{:S(2)}) copy-start(s32[64]{0:T(128)} %utt_ref.1) | copy-start | bytes 772
  23.9 6.1 %collective-permute-start.6 = (bf16[128,1024]{1,0:T(8,128)(2,1)S(1)}, bf16[128,1024]{1,0:T(8,128)(2,1)S(1)}, u32[]{:S(2)}, u32[]{:S(2)}) collective-permute-start(bf16[128,1024]{1,0:T(8,128)(2,1)S(1)} %lay_call.1), channel_id=1, source_target_pairs={{1,2},{2,1},{5,6},{6,5},{9,10},{10,9},{13,14},{14,13},{17,18},{18,... | collective-permute-start | bytes 786440 | tf_op jit(solution)/shard_map/ppermute | solution.py:535
  24.6 19.6 %collective-permute-start.5 = (bf16[192,1024]{1,0:T(8,128)(2,1)S(1)}, bf16[192,1024]{1,0:T(8,128)(2,1)S(1)}, u32[]{:S(2)}, u32[]{:S(2)}) collective-permute-start(bf16[192,1024]{1,0:T(8,128)(2,1)S(1)} %collective-permute-done.4.far), channel_id=1, source_target_pairs={{1,0},{2,3},{5,4},{6,7},{9,8},{10,11},{13,12},{14,15},{17,16},{18,... | collective-permute-start | bytes 1179656 | tf_op jit(solution)/shard_map/ppermute | solution.py:535
where the time goes:
time: 52.9 us; the launch traced here: 52.7 us
  waiting for transfers between devices  18.2 us (34%)
  starting transfers between devices  17.2 us (33%)
  Pallas kernels  17.1 us (32%)
    ppermute x7, waiting for transfers between devices, swap(): return lax.ppermute(value, 'ctx', perm)  18.2 us
    ppermute x7, starting transfers between devices, swap(): return lax.ppermute(value, 'ctx', perm)  17.2 us
    pallas_call x1, Pallas kernels, line_block(): pl.pallas_call(final_kernel, out_shape=(shape(rows_dev), shape(held_rows)...  8.47 us
    pallas_call x1, Pallas kernels, line_block(): pl.pallas_call(early_kernel, out_shape=(shape(early_rows, wide), shape(ea...  2.82 us
    pallas_call x1, Pallas kernels, hold(): pl.pallas_call(hold_kernel, out_shape=tuple((pltpu.VMEM(a.shape, a.dtype)...  2.26 us
    pallas_call x1, Pallas kernels, line_block(): pl.pallas_call(tables_kernel, out_shape=(jax.ShapeDtypeStruct((plan_sizes...  1.82 us
    pallas_call x1, Pallas kernels, line_block(): pl.pallas_call(arrange_kernel, out_shape=tuple((pltpu.VMEM((n, width), fr...  1.13 us
  transfers between devices with their start and end apart: 7, of which 4 were waited for; matrix products, arithmetic and copies ran while one was open for 0% of the time, Pallas kernels for 14%

commit v1 on v0

--- a/solution.py
+++ b/solution.py
@@ -260,7 +260,6 @@
 
 
 COUNT = 4
-SWAP_OUTER = [(0, 1), (1, 0), (2, 3), (3, 2)]
 SWAP_INNER = [(1, 2), (2, 1)]
 TO_ENDS = [(1, 0), (2, 3)]
 FROM_ENDS = [(0, 1), (3, 2)]
@@ -278,7 +277,8 @@
 
 
 def arrange_kernel(
-    me_ref, source_hbm, rows_hbm, low_ref, last_ref, high_ref, start_ref, source_ref, rows, slots, sems
+    me_ref, source_hbm, rows_hbm, whole_ref, low_ref, last_ref, high_ref, start_ref,
+    source_ref, rows, slots, sems,
 ):
     me = me_ref[0]
     rows_dev, quarter_rows = rows.shape[0], last_ref.shape[0]
@@ -301,6 +301,7 @@
     for place in range(tiles_dev):
         tile = rows[pl.ds(pl.multiple_of(slots[place] * TILE, TILE), TILE), :]
         row = place * TILE
+        whole_ref[row : row + TILE] = tile
         if row < rows_dev - quarter_rows:
             low_ref[row : row + TILE] = tile
         else:
@@ -415,26 +416,26 @@
 
 
 def early_kernel(
-    me_ref, plan, low, last, near, near_last, inner, inner_end,
+    me_ref, plan, whole, near_in, near_out, inner, inner_end,
     key_weight, value_weight, key_ref, value_ref, grouped, rows,
 ):
     me = me_ref[0]
     is_end = (me == 0) | (me == COUNT - 1)
-    piece, quarter_rows = low.shape[0], last.shape[0]
-    base = piece + quarter_rows
-    rows[0:piece] = low[...]
-    rows[piece:base] = last[...]
-    rows[base : base + piece] = near[...]
+    base, piece = whole.shape[0], near_in.shape[0]
+    rows[0:base] = whole[...]
 
     @pl.when(is_end)
     def _():
+        rows[base : base + piece] = near_in[...]
         rows[base + piece : base + 2 * piece] = inner_end[...]
+        rows[base + 2 * piece :] = jnp.zeros((base - piece, rows.shape[1]), rows.dtype)
 
     @pl.when(jnp.logical_not(is_end))
     def _():
+        rows[base : base + piece] = near_out[:piece]
         rows[base + piece : base + 2 * piece] = inner[...]
-
-    rows[base + 2 * piece :] = near_last[...]
+        rows[base + 2 * piece :] = near_out[piece:]
+
     for i in range(grouped.shape[0] // TILE):
         place = jnp.maximum(plan[i], 0)
         grouped[i * TILE : (i + 1) * TILE] = rows[
@@ -445,10 +446,10 @@
     value_ref[...] = project(normed, value_weight)
 
 
-def lay_kernel(first_ref, second_ref, out_ref):
-    rows = first_ref.shape[0]
-    out_ref[:rows] = first_ref[...]
-    out_ref[rows:] = second_ref[...]
+def middle_kernel(first, second, key_weight_ref, value_weight_ref, key_ref, value_ref):
+    normed = layer_norm(jnp.concatenate([first[...], second[...]], axis=0)).astype(jnp.bfloat16)
+    key_ref[...] = project(normed, key_weight_ref)
+    value_ref[...] = project(normed, value_weight_ref)
 
 
 def final_kernel(
@@ -491,10 +492,6 @@
         residual, plan, places_at, half_taps, half_shift[...], out_hbm, padded, residual_rows,
         out, write_sems,
     )
-
-
-def after(value, other):
-    return lax.optimization_barrier((value, other))[0]
 
 
 def line_block(
@@ -516,11 +513,11 @@
             flops=4 * rows * width * wide, bytes_accessed=rows * width * 4, transcendentals=rows
         )
 
-    low, last, high, start = pl.pallas_call(
+    whole, low, last, high, start = pl.pallas_call(
         arrange_kernel,
-        out_shape=tuple(pltpu.VMEM((n, width), frames.dtype) for n in (piece, quarter, piece, quarter)),
+        out_shape=tuple(pltpu.VMEM((n, width), frames.dtype) for n in (rows_dev, piece, quarter, piece, quarter)),
         in_specs=[SMEM] + [HBM] * 2,
-        out_specs=(VMEM,) * 4,
+        out_specs=(VMEM,) * 5,
         scratch_shapes=[
             pltpu.SMEM((total,), jnp.int32),
             pltpu.VMEM((rows_dev, width), jnp.bfloat16),
@@ -534,7 +531,7 @@
     def swap(value, perm):
         return lax.ppermute(value, "ctx", perm)
 
-    near = swap(low, SWAP_OUTER)
+    near_in = swap(low, TO_ENDS)
     inner = swap(high, SWAP_INNER)
     held_rows = rows_dev + 2 * TILE
     plan, key_utt, query_utt = pl.pallas_call(
@@ -556,38 +553,31 @@
     )
     far = swap(low, OVER_TWO)
     inner_end = swap(inner, TO_ENDS)
-    near_last = swap(after(last, near), FROM_ENDS)
+    near_out = swap(whole, FROM_ENDS)
     far_end = swap(far, TO_ENDS)
-    rest = pl.pallas_call(
-        lay_kernel,
-        out_shape=shape(2 * quarter),
-        in_specs=[VMEM] * 2,
-        out_specs=VMEM,
-        compiler_params=params(4),
-        name="lay_call",
-    )(start, near_last)
-    rest = swap(after(rest, far), SWAP_INNER)
+    inner_start = swap(start, SWAP_INNER)
+    far_last = swap(last, OVER_TWO)
 
     early_rows = rows_dev + 2 * piece + quarter
     early_key, early_value, grouped = pl.pallas_call(
         early_kernel,
         out_shape=(shape(early_rows, wide), shape(early_rows, wide), shape(held_rows)),
-        in_specs=[SMEM] * 2 + [VMEM] * 8,
+        in_specs=[SMEM] * 2 + [VMEM] * 7,
         out_specs=(VMEM,) * 3,
         scratch_shapes=[pltpu.VMEM((early_rows, width), jnp.bfloat16)],
         compiler_params=params(16),
         cost_estimate=cost(early_rows),
         name="early_call",
-    )(me, plan, low, last, near, near_last, inner, inner_end, key_weight, value_weight)
+    )(me, plan, whole, near_in, near_out, inner, inner_end, key_weight, value_weight)
     middle_key, middle_value = pl.pallas_call(
-        key_value_kernel,
+        middle_kernel,
         out_shape=(shape(2 * quarter, wide),) * 2,
-        in_specs=[VMEM] * 3,
+        in_specs=[VMEM] * 4,
         out_specs=(VMEM,) * 2,
         compiler_params=params(8),
         cost_estimate=cost(2 * quarter),
         name="middle_call",
-    )(rest, key_weight, value_weight)
+    )(inner_start, far_last, key_weight, value_weight)
     return pl.pallas_call(
         final_kernel,
         out_shape=(shape(rows_dev), shape(held_rows)),

time: 52.9 us -> 52.9 us (level)
  waiting for transfers between devices: 18.2 us -> 4.75 us
  starting transfers between devices: 17.2 us -> 30.5 us
    ppermute x7 -> x8, waiting for transfers between devices: 18.2 us -> 4.75 us  [swap(): return lax.ppermute(value, 'ctx', perm)]
    ppermute x7 -> x8, starting transfers between devices: 17.2 us -> 30.5 us  [swap(): return lax.ppermute(value, 'ctx', perm)]
  transfers between devices with their start and end apart: 7 -> 8, of which waited for: 4 -> 1; matrix products, arithmetic and copies ran while one was open for 0% -> 0% of each run, Pallas kernels for 14% -> 14%
where the time goes in v1:
time: 52.9 us; the launch traced here: 52.6 us
  starting transfers between devices  30.5 us (58%)
  Pallas kernels  17.1 us (32%)
  waiting for transfers between devices  4.75 us (9%)
    ppermute x8, starting transfers between devices, swap(): return lax.ppermute(value, 'ctx', perm)  30.5 us
    pallas_call x1, Pallas kernels, line_block(): pl.pallas_call(final_kernel, out_shape=(shape(rows_dev), shape(held_rows)...  8.48 us
    ppermute x8, waiting for transfers between devices, swap(): return lax.ppermute(value, 'ctx', perm)  4.75 us
    pallas_call x1, Pallas kernels, line_block(): pl.pallas_call(early_kernel, out_shape=(shape(early_rows, wide), shape(ea...  2.78 us
    pallas_call x1, Pallas kernels, hold(): pl.pallas_call(hold_kernel, out_shape=tuple((pltpu.VMEM(a.shape, a.dtype)...  2.26 us
    pallas_call x1, Pallas kernels, line_block(): pl.pallas_call(tables_kernel, out_shape=(jax.ShapeDtypeStruct((plan_sizes...  1.82 us
    pallas_call x1, Pallas kernels, line_block(): pl.pallas_call(arrange_kernel, out_shape=tuple((pltpu.VMEM((n, width), fr...  1.16 us
  transfers between devices with their start and end apart: 8, of which 1 were waited for; matrix products, arithmetic and copies ran while one was open for 0% of the time, Pallas kernels for 14%

profile of v1, /device:TPU:0, one launch (start us, length us, event | category | flops | bytes accessed | tf_op | source)
XLA Modules:
  0.0 52.6 jit_solution(629970356790980019)
XLA Ops:
  0.0 1.2 %arrange.1 = (bf16[256,1024]{1,0:T(8,128)(2,1)S(1)}, bf16[192,1024]{1,0:T(8,128)(2,1)S(1)}, bf16[64,1024]{1,0:T(8,128)(2,1)S(1)}, bf16[192,1024]{1,0:T(8,128)(2,1)S(1)}, bf16[64,1024]{1,0:T(8,128)(2,1)S(1)}) custom-call(s32[1]{0:T(128)} %bitcast.me_ref, s32[64]{0:T(128)} %source_hbm.1, bf16[256,1024]{1,0:T(8,128)(2,1)} %rows_hbm.1), custom_call_target="tpu_custom_call" | custom-call | tf_op jit(solution)/shard_map/arrange/pallas_call | solution.py:516
  1.2 0.7 %collective-permute-start.2 = (bf16[192,1024]{1,0:T(8,128)(2,1)S(1)}, bf16[192,1024]{1,0:T(8,128)(2,1)S(1)}, u32[]{:S(2)}, u32[]{:S(2)}) collective-permute-start(bf16[192,1024]{1,0:T(8,128)(2,1)S(1)} %get-tuple-element.30), channel_id=1, source_target_pairs={{1,2},{2,1},{5,6},{6,5},{9,10},{10,9},{13,14},{14,13},{17,18},{18,... | collective-permute-start | bytes 1179656 | tf_op jit(solution)/shard_map/ppermute | solution.py:532
  1.9 7.7 %collective-permute-start.4 = (bf16[192,1024]{1,0:T(8,128)(2,1)S(1)}, bf16[192,1024]{1,0:T(8,128)(2,1)S(1)}, u32[]{:S(2)}, u32[]{:S(2)}) collective-permute-start(bf16[192,1024]{1,0:T(8,128)(2,1)S(1)} %get-tuple-element.29), channel_id=1, source_target_pairs={{0,2},{3,1},{4,6},{7,5},{8,10},{11,9},{12,14},{15,13},{16,18},{19,... | collective-permute-start | bytes 1179656 | tf_op jit(solution)/shard_map/ppermute | solution.py:532
  9.5 1.4 %collective-permute-start.1 = (bf16[256,1024]{1,0:T(8,128)(2,1)S(1)}, bf16[256,1024]{1,0:T(8,128)(2,1)S(1)}, u32[]{:S(2)}, u32[]{:S(2)}) collective-permute-start(bf16[256,1024]{1,0:T(8,128)(2,1)S(1)} %get-tuple-element.28.whole), channel_id=1, source_target_pairs={{0,1},{3,2},{4,5},{7,6},{8,9},{11,10},{12,13},{15,14},{16,17},{19,... | collective-permute-start | bytes 1572872 | tf_op jit(solution)/shard_map/ppermute | solution.py:532
  11.0 1.3 %collective-permute-start = (bf16[192,1024]{1,0:T(8,128)(2,1)S(1)}, bf16[192,1024]{1,0:T(8,128)(2,1)S(1)}, u32[]{:S(2)}, u32[]{:S(2)}) collective-permute-start(bf16[192,1024]{1,0:T(8,128)(2,1)S(1)} %get-tuple-element.29), channel_id=1, source_target_pairs={{1,0},{2,3},{5,4},{6,7},{9,8},{10,11},{13,12},{14,15},{17,16},{18,... | collective-permute-start | bytes 1179656 | tf_op jit(solution)/shard_map/ppermute | solution.py:532
  12.3 0.0 collective-permute-done.2.inner
  12.3 1.3 %collective-permute-start.3 = (bf16[192,1024]{1,0:T(8,128)(2,1)S(1)}, bf16[192,1024]{1,0:T(8,128)(2,1)S(1)}, u32[]{:S(2)}, u32[]{:S(2)}) collective-permute-start(bf16[192,1024]{1,0:T(8,128)(2,1)S(1)} %collective-permute-done.2.inner), channel_id=1, source_target_pairs={{1,0},{2,3},{5,4},{6,7},{9,8},{10,11},{13,12},{14,15},{17,16},{18,... | collective-permute-start | bytes 1179656 | tf_op jit(solution)/shard_map/ppermute | solution.py:532
  13.6 0.0 copy-start
  13.6 0.0 copy-start.1
  13.6 0.7 %collective-permute-start.6 = (bf16[64,1024]{1,0:T(8,128)(2,1)S(1)}, bf16[64,1024]{1,0:T(8,128)(2,1)S(1)}, u32[]{:S(2)}, u32[]{:S(2)}) collective-permute-start(bf16[64,1024]{1,0:T(8,128)(2,1)S(1)} %get-tuple-element.36), channel_id=1, source_target_pairs={{1,2},{2,1},{5,6},{6,5},{9,10},{10,9},{13,14},{14,13},{17,18},{18,... | collective-permute-start | bytes 393224 | tf_op jit(solution)/shard_map/ppermute | solution.py:532
  14.3 4.7 %collective-permute-done.4.far = bf16[192,1024]{1,0:T(8,128)(2,1)S(1)} collective-permute-done((bf16[192,1024]{1,0:T(8,128)(2,1)S(1)}, bf16[192,1024]{1,0:T(8,128)(2,1)S(1)}, u32[]{:S(2)}, u32[]{:S(2)}) %collective-permute-start.4) | collective-permute-done | bytes 393248 | tf_op jit(solution)/shard_map/ppermute | solution.py:532
  19.0 1.3 %collective-permute-start.5 = (bf16[192,1024]{1,0:T(8,128)(2,1)S(1)}, bf16[192,1024]{1,0:T(8,128)(2,1)S(1)}, u32[]{:S(2)}, u32[]{:S(2)}) collective-permute-start(bf16[192,1024]{1,0:T(8,128)(2,1)S(1)} %collective-permute-done.4.far), channel_id=1, source_target_pairs={{1,0},{2,3},{5,4},{6,7},{9,8},{10,11},{13,12},{14,15},{17,16},{18,... | collective-permute-start | bytes 1179656 | tf_op jit(solution)/shard_map/ppermute | solution.py:532
  20.3 0.0 collective-permute-done.6.first
  20.3 16.2 %collective-permute-start.7 = (bf16[64,1024]{1,0:T(8,128)(2,1)S(1)}, bf16[64,1024]{1,0:T(8,128)(2,1)S(1)}, u32[]{:S(2)}, u32[]{:S(2)}) collective-permute-start(bf16[64,1024]{1,0:T(8,128)(2,1)S(1)} %get-tuple-element.37), channel_id=1, source_target_pairs={{0,2},{3,1},{4,6},{7,5},{8,10},{11,9},{12,14},{15,13},{16,18},{19,... | collective-permute-start | bytes 393224 | tf_op jit(solution)/shard_map/ppermute | solution.py:532
  36.5 1.8 %tables_call.1 = (s32[70]{0:T(128)S(1)}, s32[1,1024]{1,0:T(1,128)S(1)}, s32[288,128]{1,0:T(8,128)S(1)}) custom-call(s32[1]{0:T(128)} %bitcast.me_ref, s32[64]{0:T(128)S(1)} %copy-done, s32[64]{0:T(128)S(1)} %copy-done.1), custom_call_target="tpu_custom_call" | custom-call | tf_op jit(solution)/shard_map/tables_call/pallas_call | solution.py:537
  38.4 2.3 %hold_call.1 = (bf16[1024,512]{1,0:T(8,128)(2,1)S(1)}, bf16[1024,512]{1,0:T(8,128)(2,1)S(1)}, bf16[1024,512]{1,0:T(8,128)(2,1)S(1)}, bf16[512,1024]{1,0:T(8,128)...) custom-call(bf16[1024,512]{1,0:T(8,128)(2,1)} %refs_0_.1, bf16[1024,512]{1,0:T(8,128)(2,1)} %refs_1_.1, ...), custom_call_target="tpu_custom_call" | custom-call | bytes 8388608 | tf_op jit(solution)/shard_map/hold_call/pallas_call | solution.py:336
  40.6 0.0 collective-permute-done.7.second
  40.6 0.6 %middle_call.1 = (bf16[128,512]{1,0:T(8,128)(2,1)S(1)}, bf16[128,512]{1,0:T(8,128)(2,1)S(1)}) custom-call(bf16[64,1024]{1,0:T(8,128)(2,1)S(1)} %collective-permute-done.6.first, bf16[64,1024]{1,0:T(8,128)(2,1)S(1)} %collective-permute-done.7.second, bf16[1024,512]{1,0:T(8,128)(2,1)S(1)} %get-tuple-element.31.key_weight.key_weight_ref, ...), custom_call_target="tpu_custom_call" | custom-call | flops 268435456 | bytes 524288 | tf_op jit(solution)/shard_map/middle_call/pallas_call | solution.py:572
  41.3 0.0 collective-permute-done.near_in
  41.3 0.0 collective-permute-done.1.near_out
  41.3 0.0 collective-permute-done.3.inner_end
  41.3 2.8 %early_call.1 = (bf16[704,512]{1,0:T(8,128)(2,1)S(1)}, bf16[704,512]{1,0:T(8,128)(2,1)S(1)}, bf16[288,1024]{1,0:T(8,128)(2,1)S(1)}) custom-call(s32[1]{0:T(128)} %bitcast.me_ref, s32[70]{0:T(128)S(1)} %get-tuple-element.25.plan, bf16[256,1024]{1,0:T(8,128)(2,1)S(1)} %get-tuple-element.28.whole, bf16[192,1024]{1,0:T(8,128)(2,1)S(1)} %collective-permute-done.near_in, ...), custom_call_target="tpu_custom_call" | custom-call | flops 1476395008 | bytes 2883584 | tf_op jit(solution)/shard_map/early_call/pallas_call | solution.py:562
  44.1 0.0 collective-permute-done.5.far_end
  44.1 8.5 %final.1 = (bf16[256,1024]{1,0:T(8,128)(2,1)}, bf16[288,1024]{1,0:T(8,128)(2,1)S(1)}) custom-call(s32[1]{0:T(128)} %bitcast.me_ref, s32[70]{0:T(128)S(1)} %get-tuple-element.25.plan, s32[288,128]{1,0:T(8,128)S(1)} %get-tuple-element.26.query_utt, s32[1,1024]{1,0:T(1,128)S(1)} %get-tuple-element.27.key_utt, ...), custom_call_target="tpu_custom_call", output_to_operand_aliasing={{1}: (4, {})} | custom-call | flops 2147483648 | bytes 8388608 | tf_op jit(solution)/shard_map/final/pallas_call | solution.py:581
  (2 shorter events, 0.0 us)
Async XLA Ops:
  1.2 11.1 %collective-permute-start.2 = (bf16[192,1024]{1,0:T(8,128)(2,1)S(1)}, bf16[192,1024]{1,0:T(8,128)(2,1)S(1)}, u32[]{:S(2)}, u32[]{:S(2)}) collective-permute-start(bf16[192,1024]{1,0:T(8,128)(2,1)S(1)} %get-tuple-element.30), channel_id=1, source_target_pairs={{1,2},{2,1},{5,6},{6,5},{9,10},{10,9},{13,14},{14,13},{17,18},{18,... | collective-permute-start | bytes 1179656 | tf_op jit(solution)/shard_map/ppermute | solution.py:532
  1.9 17.1 %collective-permute-start.4 = (bf16[192,1024]{1,0:T(8,128)(2,1)S(1)}, bf16[192,1024]{1,0:T(8,128)(2,1)S(1)}, u32[]{:S(2)}, u32[]{:S(2)}) collective-permute-start(bf16[192,1024]{1,0:T(8,128)(2,1)S(1)} %get-tuple-element.29), channel_id=1, source_target_pairs={{0,2},{3,1},{4,6},{7,5},{8,10},{11,9},{12,14},{15,13},{16,18},{19,... | collective-permute-start | bytes 1179656 | tf_op jit(solution)/shard_map/ppermute | solution.py:532
  9.5 31.7 %collective-permute-start.1 = (bf16[256,1024]{1,0:T(8,128)(2,1)S(1)}, bf16[256,1024]{1,0:T(8,128)(2,1)S(1)}, u32[]{:S(2)}, u32[]{:S(2)}) collective-permute-start(bf16[256,1024]{1,0:T(8,128)(2,1)S(1)} %get-tuple-element.28.whole), channel_id=1, source_target_pairs={{0,1},{3,2},{4,5},{7,6},{8,9},{11,10},{12,13},{15,14},{16,17},{19,... | collective-permute-start | bytes 1572872 | tf_op jit(solution)/shard_map/ppermute | solution.py:532
  11.0 30.3 %collective-permute-start = (bf16[192,1024]{1,0:T(8,128)(2,1)S(1)}, bf16[192,1024]{1,0:T(8,128)(2,1)S(1)}, u32[]{:S(2)}, u32[]{:S(2)}) collective-permute-start(bf16[192,1024]{1,0:T(8,128)(2,1)S(1)} %get-tuple-element.29), channel_id=1, source_target_pairs={{1,0},{2,3},{5,4},{6,7},{9,8},{10,11},{13,12},{14,15},{17,16},{18,... | collective-permute-start | bytes 1179656 | tf_op jit(solution)/shard_map/ppermute | solution.py:532
  12.3 29.0 %collective-permute-start.3 = (bf16[192,1024]{1,0:T(8,128)(2,1)S(1)}, bf16[192,1024]{1,0:T(8,128)(2,1)S(1)}, u32[]{:S(2)}, u32[]{:S(2)}) collective-permute-start(bf16[192,1024]{1,0:T(8,128)(2,1)S(1)} %collective-permute-done.2.inner), channel_id=1, source_target_pairs={{1,0},{2,3},{5,4},{6,7},{9,8},{10,11},{13,12},{14,15},{17,16},{18,... | collective-permute-start | bytes 1179656 | tf_op jit(solution)/shard_map/ppermute | solution.py:532
  13.6 22.9 %copy-start = (s32[64]{0:T(128)S(1)}, s32[64]{0:T(128)}, u32[]{:S(2)}) copy-start(s32[64]{0:T(128)} %source_hbm.1) | copy-start | bytes 772
  13.6 22.9 %copy-start.1 = (s32[64]{0:T(128)S(1)}, s32[64]{0:T(128)}, u32[]{:S(2)}) copy-start(s32[64]{0:T(128)} %utt_ref.1) | copy-start | bytes 772
  13.6 6.7 %collective-permute-start.6 = (bf16[64,1024]{1,0:T(8,128)(2,1)S(1)}, bf16[64,1024]{1,0:T(8,128)(2,1)S(1)}, u32[]{:S(2)}, u32[]{:S(2)}) collective-permute-start(bf16[64,1024]{1,0:T(8,128)(2,1)S(1)} %get-tuple-element.36), channel_id=1, source_target_pairs={{1,2},{2,1},{5,6},{6,5},{9,10},{10,9},{13,14},{14,13},{17,18},{18,... | collective-permute-start | bytes 393224 | tf_op jit(solution)/shard_map/ppermute | solution.py:532
  19.0 25.1 %collective-permute-start.5 = (bf16[192,1024]{1,0:T(8,128)(2,1)S(1)}, bf16[192,1024]{1,0:T(8,128)(2,1)S(1)}, u32[]{:S(2)}, u32[]{:S(2)}) collective-permute-start(bf16[192,1024]{1,0:T(8,128)(2,1)S(1)} %collective-permute-done.4.far), channel_id=1, source_target_pairs={{1,0},{2,3},{5,4},{6,7},{9,8},{10,11},{13,12},{14,15},{17,16},{18,... | collective-permute-start | bytes 1179656 | tf_op jit(solution)/shard_map/ppermute | solution.py:532
  20.3 20.3 %collective-permute-start.7 = (bf16[64,1024]{1,0:T(8,128)(2,1)S(1)}, bf16[64,1024]{1,0:T(8,128)(2,1)S(1)}, u32[]{:S(2)}, u32[]{:S(2)}) collective-permute-start(bf16[64,1024]{1,0:T(8,128)(2,1)S(1)} %get-tuple-element.37), channel_id=1, source_target_pairs={{0,2},{3,1},{4,6},{7,5},{8,10},{11,9},{12,14},{15,13},{16,18},{19,... | collective-permute-start | bytes 393224 | tf_op jit(solution)/shard_map/ppermute | solution.py:532

commit v2 on v0

--- a/solution.py
+++ b/solution.py
@@ -381,11 +381,11 @@
         quarter = quarter_of(source, divide(position, tiles_dev))
         row = quarter * quarter_tiles + ranks[position]
         early = jnp.where(apart == 0, row, -1)
-        near = tiles_dev + row + jnp.where(quarter == COUNT - 1, 3 * quarter_tiles, 0)
-        early = jnp.where(apart == 1, near, early)
+        near_last = (apart == 1) & (quarter == COUNT - 1)
+        early = jnp.where((apart == 1) & (quarter < COUNT - 1), tiles_dev + row, early)
         early = jnp.where(apart == second, tiles_dev + 2 * quarter_tiles + row, early)
         plan_ref[i] = early
-        plan_ref[held + i] = jnp.where(apart == third, row, -1)
+        plan_ref[held + i] = jnp.where((apart == third) | near_last, row, -1)
         query_utt_ref[i * TILE : (i + 1) * TILE] = jnp.full(
             (TILE, 128), utt_ref[position], jnp.int32
         )
@@ -415,7 +415,7 @@
 
 
 def early_kernel(
-    me_ref, plan, low, last, near, near_last, inner, inner_end,
+    me_ref, plan, low, last, near, inner, inner_end,
     key_weight, value_weight, key_ref, value_ref, grouped, rows,
 ):
     me = me_ref[0]
@@ -428,13 +428,12 @@
 
     @pl.when(is_end)
     def _():
-        rows[base + piece : base + 2 * piece] = inner_end[...]
+        rows[base + piece :] = inner_end[...]
 
     @pl.when(jnp.logical_not(is_end))
     def _():
-        rows[base + piece : base + 2 * piece] = inner[...]
-
-    rows[base + 2 * piece :] = near_last[...]
+        rows[base + piece :] = inner[...]
+
     for i in range(grouped.shape[0] // TILE):
         place = jnp.maximum(plan[i], 0)
         grouped[i * TILE : (i + 1) * TILE] = rows[
@@ -445,14 +444,16 @@
     value_ref[...] = project(normed, value_weight)
 
 
-def lay_kernel(first_ref, second_ref, out_ref):
-    rows = first_ref.shape[0]
-    out_ref[:rows] = first_ref[...]
-    out_ref[rows:] = second_ref[...]
+def middle_kernel(*refs):
+    parts, (key_weight, value_weight, key_ref, value_ref) = refs[:-4], refs[-4:]
+    rows = jnp.concatenate([part[...] for part in parts], axis=0)
+    normed = layer_norm(rows).astype(jnp.bfloat16)
+    key_ref[...] = project(normed, key_weight)
+    value_ref[...] = project(normed, value_weight)
 
 
 def final_kernel(
-    me_ref, plan, query_utt, key_utt, early_grouped, far, far_end,
+    me_ref, plan, query_utt, key_utt, early_grouped, far, far_end, near_last,
     early_key, early_value, middle_key, middle_value,
     key_weight, value_weight, query_weight, output_weight, half_taps, half_shift,
     out_hbm, grouped, padded, residual_rows, out, write_sems, late,
@@ -460,14 +461,15 @@
     me = me_ref[0]
     is_end = (me == 0) | (me == COUNT - 1)
     held, places_at, _ = plan_sizes(out.shape[0] // TILE)
+    late[far.shape[0] :] = near_last[...]
 
     @pl.when(is_end)
     def _():
-        late[...] = far_end[...]
+        late[: far.shape[0]] = far_end[...]
 
     @pl.when(jnp.logical_not(is_end))
     def _():
-        late[...] = far[...]
+        late[: far.shape[0]] = far[...]
 
     for i in range(held):
         row = plan[held + i]
@@ -479,7 +481,7 @@
             ]
 
     padded[...] = jnp.zeros_like(padded)
-    normed = layer_norm(late[...]).astype(jnp.bfloat16)
+    normed = layer_norm(late[: far.shape[0]]).astype(jnp.bfloat16)
     late_key = project(normed, key_weight)
     late_value = project(normed, value_weight)
     residual = attend(
@@ -491,10 +493,6 @@
         residual, plan, places_at, half_taps, half_shift[...], out_hbm, padded, residual_rows,
         out, write_sems,
     )
-
-
-def after(value, other):
-    return lax.optimization_barrier((value, other))[0]
 
 
 def line_block(
@@ -556,52 +554,45 @@
     )
     far = swap(low, OVER_TWO)
     inner_end = swap(inner, TO_ENDS)
-    near_last = swap(after(last, near), FROM_ENDS)
     far_end = swap(far, TO_ENDS)
-    rest = pl.pallas_call(
-        lay_kernel,
-        out_shape=shape(2 * quarter),
-        in_specs=[VMEM] * 2,
-        out_specs=VMEM,
-        compiler_params=params(4),
-        name="lay_call",
-    )(start, near_last)
-    rest = swap(after(rest, far), SWAP_INNER)
-
-    early_rows = rows_dev + 2 * piece + quarter
+    far_last = swap(last, OVER_TWO)
+    near_last = swap(last, FROM_ENDS)
+    inner_start = swap(start, SWAP_INNER)
+
+    early_rows = rows_dev + 2 * piece
     early_key, early_value, grouped = pl.pallas_call(
         early_kernel,
         out_shape=(shape(early_rows, wide), shape(early_rows, wide), shape(held_rows)),
-        in_specs=[SMEM] * 2 + [VMEM] * 8,
+        in_specs=[SMEM] * 2 + [VMEM] * 7,
         out_specs=(VMEM,) * 3,
         scratch_shapes=[pltpu.VMEM((early_rows, width), jnp.bfloat16)],
         compiler_params=params(16),
         cost_estimate=cost(early_rows),
         name="early_call",
-    )(me, plan, low, last, near, near_last, inner, inner_end, key_weight, value_weight)
+    )(me, plan, low, last, near, inner, inner_end, key_weight, value_weight)
     middle_key, middle_value = pl.pallas_call(
-        key_value_kernel,
-        out_shape=(shape(2 * quarter, wide),) * 2,
-        in_specs=[VMEM] * 3,
+        middle_kernel,
+        out_shape=(shape(3 * quarter, wide),) * 2,
+        in_specs=[VMEM] * 5,
         out_specs=(VMEM,) * 2,
         compiler_params=params(8),
-        cost_estimate=cost(2 * quarter),
+        cost_estimate=cost(3 * quarter),
         name="middle_call",
-    )(rest, key_weight, value_weight)
+    )(near_last, inner_start, far_last, key_weight, value_weight)
     return pl.pallas_call(
         final_kernel,
         out_shape=(shape(rows_dev), shape(held_rows)),
-        in_specs=[SMEM] * 2 + [VMEM] * 15,
+        in_specs=[SMEM] * 2 + [VMEM] * 16,
         out_specs=(HBM, VMEM),
         input_output_aliases={4: 1},
-        scratch_shapes=block_scratch(rows_dev, width) + [pltpu.VMEM((piece, width), jnp.bfloat16)],
+        scratch_shapes=block_scratch(rows_dev, width) + [pltpu.VMEM((rows_dev, width), jnp.bfloat16)],
         compiler_params=params(28),
         cost_estimate=pl.CostEstimate(
             flops=2 << 30, bytes_accessed=8 << 20, transcendentals=1 << 20
         ),
         name="final",
     )(
-        me, plan, query_utt, key_utt, grouped, far, far_end,
+        me, plan, query_utt, key_utt, grouped, far, far_end, near_last,
         early_key, early_value, middle_key, middle_value,
         key_weight, value_weight, query_weight, output_weight, half_taps, half_shift,
     )[0]

time: 52.9 us -> 52.5 us (level)
  waiting for transfers between devices: 18.2 us -> 0.02 us
  starting transfers between devices: 17.2 us -> 35 us
    ppermute x7 -> x8, waiting for transfers between devices: 18.2 us -> 0.02 us  [swap(): return lax.ppermute(value, 'ctx', perm)]
    ppermute x7 -> x8, starting transfers between devices: 17.2 us -> 35 us  [swap(): return lax.ppermute(value, 'ctx', perm)]
  transfers between devices with their start and end apart: 7 -> 8, of which waited for: 4 -> 0; matrix products, arithmetic and copies ran while one was open for 0% -> 0% of each run, Pallas kernels for 14% -> 14%
where the time goes in v2:
time: 52.5 us; the launch traced here: 52.3 us
  starting transfers between devices  35 us (67%)
  Pallas kernels  17.1 us (33%)
    ppermute x8, starting transfers between devices, swap(): return lax.ppermute(value, 'ctx', perm)  35 us
    pallas_call x1, Pallas kernels, line_block(): pl.pallas_call(final_kernel, out_shape=(shape(rows_dev), shape(held_rows)...  8.48 us
    pallas_call x1, Pallas kernels, line_block(): pl.pallas_call(early_kernel, out_shape=(shape(early_rows, wide), shape(ea...  2.62 us
    pallas_call x1, Pallas kernels, hold(): pl.pallas_call(hold_kernel, out_shape=tuple((pltpu.VMEM(a.shape, a.dtype)...  2.26 us
    pallas_call x1, Pallas kernels, line_block(): pl.pallas_call(tables_kernel, out_shape=(jax.ShapeDtypeStruct((plan_sizes...  1.84 us
    pallas_call x1, Pallas kernels, line_block(): pl.pallas_call(arrange_kernel, out_shape=tuple((pltpu.VMEM((n, width), fr...  1.13 us
  transfers between devices with their start and end apart: 8, of which 0 were waited for; matrix products, arithmetic and copies ran while one was open for 0% of the time, Pallas kernels for 14%

profile of v2, /device:TPU:0, one launch (start us, length us, event | category | flops | bytes accessed | tf_op | source)
XLA Modules:
  0.0 52.3 jit_solution(1248888009484127533)
XLA Ops:
  0.0 1.1 %arrange.1 = (bf16[192,1024]{1,0:T(8,128)(2,1)S(1)}, bf16[64,1024]{1,0:T(8,128)(2,1)S(1)}, bf16[192,1024]{1,0:T(8,128)(2,1)S(1)}, bf16[64,1024]{1,0:T(8,128)(2,1)S(1)}) custom-call(s32[1]{0:T(128)} %bitcast.me_ref, s32[64]{0:T(128)} %source_hbm.1, bf16[256,1024]{1,0:T(8,128)(2,1)} %rows_hbm.1), custom_call_target="tpu_custom_call" | custom-call | tf_op jit(solution)/shard_map/arrange/pallas_call | solution.py:517
  1.1 0.7 %collective-permute-start.1 = (bf16[192,1024]{1,0:T(8,128)(2,1)S(1)}, bf16[192,1024]{1,0:T(8,128)(2,1)S(1)}, u32[]{:S(2)}, u32[]{:S(2)}) collective-permute-start(bf16[192,1024]{1,0:T(8,128)(2,1)S(1)} %get-tuple-element.29), channel_id=1, source_target_pairs={{1,2},{2,1},{5,6},{6,5},{9,10},{10,9},{13,14},{14,13},{17,18},{18,... | collective-permute-start | bytes 1179656 | tf_op jit(solution)/shard_map/ppermute | solution.py:533
  1.8 7.7 %collective-permute-start.3 = (bf16[192,1024]{1,0:T(8,128)(2,1)S(1)}, bf16[192,1024]{1,0:T(8,128)(2,1)S(1)}, u32[]{:S(2)}, u32[]{:S(2)}) collective-permute-start(bf16[192,1024]{1,0:T(8,128)(2,1)S(1)} %get-tuple-element.27.low), channel_id=1, source_target_pairs={{0,2},{3,1},{4,6},{7,5},{8,10},{11,9},{12,14},{15,13},{16,18},{19,... | collective-permute-start | bytes 1179656 | tf_op jit(solution)/shard_map/ppermute | solution.py:533
  9.5 0.1 collective-permute-start
  9.6 0.0 collective-permute-done.1.inner
  9.6 1.3 %collective-permute-start.2 = (bf16[192,1024]{1,0:T(8,128)(2,1)S(1)}, bf16[192,1024]{1,0:T(8,128)(2,1)S(1)}, u32[]{:S(2)}, u32[]{:S(2)}) collective-permute-start(bf16[192,1024]{1,0:T(8,128)(2,1)S(1)} %collective-permute-done.1.inner), channel_id=1, source_target_pairs={{1,0},{2,3},{5,4},{6,7},{9,8},{10,11},{13,12},{14,15},{17,16},{18,... | collective-permute-start | bytes 1179656 | tf_op jit(solution)/shard_map/ppermute | solution.py:533
  10.9 0.0 copy-start
  10.9 0.0 copy-start.1
  10.9 17.7 %collective-permute-start.5 = (bf16[64,1024]{1,0:T(8,128)(2,1)S(1)}, bf16[64,1024]{1,0:T(8,128)(2,1)S(1)}, u32[]{:S(2)}, u32[]{:S(2)}) collective-permute-start(bf16[64,1024]{1,0:T(8,128)(2,1)S(1)} %get-tuple-element.28.last), channel_id=1, source_target_pairs={{0,1},{3,2},{4,5},{7,6},{8,9},{11,10},{12,13},{15,14},{16,17},{19,... | collective-permute-start | bytes 393224 | tf_op jit(solution)/shard_map/ppermute | solution.py:533
  28.6 0.0 collective-permute-done.3.far
  28.6 1.3 %collective-permute-start.4 = (bf16[192,1024]{1,0:T(8,128)(2,1)S(1)}, bf16[192,1024]{1,0:T(8,128)(2,1)S(1)}, u32[]{:S(2)}, u32[]{:S(2)}) collective-permute-start(bf16[192,1024]{1,0:T(8,128)(2,1)S(1)} %collective-permute-done.3.far), channel_id=1, source_target_pairs={{1,0},{2,3},{5,4},{6,7},{9,8},{10,11},{13,12},{14,15},{17,16},{18,... | collective-permute-start | bytes 1179656 | tf_op jit(solution)/shard_map/ppermute | solution.py:533
  29.9 5.6 %collective-permute-start.7 = (bf16[64,1024]{1,0:T(8,128)(2,1)S(1)}, bf16[64,1024]{1,0:T(8,128)(2,1)S(1)}, u32[]{:S(2)}, u32[]{:S(2)}) collective-permute-start(bf16[64,1024]{1,0:T(8,128)(2,1)S(1)} %get-tuple-element.28.last), channel_id=1, source_target_pairs={{0,2},{3,1},{4,6},{7,5},{8,10},{11,9},{12,14},{15,13},{16,18},{19,... | collective-permute-start | bytes 393224 | tf_op jit(solution)/shard_map/ppermute | solution.py:533
  35.5 0.0 collective-permute-done.5.refs_0_.near_last
  35.5 0.7 %collective-permute-start.6 = (bf16[64,1024]{1,0:T(8,128)(2,1)S(1)}, bf16[64,1024]{1,0:T(8,128)(2,1)S(1)}, u32[]{:S(2)}, u32[]{:S(2)}) collective-permute-start(bf16[64,1024]{1,0:T(8,128)(2,1)S(1)} %get-tuple-element.35), channel_id=1, source_target_pairs={{1,2},{2,1},{5,6},{6,5},{9,10},{10,9},{13,14},{14,13},{17,18},{18,... | collective-permute-start | bytes 393224 | tf_op jit(solution)/shard_map/ppermute | solution.py:533
  36.2 1.8 %tables_call.1 = (s32[70]{0:T(128)S(1)}, s32[1,1024]{1,0:T(1,128)S(1)}, s32[288,128]{1,0:T(8,128)S(1)}) custom-call(s32[1]{0:T(128)} %bitcast.me_ref, s32[64]{0:T(128)S(1)} %copy-done, s32[64]{0:T(128)S(1)} %copy-done.1), custom_call_target="tpu_custom_call" | custom-call | tf_op jit(solution)/shard_map/tables_call/pallas_call | solution.py:538
  38.1 2.3 %hold_call.1 = (bf16[1024,512]{1,0:T(8,128)(2,1)S(1)}, bf16[1024,512]{1,0:T(8,128)(2,1)S(1)}, bf16[1024,512]{1,0:T(8,128)(2,1)S(1)}, bf16[512,1024]{1,0:T(8,128)...) custom-call(bf16[1024,512]{1,0:T(8,128)(2,1)} %refs_0_.1, bf16[1024,512]{1,0:T(8,128)(2,1)} %refs_1_.1, ...), custom_call_target="tpu_custom_call" | custom-call | bytes 8388608 | tf_op jit(solution)/shard_map/hold_call/pallas_call | solution.py:335
  40.3 0.0 collective-permute-done.7.refs_2_
  40.3 0.0 collective-permute-done.6.refs_1_
  40.4 0.8 %middle_call.1 = (bf16[192,512]{1,0:T(8,128)(2,1)S(1)}, bf16[192,512]{1,0:T(8,128)(2,1)S(1)}) custom-call(bf16[64,1024]{1,0:T(8,128)(2,1)S(1)} %collective-permute-done.5.refs_0_.near_last, bf16[64,1024]{1,0:T(8,128)(2,1)S(1)} %collective-permute-done.6.refs_1_, bf16[64,1024]{1,0:T(8,128)(2,1)S(1)} %collective-permute-done.7.refs_2_, ...), custom_call_target="tpu_custom_call" | custom-call | flops 402653184 | bytes 786432 | tf_op jit(solution)/shard_map/middle_call/pallas_call | solution.py:573
  41.1 0.0 collective-permute-done.near
  41.2 0.0 collective-permute-done.2.inner_end
  41.2 2.6 %early_call.1 = (bf16[640,512]{1,0:T(8,128)(2,1)S(1)}, bf16[640,512]{1,0:T(8,128)(2,1)S(1)}, bf16[288,1024]{1,0:T(8,128)(2,1)S(1)}) custom-call(s32[1]{0:T(128)} %bitcast.me_ref, s32[70]{0:T(128)S(1)} %get-tuple-element.24.plan, bf16[192,1024]{1,0:T(8,128)(2,1)S(1)} %get-tuple-element.27.low, bf16[64,1024]{1,0:T(8,128)(2,1)S(1)} %get-tuple-element.28.last, ...), custom_call_target="tpu_custom_call" | custom-call | flops 1342177280 | bytes 2621440 | tf_op jit(solution)/shard_map/early_call/pallas_call | solution.py:563
  43.8 0.0 collective-permute-done.4.far_end
  43.8 8.5 %final.1 = (bf16[256,1024]{1,0:T(8,128)(2,1)}, bf16[288,1024]{1,0:T(8,128)(2,1)S(1)}) custom-call(s32[1]{0:T(128)} %bitcast.me_ref, s32[70]{0:T(128)S(1)} %get-tuple-element.24.plan, s32[288,128]{1,0:T(8,128)S(1)} %get-tuple-element.25.query_utt, s32[1,1024]{1,0:T(1,128)S(1)} %get-tuple-element.26.key_utt, ...), custom_call_target="tpu_custom_call", output_to_operand_aliasing={{1}: (4, {})} | custom-call | flops 2147483648 | bytes 8388608 | tf_op jit(solution)/shard_map/final/pallas_call | solution.py:582
  (2 shorter events, 0.0 us)
Async XLA Ops:
  1.1 8.4 %collective-permute-start.1 = (bf16[192,1024]{1,0:T(8,128)(2,1)S(1)}, bf16[192,1024]{1,0:T(8,128)(2,1)S(1)}, u32[]{:S(2)}, u32[]{:S(2)}) collective-permute-start(bf16[192,1024]{1,0:T(8,128)(2,1)S(1)} %get-tuple-element.29), channel_id=1, source_target_pairs={{1,2},{2,1},{5,6},{6,5},{9,10},{10,9},{13,14},{14,13},{17,18},{18,... | collective-permute-start | bytes 1179656 | tf_op jit(solution)/shard_map/ppermute | solution.py:533
  1.8 26.8 %collective-permute-start.3 = (bf16[192,1024]{1,0:T(8,128)(2,1)S(1)}, bf16[192,1024]{1,0:T(8,128)(2,1)S(1)}, u32[]{:S(2)}, u32[]{:S(2)}) collective-permute-start(bf16[192,1024]{1,0:T(8,128)(2,1)S(1)} %get-tuple-element.27.low), channel_id=1, source_target_pairs={{0,2},{3,1},{4,6},{7,5},{8,10},{11,9},{12,14},{15,13},{16,18},{19,... | collective-permute-start | bytes 1179656 | tf_op jit(solution)/shard_map/ppermute | solution.py:533
  9.5 31.7 %collective-permute-start = (bf16[192,1024]{1,0:T(8,128)(2,1)S(1)}, bf16[192,1024]{1,0:T(8,128)(2,1)S(1)}, u32[]{:S(2)}, u32[]{:S(2)}) collective-permute-start(bf16[192,1024]{1,0:T(8,128)(2,1)S(1)} %get-tuple-element.27.low), channel_id=1, source_target_pairs={{0,1},{1,0},{2,3},{3,2},{4,5},{5,4},{6,7},{7,6},{8,9},{9,8},{10,11... | collective-permute-start | bytes 1179656 | tf_op jit(solution)/shard_map/ppermute | solution.py:533
  9.6 31.6 %collective-permute-start.2 = (bf16[192,1024]{1,0:T(8,128)(2,1)S(1)}, bf16[192,1024]{1,0:T(8,128)(2,1)S(1)}, u32[]{:S(2)}, u32[]{:S(2)}) collective-permute-start(bf16[192,1024]{1,0:T(8,128)(2,1)S(1)} %collective-permute-done.1.inner), channel_id=1, source_target_pairs={{1,0},{2,3},{5,4},{6,7},{9,8},{10,11},{13,12},{14,15},{17,16},{18,... | collective-permute-start | bytes 1179656 | tf_op jit(solution)/shard_map/ppermute | solution.py:533
  10.9 25.3 %copy-start = (s32[64]{0:T(128)S(1)}, s32[64]{0:T(128)}, u32[]{:S(2)}) copy-start(s32[64]{0:T(128)} %source_hbm.1) | copy-start | bytes 772
  10.9 25.3 %copy-start.1 = (s32[64]{0:T(128)S(1)}, s32[64]{0:T(128)}, u32[]{:S(2)}) copy-start(s32[64]{0:T(128)} %utt_ref.1) | copy-start | bytes 772
  10.9 24.6 %collective-permute-start.5 = (bf16[64,1024]{1,0:T(8,128)(2,1)S(1)}, bf16[64,1024]{1,0:T(8,128)(2,1)S(1)}, u32[]{:S(2)}, u32[]{:S(2)}) collective-permute-start(bf16[64,1024]{1,0:T(8,128)(2,1)S(1)} %get-tuple-element.28.last), channel_id=1, source_target_pairs={{0,1},{3,2},{4,5},{7,6},{8,9},{11,10},{12,13},{15,14},{16,17},{19,... | collective-permute-start | bytes 393224 | tf_op jit(solution)/shard_map/ppermute | solution.py:533
  28.6 15.2 %collective-permute-start.4 = (bf16[192,1024]{1,0:T(8,128)(2,1)S(1)}, bf16[192,1024]{1,0:T(8,128)(2,1)S(1)}, u32[]{:S(2)}, u32[]{:S(2)}) collective-permute-start(bf16[192,1024]{1,0:T(8,128)(2,1)S(1)} %collective-permute-done.3.far), channel_id=1, source_target_pairs={{1,0},{2,3},{5,4},{6,7},{9,8},{10,11},{13,12},{14,15},{17,16},{18,... | collective-permute-start | bytes 1179656 | tf_op jit(solution)/shard_map/ppermute | solution.py:533
  29.9 10.4 %collective-permute-start.7 = (bf16[64,1024]{1,0:T(8,128)(2,1)S(1)}, bf16[64,1024]{1,0:T(8,128)(2,1)S(1)}, u32[]{:S(2)}, u32[]{:S(2)}) collective-permute-start(bf16[64,1024]{1,0:T(8,128)(2,1)S(1)} %get-tuple-element.28.last), channel_id=1, source_target_pairs={{0,2},{3,1},{4,6},{7,5},{8,10},{11,9},{12,14},{15,13},{16,18},{19,... | collective-permute-start | bytes 393224 | tf_op jit(solution)/shard_map/ppermute | solution.py:533
  35.5 4.8 %collective-permute-start.6 = (bf16[64,1024]{1,0:T(8,128)(2,1)S(1)}, bf16[64,1024]{1,0:T(8,128)(2,1)S(1)}, u32[]{:S(2)}, u32[]{:S(2)}) collective-permute-start(bf16[64,1024]{1,0:T(8,128)(2,1)S(1)} %get-tuple-element.35), channel_id=1, source_target_pairs={{1,2},{2,1},{5,6},{6,5},{9,10},{10,9},{13,14},{14,13},{17,18},{18,... | collective-permute-start | bytes 393224 | tf_op jit(solution)/shard_map/ppermute | solution.py:533

commit v3 on v2

--- a/solution.py
+++ b/solution.py
@@ -347,7 +347,7 @@
 
 def plan_sizes(tiles_dev):
     held = tiles_dev + 2
-    return held, 2 * held, 3 * held + tiles_dev
+    return held, 3 * held, 4 * held + tiles_dev
 
 
 def tables_kernel(
@@ -383,7 +383,7 @@
         early = jnp.where(apart == 0, row, -1)
         near_last = (apart == 1) & (quarter == COUNT - 1)
         early = jnp.where((apart == 1) & (quarter < COUNT - 1), tiles_dev + row, early)
-        early = jnp.where(apart == second, tiles_dev + 2 * quarter_tiles + row, early)
+        plan_ref[2 * held + i] = jnp.where(apart == second, row - quarter_tiles, -1)
         plan_ref[i] = early
         plan_ref[held + i] = jnp.where((apart == third) | near_last, row, -1)
         query_utt_ref[i * TILE : (i + 1) * TILE] = jnp.full(
@@ -414,31 +414,48 @@
         key_utt_ref[:, start * TILE : start * TILE + 128] = vector
 
 
+def place_tiles(grouped, rows, plan, at):
+    for i in range(grouped.shape[0] // TILE):
+        place = plan[at + i]
+
+        @pl.when(place >= 0)
+        def _(place=place, i=i):
+            grouped[i * TILE : (i + 1) * TILE] = rows[
+                pl.ds(pl.multiple_of(place * TILE, TILE), TILE), :
+            ]
+
+
 def early_kernel(
-    me_ref, plan, low, last, near, inner, inner_end,
-    key_weight, value_weight, key_ref, value_ref, grouped, rows,
-):
-    me = me_ref[0]
-    is_end = (me == 0) | (me == COUNT - 1)
+    plan, low, last, near, key_weight, value_weight, key_ref, value_ref, grouped, rows
+):
     piece, quarter_rows = low.shape[0], last.shape[0]
     base = piece + quarter_rows
     rows[0:piece] = low[...]
     rows[piece:base] = last[...]
-    rows[base : base + piece] = near[...]
+    rows[base:] = near[...]
+    grouped[...] = jnp.zeros_like(grouped)
+    place_tiles(grouped, rows, plan, 0)
+    normed = layer_norm(rows[...]).astype(jnp.bfloat16)
+    key_ref[...] = project(normed, key_weight)
+    value_ref[...] = project(normed, value_weight)
+
+
+def second_kernel(
+    me_ref, plan, early_grouped, inner, inner_end, key_weight, value_weight,
+    key_ref, value_ref, grouped, rows,
+):
+    me = me_ref[0]
+    is_end = (me == 0) | (me == COUNT - 1)
 
     @pl.when(is_end)
     def _():
-        rows[base + piece :] = inner_end[...]
+        rows[...] = inner_end[...]
 
     @pl.when(jnp.logical_not(is_end))
     def _():
-        rows[base + piece :] = inner[...]
-
-    for i in range(grouped.shape[0] // TILE):
-        place = jnp.maximum(plan[i], 0)
-        grouped[i * TILE : (i + 1) * TILE] = rows[
-            pl.ds(pl.multiple_of(place * TILE, TILE), TILE), :
-        ]
+        rows[...] = inner[...]
+
+    place_tiles(grouped, rows, plan, 2 * (grouped.shape[0] // TILE))
     normed = layer_norm(rows[...]).astype(jnp.bfloat16)
     key_ref[...] = project(normed, key_weight)
     value_ref[...] = project(normed, value_weight)
@@ -454,7 +471,7 @@
 
 def final_kernel(
     me_ref, plan, query_utt, key_utt, early_grouped, far, far_end, near_last,
-    early_key, early_value, middle_key, middle_value,
+    early_key, early_value, second_key, second_value, middle_key, middle_value,
     key_weight, value_weight, query_weight, output_weight, half_taps, half_shift,
     out_hbm, grouped, padded, residual_rows, out, write_sems, late,
 ):
@@ -471,22 +488,15 @@
     def _():
         late[: far.shape[0]] = far[...]
 
-    for i in range(held):
-        row = plan[held + i]
-
-        @pl.when(row >= 0)
-        def _(row=row, i=i):
-            grouped[i * TILE : (i + 1) * TILE] = late[
-                pl.ds(pl.multiple_of(row * TILE, TILE), TILE), :
-            ]
-
+    place_tiles(grouped, late, plan, held)
     padded[...] = jnp.zeros_like(padded)
     normed = layer_norm(late[: far.shape[0]]).astype(jnp.bfloat16)
     late_key = project(normed, key_weight)
     late_value = project(normed, value_weight)
     residual = attend(
         grouped, query_utt, key_utt[...],
-        [early_key, middle_key, late_key], [early_value, middle_value, late_value],
+        [early_key, second_key, middle_key, late_key],
+        [early_value, second_value, middle_value, late_value],
         query_weight, output_weight,
     )
     convolve(
@@ -559,17 +569,28 @@
     near_last = swap(last, FROM_ENDS)
     inner_start = swap(start, SWAP_INNER)
 
-    early_rows = rows_dev + 2 * piece
+    early_rows = rows_dev + piece
     early_key, early_value, grouped = pl.pallas_call(
         early_kernel,
         out_shape=(shape(early_rows, wide), shape(early_rows, wide), shape(held_rows)),
-        in_specs=[SMEM] * 2 + [VMEM] * 7,
+        in_specs=[SMEM] + [VMEM] * 5,
         out_specs=(VMEM,) * 3,
         scratch_shapes=[pltpu.VMEM((early_rows, width), jnp.bfloat16)],
-        compiler_params=params(16),
+        compiler_params=params(12),
         cost_estimate=cost(early_rows),
         name="early_call",
-    )(me, plan, low, last, near, inner, inner_end, key_weight, value_weight)
+    )(plan, low, last, near, key_weight, value_weight)
+    second_key, second_value, grouped = pl.pallas_call(
+        second_kernel,
+        out_shape=(shape(piece, wide), shape(piece, wide), shape(held_rows)),
+        in_specs=[SMEM] * 2 + [VMEM] * 5,
+        out_specs=(VMEM,) * 3,
+        input_output_aliases={2: 2},
+        scratch_shapes=[pltpu.VMEM((piece, width), jnp.bfloat16)],
+        compiler_params=params(8),
+        cost_estimate=cost(piece),
+        name="second_call",
+    )(me, plan, grouped, inner, inner_end, key_weight, value_weight)
     middle_key, middle_value = pl.pallas_call(
         middle_kernel,
         out_shape=(shape(3 * quarter, wide),) * 2,
@@ -582,7 +603,7 @@
     return pl.pallas_call(
         final_kernel,
         out_shape=(shape(rows_dev), shape(held_rows)),
-        in_specs=[SMEM] * 2 + [VMEM] * 16,
+        in_specs=[SMEM] * 2 + [VMEM] * 18,
         out_specs=(HBM, VMEM),
         input_output_aliases={4: 1},
         scratch_shapes=block_scratch(rows_dev, width) + [pltpu.VMEM((rows_dev, width), jnp.bfloat16)],
@@ -593,7 +614,7 @@
         name="final",
     )(
         me, plan, query_utt, key_utt, grouped, far, far_end, near_last,
-        early_key, early_value, middle_key, middle_value,
+        early_key, early_value, second_key, second_value, middle_key, middle_value,
         key_weight, value_weight, query_weight, output_weight, half_taps, half_shift,
     )[0]
 

time: 52.5 us -> 53.6 us (1.021)
  Pallas kernels: 17.1 us -> 18.2 us
    pallas_call x0 -> x1, Pallas kernels: none -> 1.48 us  [line_block(): pl.pallas_call(second_kernel, out_shape=(shape(piece, wide), shape(piece,...]
  transfers between devices with their start and end apart: 8 -> 8, of which waited for: 0 -> 0; matrix products, arithmetic and copies ran while one was open for 0% -> 0% of each run, Pallas kernels for 14% -> 16%
where the time goes in v3:
time: 53.6 us; the launch traced here: 53.4 us
  starting transfers between devices  35 us (65%)
  Pallas kernels  18.2 us (34%)
    ppermute x8, starting transfers between devices, swap(): return lax.ppermute(value, 'ctx', perm)  35 us
    pallas_call x1, Pallas kernels, line_block(): pl.pallas_call(final_kernel, out_shape=(shape(rows_dev), shape(held_rows)...  8.45 us
    pallas_call x1, Pallas kernels, hold(): pl.pallas_call(hold_kernel, out_shape=tuple((pltpu.VMEM(a.shape, a.dtype)...  2.26 us
    pallas_call x1, Pallas kernels, line_block(): pl.pallas_call(early_kernel, out_shape=(shape(early_rows, wide), shape(ea...  2.24 us
    pallas_call x1, Pallas kernels, line_block(): pl.pallas_call(tables_kernel, out_shape=(jax.ShapeDtypeStruct((plan_sizes...  1.84 us
    pallas_call x1, Pallas kernels, line_block(): pl.pallas_call(second_kernel, out_shape=(shape(piece, wide), shape(piece,...  1.48 us
    pallas_call x1, Pallas kernels, line_block(): pl.pallas_call(arrange_kernel, out_shape=tuple((pltpu.VMEM((n, width), fr...  1.13 us
  transfers between devices with their start and end apart: 8, of which 0 were waited for; matrix products, arithmetic and copies ran while one was open for 0% of the time, Pallas kernels for 16%

profile of v3, /device:TPU:0, one launch (start us, length us, event | category | flops | bytes accessed | tf_op | source)
XLA Modules:
  0.0 53.4 jit_solution(5664896287672212790)
XLA Ops:
  0.0 1.1 %arrange.1 = (bf16[192,1024]{1,0:T(8,128)(2,1)S(1)}, bf16[64,1024]{1,0:T(8,128)(2,1)S(1)}, bf16[192,1024]{1,0:T(8,128)(2,1)S(1)}, bf16[64,1024]{1,0:T(8,128)(2,1)S(1)}) custom-call(s32[1]{0:T(128)} %bitcast.me_ref, s32[64]{0:T(128)} %source_hbm.1, bf16[256,1024]{1,0:T(8,128)(2,1)} %rows_hbm.1), custom_call_target="tpu_custom_call" | custom-call | tf_op jit(solution)/shard_map/arrange/pallas_call | solution.py:527
  1.1 0.7 %collective-permute-start.1 = (bf16[192,1024]{1,0:T(8,128)(2,1)S(1)}, bf16[192,1024]{1,0:T(8,128)(2,1)S(1)}, u32[]{:S(2)}, u32[]{:S(2)}) collective-permute-start(bf16[192,1024]{1,0:T(8,128)(2,1)S(1)} %get-tuple-element.35), channel_id=1, source_target_pairs={{1,2},{2,1},{5,6},{6,5},{9,10},{10,9},{13,14},{14,13},{17,18},{18,... | collective-permute-start | bytes 1179656 | tf_op jit(solution)/shard_map/ppermute | solution.py:543
  1.8 7.7 %collective-permute-start.3 = (bf16[192,1024]{1,0:T(8,128)(2,1)S(1)}, bf16[192,1024]{1,0:T(8,128)(2,1)S(1)}, u32[]{:S(2)}, u32[]{:S(2)}) collective-permute-start(bf16[192,1024]{1,0:T(8,128)(2,1)S(1)} %get-tuple-element.30.low), channel_id=1, source_target_pairs={{0,2},{3,1},{4,6},{7,5},{8,10},{11,9},{12,14},{15,13},{16,18},{19,... | collective-permute-start | bytes 1179656 | tf_op jit(solution)/shard_map/ppermute | solution.py:543
  9.5 0.1 collective-permute-start
  9.6 0.0 collective-permute-done.1.inner
  9.6 1.3 %collective-permute-start.2 = (bf16[192,1024]{1,0:T(8,128)(2,1)S(1)}, bf16[192,1024]{1,0:T(8,128)(2,1)S(1)}, u32[]{:S(2)}, u32[]{:S(2)}) collective-permute-start(bf16[192,1024]{1,0:T(8,128)(2,1)S(1)} %collective-permute-done.1.inner), channel_id=1, source_target_pairs={{1,0},{2,3},{5,4},{6,7},{9,8},{10,11},{13,12},{14,15},{17,16},{18,... | collective-permute-start | bytes 1179656 | tf_op jit(solution)/shard_map/ppermute | solution.py:543
  10.9 0.0 copy-start
  10.9 0.0 copy-start.1
  10.9 17.7 %collective-permute-start.5 = (bf16[64,1024]{1,0:T(8,128)(2,1)S(1)}, bf16[64,1024]{1,0:T(8,128)(2,1)S(1)}, u32[]{:S(2)}, u32[]{:S(2)}) collective-permute-start(bf16[64,1024]{1,0:T(8,128)(2,1)S(1)} %get-tuple-element.31.last), channel_id=1, source_target_pairs={{0,1},{3,2},{4,5},{7,6},{8,9},{11,10},{12,13},{15,14},{16,17},{19,... | collective-permute-start | bytes 393224 | tf_op jit(solution)/shard_map/ppermute | solution.py:543
  28.6 0.0 collective-permute-done.3.far
  28.6 1.3 %collective-permute-start.4 = (bf16[192,1024]{1,0:T(8,128)(2,1)S(1)}, bf16[192,1024]{1,0:T(8,128)(2,1)S(1)}, u32[]{:S(2)}, u32[]{:S(2)}) collective-permute-start(bf16[192,1024]{1,0:T(8,128)(2,1)S(1)} %collective-permute-done.3.far), channel_id=1, source_target_pairs={{1,0},{2,3},{5,4},{6,7},{9,8},{10,11},{13,12},{14,15},{17,16},{18,... | collective-permute-start | bytes 1179656 | tf_op jit(solution)/shard_map/ppermute | solution.py:543
  29.9 5.6 %collective-permute-start.7 = (bf16[64,1024]{1,0:T(8,128)(2,1)S(1)}, bf16[64,1024]{1,0:T(8,128)(2,1)S(1)}, u32[]{:S(2)}, u32[]{:S(2)}) collective-permute-start(bf16[64,1024]{1,0:T(8,128)(2,1)S(1)} %get-tuple-element.31.last), channel_id=1, source_target_pairs={{0,2},{3,1},{4,6},{7,5},{8,10},{11,9},{12,14},{15,13},{16,18},{19,... | collective-permute-start | bytes 393224 | tf_op jit(solution)/shard_map/ppermute | solution.py:543
  35.5 0.0 collective-permute-done.5.refs_0_.near_last
  35.5 0.7 %collective-permute-start.6 = (bf16[64,1024]{1,0:T(8,128)(2,1)S(1)}, bf16[64,1024]{1,0:T(8,128)(2,1)S(1)}, u32[]{:S(2)}, u32[]{:S(2)}) collective-permute-start(bf16[64,1024]{1,0:T(8,128)(2,1)S(1)} %get-tuple-element.41), channel_id=1, source_target_pairs={{1,2},{2,1},{5,6},{6,5},{9,10},{10,9},{13,14},{14,13},{17,18},{18,... | collective-permute-start | bytes 393224 | tf_op jit(solution)/shard_map/ppermute | solution.py:543
  36.2 1.8 %tables_call.1 = (s32[88]{0:T(128)S(1)}, s32[1,1024]{1,0:T(1,128)S(1)}, s32[288,128]{1,0:T(8,128)S(1)}) custom-call(s32[1]{0:T(128)} %bitcast.me_ref, s32[64]{0:T(128)S(1)} %copy-done, s32[64]{0:T(128)S(1)} %copy-done.1), custom_call_target="tpu_custom_call" | custom-call | tf_op jit(solution)/shard_map/tables_call/pallas_call | solution.py:548
  38.1 2.3 %hold_call.1 = (bf16[1024,512]{1,0:T(8,128)(2,1)S(1)}, bf16[1024,512]{1,0:T(8,128)(2,1)S(1)}, bf16[1024,512]{1,0:T(8,128)(2,1)S(1)}, bf16[512,1024]{1,0:T(8,128)...) custom-call(bf16[1024,512]{1,0:T(8,128)(2,1)} %refs_0_.1, bf16[1024,512]{1,0:T(8,128)(2,1)} %refs_1_.1, ...), custom_call_target="tpu_custom_call" | custom-call | bytes 8388608 | tf_op jit(solution)/shard_map/hold_call/pallas_call | solution.py:335
  40.3 0.0 collective-permute-done.7.refs_2_
  40.4 0.0 collective-permute-done.6.refs_1_
  40.4 0.8 %middle_call.1 = (bf16[192,512]{1,0:T(8,128)(2,1)S(1)}, bf16[192,512]{1,0:T(8,128)(2,1)S(1)}) custom-call(bf16[64,1024]{1,0:T(8,128)(2,1)S(1)} %collective-permute-done.5.refs_0_.near_last, bf16[64,1024]{1,0:T(8,128)(2,1)S(1)} %collective-permute-done.6.refs_1_, bf16[64,1024]{1,0:T(8,128)(2,1)S(1)} %collective-permute-done.7.refs_2_, ...), custom_call_target="tpu_custom_call" | custom-call | flops 402653184 | bytes 786432 | tf_op jit(solution)/shard_map/middle_call/pallas_call | solution.py:594
  41.2 0.0 collective-permute-done.near
  41.2 2.2 %early_call.1 = (bf16[448,512]{1,0:T(8,128)(2,1)S(1)}, bf16[448,512]{1,0:T(8,128)(2,1)S(1)}, bf16[288,1024]{1,0:T(8,128)(2,1)S(1)}) custom-call(s32[88]{0:T(128)S(1)} %get-tuple-element.27.plan, bf16[192,1024]{1,0:T(8,128)(2,1)S(1)} %get-tuple-element.30.low, bf16[64,1024]{1,0:T(8,128)(2,1)S(1)} %get-tuple-element.31.last, ...), custom_call_target="tpu_custom_call" | custom-call | flops 939524096 | bytes 1835008 | tf_op jit(solution)/shard_map/early_call/pallas_call | solution.py:573
  43.4 1.5 %second_call.1 = (bf16[192,512]{1,0:T(8,128)(2,1)S(1)}, bf16[192,512]{1,0:T(8,128)(2,1)S(1)}, bf16[288,1024]{1,0:T(8,128)(2,1)S(1)}) custom-call(s32[1]{0:T(128)} %bitcast.me_ref, s32[88]{0:T(128)S(1)} %get-tuple-element.27.plan, bf16[288,1024]{1,0:T(8,128)(2,1)S(1)} %get-tuple-element.34.early_grouped, ...), custom_call_target="tpu_custom_call", output_to_operand_aliasing={{2}: (2, {})} | custom-call | flops 402653184 | bytes 786432 | tf_op jit(solution)/shard_map/second_call/pallas_call | solution.py:583
  44.9 0.0 collective-permute-done.4.far_end
  44.9 8.4 %final.1 = (bf16[256,1024]{1,0:T(8,128)(2,1)}, bf16[288,1024]{1,0:T(8,128)(2,1)S(1)}) custom-call(s32[1]{0:T(128)} %bitcast.me_ref, s32[88]{0:T(128)S(1)} %get-tuple-element.27.plan, s32[288,128]{1,0:T(8,128)S(1)} %get-tuple-element.28.query_utt, s32[1,1024]{1,0:T(1,128)S(1)} %get-tuple-element.29.key_utt, ...), custom_call_target="tpu_custom_call", output_to_operand_aliasing={{1}: (4, {})} | custom-call | flops 2147483648 | bytes 8388608 | tf_op jit(solution)/shard_map/final/pallas_call | solution.py:603
  (3 shorter events, 0.0 us)
Async XLA Ops:
  1.1 8.4 %collective-permute-start.1 = (bf16[192,1024]{1,0:T(8,128)(2,1)S(1)}, bf16[192,1024]{1,0:T(8,128)(2,1)S(1)}, u32[]{:S(2)}, u32[]{:S(2)}) collective-permute-start(bf16[192,1024]{1,0:T(8,128)(2,1)S(1)} %get-tuple-element.35), channel_id=1, source_target_pairs={{1,2},{2,1},{5,6},{6,5},{9,10},{10,9},{13,14},{14,13},{17,18},{18,... | collective-permute-start | bytes 1179656 | tf_op jit(solution)/shard_map/ppermute | solution.py:543
  1.8 26.8 %collective-permute-start.3 = (bf16[192,1024]{1,0:T(8,128)(2,1)S(1)}, bf16[192,1024]{1,0:T(8,128)(2,1)S(1)}, u32[]{:S(2)}, u32[]{:S(2)}) collective-permute-start(bf16[192,1024]{1,0:T(8,128)(2,1)S(1)} %get-tuple-element.30.low), channel_id=1, source_target_pairs={{0,2},{3,1},{4,6},{7,5},{8,10},{11,9},{12,14},{15,13},{16,18},{19,... | collective-permute-start | bytes 1179656 | tf_op jit(solution)/shard_map/ppermute | solution.py:543
  9.5 31.7 %collective-permute-start = (bf16[192,1024]{1,0:T(8,128)(2,1)S(1)}, bf16[192,1024]{1,0:T(8,128)(2,1)S(1)}, u32[]{:S(2)}, u32[]{:S(2)}) collective-permute-start(bf16[192,1024]{1,0:T(8,128)(2,1)S(1)} %get-tuple-element.30.low), channel_id=1, source_target_pairs={{0,1},{1,0},{2,3},{3,2},{4,5},{5,4},{6,7},{7,6},{8,9},{9,8},{10,11... | collective-permute-start | bytes 1179656 | tf_op jit(solution)/shard_map/ppermute | solution.py:543
  9.6 33.8 %collective-permute-start.2 = (bf16[192,1024]{1,0:T(8,128)(2,1)S(1)}, bf16[192,1024]{1,0:T(8,128)(2,1)S(1)}, u32[]{:S(2)}, u32[]{:S(2)}) collective-permute-start(bf16[192,1024]{1,0:T(8,128)(2,1)S(1)} %collective-permute-done.1.inner), channel_id=1, source_target_pairs={{1,0},{2,3},{5,4},{6,7},{9,8},{10,11},{13,12},{14,15},{17,16},{18,... | collective-permute-start | bytes 1179656 | tf_op jit(solution)/shard_map/ppermute | solution.py:543
  10.9 25.3 %copy-start = (s32[64]{0:T(128)S(1)}, s32[64]{0:T(128)}, u32[]{:S(2)}) copy-start(s32[64]{0:T(128)} %source_hbm.1) | copy-start | bytes 772
  10.9 25.3 %copy-start.1 = (s32[64]{0:T(128)S(1)}, s32[64]{0:T(128)}, u32[]{:S(2)}) copy-start(s32[64]{0:T(128)} %utt_ref.1) | copy-start | bytes 772
  10.9 24.6 %collective-permute-start.5 = (bf16[64,1024]{1,0:T(8,128)(2,1)S(1)}, bf16[64,1024]{1,0:T(8,128)(2,1)S(1)}, u32[]{:S(2)}, u32[]{:S(2)}) collective-permute-start(bf16[64,1024]{1,0:T(8,128)(2,1)S(1)} %get-tuple-element.31.last), channel_id=1, source_target_pairs={{0,1},{3,2},{4,5},{7,6},{8,9},{11,10},{12,13},{15,14},{16,17},{19,... | collective-permute-start | bytes 393224 | tf_op jit(solution)/shard_map/ppermute | solution.py:543
  28.6 16.3 %collective-permute-start.4 = (bf16[192,1024]{1,0:T(8,128)(2,1)S(1)}, bf16[192,1024]{1,0:T(8,128)(2,1)S(1)}, u32[]{:S(2)}, u32[]{:S(2)}) collective-permute-start(bf16[192,1024]{1,0:T(8,128)(2,1)S(1)} %collective-permute-done.3.far), channel_id=1, source_target_pairs={{1,0},{2,3},{5,4},{6,7},{9,8},{10,11},{13,12},{14,15},{17,16},{18,... | collective-permute-start | bytes 1179656 | tf_op jit(solution)/shard_map/ppermute | solution.py:543
  29.9 10.4 %collective-permute-start.7 = (bf16[64,1024]{1,0:T(8,128)(2,1)S(1)}, bf16[64,1024]{1,0:T(8,128)(2,1)S(1)}, u32[]{:S(2)}, u32[]{:S(2)}) collective-permute-start(bf16[64,1024]{1,0:T(8,128)(2,1)S(1)} %get-tuple-element.31.last), channel_id=1, source_target_pairs={{0,2},{3,1},{4,6},{7,5},{8,10},{11,9},{12,14},{15,13},{16,18},{19,... | collective-permute-start | bytes 393224 | tf_op jit(solution)/shard_map/ppermute | solution.py:543
  35.5 4.8 %collective-permute-start.6 = (bf16[64,1024]{1,0:T(8,128)(2,1)S(1)}, bf16[64,1024]{1,0:T(8,128)(2,1)S(1)}, u32[]{:S(2)}, u32[]{:S(2)}) collective-permute-start(bf16[64,1024]{1,0:T(8,128)(2,1)S(1)} %get-tuple-element.41), channel_id=1, source_target_pairs={{1,2},{2,1},{5,6},{6,5},{9,10},{10,9},{13,14},{14,13},{17,18},{18,... | collective-permute-start | bytes 393224 | tf_op jit(solution)/shard_map/ppermute | solution.py:543

commit v4 on v3

--- a/solution.py
+++ b/solution.py
@@ -37,11 +37,13 @@
     return jnp.dot(rows, weight_ref[...], preferred_element_type=jnp.float32).astype(jnp.bfloat16)
 
 
-def attend(
-    grouped, query_utt, key_utt, key_parts, value_parts, query_weight, output_weight
-):
+def mask_bias(query_utt, key_utt):
+    return jnp.where(query_utt == key_utt, 0.0, NEGATIVE)
+
+
+def attend(grouped, bias, key_parts, value_parts, query_weight, output_weight):
     queries = project(layer_norm(grouped[...]).astype(jnp.bfloat16), query_weight)
-    allowed = query_utt[:, :1] == key_utt
+    ones = jnp.ones((bias.shape[1], HEAD_DIM), jnp.bfloat16)
     exponent_scale = math.log2(math.e) / math.sqrt(HEAD_DIM)
     heads = []
     for head in range(HEADS):
@@ -54,14 +56,15 @@
             (((1,), (1,)), ((), ())),
             preferred_element_type=jnp.float32,
         )
-        scores = jnp.where(allowed, scores, NEGATIVE)
+        scores = scores + bias[...]
         top = jnp.max(scores, axis=-1, keepdims=True)
         weights = jnp.exp2((scores - top) * exponent_scale)
-        row_sum = jnp.sum(weights, axis=-1, keepdims=True)
         summed = jnp.dot(
-            weights.astype(jnp.bfloat16), value_head, preferred_element_type=jnp.float32
+            weights.astype(jnp.bfloat16),
+            jnp.concatenate([value_head, ones], axis=1),
+            preferred_element_type=jnp.float32,
         )
-        heads.append((summed / row_sum).astype(jnp.bfloat16))
+        heads.append((summed[:, :HEAD_DIM] / summed[:, HEAD_DIM:]).astype(jnp.bfloat16))
     attended = jnp.concatenate(heads, axis=1)
     return (
         grouped[...].astype(jnp.float32)
@@ -204,9 +207,8 @@
         pltpu.make_async_copy(
             chunks[0].at[pl.ds(0, TILE), :], grouped.at[pl.ds(i * TILE, TILE), :], sems.at[i]
         ).wait()
-    residual = attend(
-        grouped, query_utt, key_utt_ref[...], keys, values, query_weight, output_weight
-    )
+    bias = mask_bias(query_utt[:, :1], key_utt_ref[...])
+    residual = attend(grouped, bias, keys, values, query_weight, output_weight)
     convolve(
         residual, plan, 0, half_taps, 0.5 * shift[...], out_hbm, padded, residual_rows, out,
         write_sems,
@@ -351,7 +353,8 @@
 
 
 def tables_kernel(
-    me_ref, source_ref, utt_ref, plan_ref, key_utt_ref, query_utt_ref, filled, ranks, key_utts
+    me_ref, source_ref, utt_ref, plan_ref, bias_ref, padded_ref,
+    key_utt_ref, query_utt_ref, filled, ranks, key_utts,
 ):
     me = me_ref[0]
     total = source_ref.shape[0]
@@ -412,6 +415,8 @@
         for k in range(1, per_vector):
             vector = jnp.where(lane_tile == k, tile_values[start + k], vector)
         key_utt_ref[:, start * TILE : start * TILE + 128] = vector
+    bias_ref[...] = mask_bias(query_utt_ref[:, :1], key_utt_ref[...])
+    padded_ref[...] = jnp.zeros_like(padded_ref)
 
 
 def place_tiles(grouped, rows, plan, at):
@@ -470,7 +475,7 @@
 
 
 def final_kernel(
-    me_ref, plan, query_utt, key_utt, early_grouped, far, far_end, near_last,
+    me_ref, plan, bias, early_grouped, early_padded, far, far_end, near_last,
     early_key, early_value, second_key, second_value, middle_key, middle_value,
     key_weight, value_weight, query_weight, output_weight, half_taps, half_shift,
     out_hbm, grouped, padded, residual_rows, out, write_sems, late,
@@ -489,12 +494,11 @@
         late[: far.shape[0]] = far[...]
 
     place_tiles(grouped, late, plan, held)
-    padded[...] = jnp.zeros_like(padded)
     normed = layer_norm(late[: far.shape[0]]).astype(jnp.bfloat16)
     late_key = project(normed, key_weight)
     late_value = project(normed, value_weight)
     residual = attend(
-        grouped, query_utt, key_utt[...],
+        grouped, bias,
         [early_key, second_key, middle_key, late_key],
         [early_value, second_value, middle_value, late_value],
         query_weight, output_weight,
@@ -545,17 +549,24 @@
     near = swap(low, SWAP_OUTER)
     inner = swap(high, SWAP_INNER)
     held_rows = rows_dev + 2 * TILE
-    plan, key_utt, query_utt = pl.pallas_call(
+    padded_shape = jax.ShapeDtypeStruct(
+        (width // 128, padded_rows(rows_dev // TILE), 128), jnp.float32
+    )
+    plan, bias, padded = pl.pallas_call(
         tables_kernel,
         out_shape=(
             jax.ShapeDtypeStruct((plan_sizes(rows_dev // TILE)[2],), jnp.int32),
-            shape(1, total * TILE, jnp.int32),
-            shape(held_rows, 128, jnp.int32),
+            shape(held_rows, total * TILE, jnp.float32),
+            padded_shape,
         ),
         in_specs=[SMEM] * 3,
         out_specs=(SMEM, VMEM, VMEM),
-        scratch_shapes=[pltpu.SMEM((n,), jnp.int32) for n in (COUNT * COUNT, total, total)],
-        compiler_params=params(4),
+        scratch_shapes=[
+            pltpu.VMEM((1, total * TILE), jnp.int32),
+            pltpu.VMEM((held_rows, 128), jnp.int32),
+        ]
+        + [pltpu.SMEM((n,), jnp.int32) for n in (COUNT * COUNT, total, total)],
+        compiler_params=params(8),
         name="tables_call",
     )(me, tile_source, tile_utt)
     key_weight, value_weight, query_weight, output_weight, half_taps, half_shift = hold(
@@ -602,18 +613,18 @@
     )(near_last, inner_start, far_last, key_weight, value_weight)
     return pl.pallas_call(
         final_kernel,
-        out_shape=(shape(rows_dev), shape(held_rows)),
+        out_shape=(shape(rows_dev), shape(held_rows), padded_shape),
         in_specs=[SMEM] * 2 + [VMEM] * 18,
-        out_specs=(HBM, VMEM),
-        input_output_aliases={4: 1},
-        scratch_shapes=block_scratch(rows_dev, width) + [pltpu.VMEM((rows_dev, width), jnp.bfloat16)],
+        out_specs=(HBM, VMEM, VMEM),
+        input_output_aliases={3: 1, 4: 2},
+        scratch_shapes=block_scratch(rows_dev, width)[1:] + [pltpu.VMEM((rows_dev, width), jnp.bfloat16)],
         compiler_params=params(28),
         cost_estimate=pl.CostEstimate(
             flops=2 << 30, bytes_accessed=8 << 20, transcendentals=1 << 20
         ),
         name="final",
     )(
-        me, plan, query_utt, key_utt, grouped, far, far_end, near_last,
+        me, plan, bias, grouped, padded, far, far_end, near_last,
         early_key, early_value, second_key, second_value, middle_key, middle_value,
         key_weight, value_weight, query_weight, output_weight, half_taps, half_shift,
     )[0]

time: 53.6 us -> 57.1 us (1.065)
  waiting for transfers between devices: 0.02 us -> 7.73 us
  starting transfers between devices: 35 us -> 27.3 us
  Pallas kernels: 18.2 us -> 20.3 us
  local copies, waits for them, and re-layouts: 0.01 us -> 1.31 us
    ppermute x8, waiting for transfers between devices: 0.02 us -> 7.73 us  [swap(): return lax.ppermute(value, 'ctx', perm)]
    ppermute x8, starting transfers between devices: 35 us -> 27.3 us  [swap(): return lax.ppermute(value, 'ctx', perm)]
    unnamed x4, local copies, waits for them, and re-layouts: 0.01 us -> 1.31 us
    pallas_call x1, Pallas kernels: 1.13 us -> 1.92 us  [line_block(): pl.pallas_call(arrange_kernel, out_shape=tuple((pltpu.VMEM((n, width), fr...]
    pallas_call x1, Pallas kernels: 2.24 us -> 2.89 us  [line_block(): pl.pallas_call(early_kernel, out_shape=(shape(early_rows, wide), shape(ea...]
    pallas_call x1, Pallas kernels: 1.48 us -> 2.07 us  [line_block(): pl.pallas_call(second_kernel, out_shape=(shape(piece, wide), shape(piece,...]
  transfers between devices with their start and end apart: 8 -> 8, of which waited for: 0 -> 1; matrix products, arithmetic and copies ran while one was open for 0% -> 0% of each run, Pallas kernels for 16% -> 17%
where the time goes in v4:
time: 57.1 us; the launch traced here: 56.8 us
  starting transfers between devices  27.3 us (48%)
  Pallas kernels  20.3 us (36%)
  waiting for transfers between devices  7.73 us (14%)
  local copies, waits for them, and re-layouts  1.31 us (2%)
    ppermute x8, starting transfers between devices, swap(): return lax.ppermute(value, 'ctx', perm)  27.3 us
    pallas_call x1, Pallas kernels, line_block(): pl.pallas_call(final_kernel, out_shape=(shape(rows_dev), shape(held_rows)...  8.49 us
    ppermute x8, waiting for transfers between devices, swap(): return lax.ppermute(value, 'ctx', perm)  7.73 us
    pallas_call x1, Pallas kernels, line_block(): pl.pallas_call(early_kernel, out_shape=(shape(early_rows, wide), shape(ea...  2.89 us
    pallas_call x1, Pallas kernels, hold(): pl.pallas_call(hold_kernel, out_shape=tuple((pltpu.VMEM(a.shape, a.dtype)...  2.26 us
    pallas_call x1, Pallas kernels, line_block(): pl.pallas_call(second_kernel, out_shape=(shape(piece, wide), shape(piece,...  2.07 us
    pallas_call x1, Pallas kernels, line_block(): pl.pallas_call(arrange_kernel, out_shape=tuple((pltpu.VMEM((n, width), fr...  1.92 us
    pallas_call x1, Pallas kernels, line_block(): pl.pallas_call(tables_kernel, out_shape=(jax.ShapeDtypeStruct((plan_sizes...  1.85 us
  transfers between devices with their start and end apart: 8, of which 1 were waited for; matrix products, arithmetic and copies ran while one was open for 0% of the time, Pallas kernels for 17%

profile of v4, /device:TPU:0, one launch (start us, length us, event | category | flops | bytes accessed | tf_op | source)
XLA Modules:
  0.0 56.8 jit_solution(12382397084825988798)
XLA Ops:
  0.0 1.9 %arrange.1 = (bf16[192,1024]{1,0:T(8,128)(2,1)}, bf16[64,1024]{1,0:T(8,128)(2,1)}, bf16[192,1024]{1,0:T(8,128)(2,1)S(1)}, bf16[64,1024]{1,0:T(8,128)(2,1)S(1)}) custom-call(s32[1]{0:T(128)} %bitcast.me_ref, s32[64]{0:T(128)} %source_hbm.1, bf16[256,1024]{1,0:T(8,128)(2,1)} %rows_hbm.1), custom_call_target="tpu_custom_call" | custom-call | tf_op jit(solution)/shard_map/arrange/pallas_call | solution.py:531
  1.9 1.4 %collective-permute-start.1 = (bf16[192,1024]{1,0:T(8,128)(2,1)S(1)}, bf16[192,1024]{1,0:T(8,128)(2,1)}, u32[]{:S(2)}, u32[]{:S(2)}) collective-permute-start(bf16[192,1024]{1,0:T(8,128)(2,1)S(1)} %get-tuple-element.34), channel_id=1, source_target_pairs={{1,2},{2,1},{5,6},{6,5},{9,10},{10,9},{13,14},{14,13},{17,18},{18,... | collective-permute-start | bytes 1179656 | tf_op jit(solution)/shard_map/ppermute | solution.py:547
  3.4 6.9 %collective-permute-start.3 = (bf16[192,1024]{1,0:T(8,128)(2,1)}, bf16[192,1024]{1,0:T(8,128)(2,1)S(1)}, u32[]{:S(2)}, u32[]{:S(2)}) collective-permute-start(bf16[192,1024]{1,0:T(8,128)(2,1)} %get-tuple-element.29.low), channel_id=1, source_target_pairs={{0,2},{3,1},{4,6},{7,5},{8,10},{11,9},{12,14},{15,13},{16,18},{19,... | collective-permute-start | bytes 1179656 | tf_op jit(solution)/shard_map/ppermute | solution.py:547
  10.3 0.1 collective-permute-start
  10.4 0.0 collective-permute-done.1.inner
  10.4 1.3 %collective-permute-start.2 = (bf16[192,1024]{1,0:T(8,128)(2,1)}, bf16[192,1024]{1,0:T(8,128)(2,1)}, u32[]{:S(2)}, u32[]{:S(2)}) collective-permute-start(bf16[192,1024]{1,0:T(8,128)(2,1)} %collective-permute-done.1.inner), channel_id=1, source_target_pairs={{1,0},{2,3},{5,4},{6,7},{9,8},{10,11},{13,12},{14,15},{17,16},{18,... | collective-permute-start | bytes 1179656 | tf_op jit(solution)/shard_map/ppermute | solution.py:547
  11.7 0.7 %collective-permute-start.6 = (bf16[64,1024]{1,0:T(8,128)(2,1)S(1)}, bf16[64,1024]{1,0:T(8,128)(2,1)S(1)}, u32[]{:S(2)}, u32[]{:S(2)}) collective-permute-start(bf16[64,1024]{1,0:T(8,128)(2,1)S(1)} %get-tuple-element.41), channel_id=1, source_target_pairs={{1,2},{2,1},{5,6},{6,5},{9,10},{10,9},{13,14},{14,13},{17,18},{18,... | collective-permute-start | bytes 393224 | tf_op jit(solution)/shard_map/ppermute | solution.py:547
  12.4 7.7 %collective-permute-done.3.far = bf16[192,1024]{1,0:T(8,128)(2,1)S(1)} collective-permute-done((bf16[192,1024]{1,0:T(8,128)(2,1)}, bf16[192,1024]{1,0:T(8,128)(2,1)S(1)}, u32[]{:S(2)}, u32[]{:S(2)}) %collective-permute-start.3) | collective-permute-done | bytes 393248 | tf_op jit(solution)/shard_map/ppermute | solution.py:547
  20.1 1.3 %collective-permute-start.4 = (bf16[192,1024]{1,0:T(8,128)(2,1)S(1)}, bf16[192,1024]{1,0:T(8,128)(2,1)S(1)}, u32[]{:S(2)}, u32[]{:S(2)}) collective-permute-start(bf16[192,1024]{1,0:T(8,128)(2,1)S(1)} %collective-permute-done.3.far), channel_id=1, source_target_pairs={{1,0},{2,3},{5,4},{6,7},{9,8},{10,11},{13,12},{14,15},{17,16},{18,... | collective-permute-start | bytes 1179656 | tf_op jit(solution)/shard_map/ppermute | solution.py:547
  21.4 13.5 %collective-permute-start.7 = (bf16[64,1024]{1,0:T(8,128)(2,1)}, bf16[64,1024]{1,0:T(8,128)(2,1)S(1)}, u32[]{:S(2)}, u32[]{:S(2)}) collective-permute-start(bf16[64,1024]{1,0:T(8,128)(2,1)} %get-tuple-element.30.last), channel_id=1, source_target_pairs={{0,2},{3,1},{4,6},{7,5},{8,10},{11,9},{12,14},{15,13},{16,18},{19,... | collective-permute-start | bytes 393224 | tf_op jit(solution)/shard_map/ppermute | solution.py:547
  34.9 0.0 collective-permute-done.6.refs_1_
  34.9 2.1 %collective-permute-start.5 = (bf16[64,1024]{1,0:T(8,128)(2,1)}, bf16[64,1024]{1,0:T(8,128)(2,1)S(1)}, u32[]{:S(2)}, u32[]{:S(2)}) collective-permute-start(bf16[64,1024]{1,0:T(8,128)(2,1)} %get-tuple-element.30.last), channel_id=1, source_target_pairs={{0,1},{3,2},{4,5},{7,6},{8,9},{11,10},{12,13},{15,14},{16,17},{19,... | collective-permute-start | bytes 393224 | tf_op jit(solution)/shard_map/ppermute | solution.py:547
  37.1 0.0 copy-start
  37.1 0.6 %copy-done = s32[64]{0:T(128)S(1)} copy-done((s32[64]{0:T(128)S(1)}, s32[64]{0:T(128)}, u32[]{:S(2)}) %copy-start) | copy-done | bytes 280
  37.7 0.7 %copy-done.1 = s32[64]{0:T(128)S(1)} copy-done((s32[64]{0:T(128)S(1)}, s32[64]{0:T(128)}, u32[]{:S(2)}) %copy-start.1) | copy-done | bytes 280
  38.4 1.8 %tables_call.1 = (s32[88]{0:T(128)S(1)}, f32[288,1024]{1,0:T(8,128)S(1)}, f32[8,384,128]{2,1,0:T(8,128)S(1)}) custom-call(s32[1]{0:T(128)} %bitcast.me_ref, s32[64]{0:T(128)S(1)} %copy-done, s32[64]{0:T(128)S(1)} %copy-done.1), custom_call_target="tpu_custom_call" | custom-call | tf_op jit(solution)/shard_map/tables_call/pallas_call | solution.py:555
  40.2 2.3 %hold_call.1 = (bf16[1024,512]{1,0:T(8,128)(2,1)S(1)}, bf16[1024,512]{1,0:T(8,128)(2,1)S(1)}, bf16[1024,512]{1,0:T(8,128)(2,1)S(1)}, bf16[512,1024]{1,0:T(8,128)...) custom-call(bf16[1024,512]{1,0:T(8,128)(2,1)} %refs_0_.1, bf16[1024,512]{1,0:T(8,128)(2,1)} %refs_1_.1, ...), custom_call_target="tpu_custom_call" | custom-call | bytes 8388608 | tf_op jit(solution)/shard_map/hold_call/pallas_call | solution.py:337
  42.5 0.0 collective-permute-done.7.refs_2_
  42.5 0.0 collective-permute-done.5.refs_0_.near_last
  42.5 0.8 %middle_call.1 = (bf16[192,512]{1,0:T(8,128)(2,1)S(1)}, bf16[192,512]{1,0:T(8,128)(2,1)S(1)}) custom-call(bf16[64,1024]{1,0:T(8,128)(2,1)S(1)} %collective-permute-done.5.refs_0_.near_last, bf16[64,1024]{1,0:T(8,128)(2,1)S(1)} %collective-permute-done.6.refs_1_, bf16[64,1024]{1,0:T(8,128)(2,1)S(1)} %collective-permute-done.7.refs_2_, ...), custom_call_target="tpu_custom_call" | custom-call | flops 402653184 | bytes 786432 | tf_op jit(solution)/shard_map/middle_call/pallas_call | solution.py:605
  43.3 0.0 collective-permute-done.near
  43.3 2.9 %early_call.1 = (bf16[448,512]{1,0:T(8,128)(2,1)S(1)}, bf16[448,512]{1,0:T(8,128)(2,1)S(1)}, bf16[288,1024]{1,0:T(8,128)(2,1)S(1)}) custom-call(s32[88]{0:T(128)S(1)} %get-tuple-element.27.plan, bf16[192,1024]{1,0:T(8,128)(2,1)} %get-tuple-element.29.low, bf16[64,1024]{1,0:T(8,128)(2,1)} %get-tuple-element.30.last, ...), custom_call_target="tpu_custom_call" | custom-call | flops 939524096 | bytes 1835008 | tf_op jit(solution)/shard_map/early_call/pallas_call | solution.py:584
  46.2 2.1 %second_call.1 = (bf16[192,512]{1,0:T(8,128)(2,1)S(1)}, bf16[192,512]{1,0:T(8,128)(2,1)S(1)}, bf16[288,1024]{1,0:T(8,128)(2,1)S(1)}) custom-call(s32[1]{0:T(128)} %bitcast.me_ref, s32[88]{0:T(128)S(1)} %get-tuple-element.27.plan, bf16[288,1024]{1,0:T(8,128)(2,1)S(1)} %get-tuple-element.33.early_grouped, ...), custom_call_target="tpu_custom_call", output_to_operand_aliasing={{2}: (2, {})} | custom-call | flops 402653184 | bytes 786432 | tf_op jit(solution)/shard_map/second_call/pallas_call | solution.py:594
  48.3 8.5 %final.1 = (bf16[256,1024]{1,0:T(8,128)(2,1)}, bf16[288,1024]{1,0:T(8,128)(2,1)S(1)}, f32[8,384,128]{2,1,0:T(8,128)S(1)}) custom-call(s32[1]{0:T(128)} %bitcast.me_ref, s32[88]{0:T(128)S(1)} %get-tuple-element.27.plan, f32[288,1024]{1,0:T(8,128)S(1)} %get-tuple-element.28.bias, ...), custom_call_target="tpu_custom_call", output_to_operand_aliasing={{1}: (3, {}), {2}: (4, {})} | custom-call | flops 2147483648 | bytes 8388608 | tf_op jit(solution)/shard_map/final/pallas_call | solution.py:614
  (3 shorter events, 0.0 us)
Async XLA Ops:
  1.9 8.5 %collective-permute-start.1 = (bf16[192,1024]{1,0:T(8,128)(2,1)S(1)}, bf16[192,1024]{1,0:T(8,128)(2,1)}, u32[]{:S(2)}, u32[]{:S(2)}) collective-permute-start(bf16[192,1024]{1,0:T(8,128)(2,1)S(1)} %get-tuple-element.34), channel_id=1, source_target_pairs={{1,2},{2,1},{5,6},{6,5},{9,10},{10,9},{13,14},{14,13},{17,18},{18,... | collective-permute-start | bytes 1179656 | tf_op jit(solution)/shard_map/ppermute | solution.py:547
  3.4 16.7 %collective-permute-start.3 = (bf16[192,1024]{1,0:T(8,128)(2,1)}, bf16[192,1024]{1,0:T(8,128)(2,1)S(1)}, u32[]{:S(2)}, u32[]{:S(2)}) collective-permute-start(bf16[192,1024]{1,0:T(8,128)(2,1)} %get-tuple-element.29.low), channel_id=1, source_target_pairs={{0,2},{3,1},{4,6},{7,5},{8,10},{11,9},{12,14},{15,13},{16,18},{19,... | collective-permute-start | bytes 1179656 | tf_op jit(solution)/shard_map/ppermute | solution.py:547
  10.3 33.0 %collective-permute-start = (bf16[192,1024]{1,0:T(8,128)(2,1)}, bf16[192,1024]{1,0:T(8,128)(2,1)}, u32[]{:S(2)}, u32[]{:S(2)}) collective-permute-start(bf16[192,1024]{1,0:T(8,128)(2,1)} %get-tuple-element.29.low), channel_id=1, source_target_pairs={{0,1},{1,0},{2,3},{3,2},{4,5},{5,4},{6,7},{7,6},{8,9},{9,8},{10,11... | collective-permute-start | bytes 1179656 | tf_op jit(solution)/shard_map/ppermute | solution.py:547
  10.4 35.8 %collective-permute-start.2 = (bf16[192,1024]{1,0:T(8,128)(2,1)}, bf16[192,1024]{1,0:T(8,128)(2,1)}, u32[]{:S(2)}, u32[]{:S(2)}) collective-permute-start(bf16[192,1024]{1,0:T(8,128)(2,1)} %collective-permute-done.1.inner), channel_id=1, source_target_pairs={{1,0},{2,3},{5,4},{6,7},{9,8},{10,11},{13,12},{14,15},{17,16},{18,... | collective-permute-start | bytes 1179656 | tf_op jit(solution)/shard_map/ppermute | solution.py:547
  11.7 23.2 %collective-permute-start.6 = (bf16[64,1024]{1,0:T(8,128)(2,1)S(1)}, bf16[64,1024]{1,0:T(8,128)(2,1)S(1)}, u32[]{:S(2)}, u32[]{:S(2)}) collective-permute-start(bf16[64,1024]{1,0:T(8,128)(2,1)S(1)} %get-tuple-element.41), channel_id=1, source_target_pairs={{1,2},{2,1},{5,6},{6,5},{9,10},{10,9},{13,14},{14,13},{17,18},{18,... | collective-permute-start | bytes 393224 | tf_op jit(solution)/shard_map/ppermute | solution.py:547
  20.1 28.2 %collective-permute-start.4 = (bf16[192,1024]{1,0:T(8,128)(2,1)S(1)}, bf16[192,1024]{1,0:T(8,128)(2,1)S(1)}, u32[]{:S(2)}, u32[]{:S(2)}) collective-permute-start(bf16[192,1024]{1,0:T(8,128)(2,1)S(1)} %collective-permute-done.3.far), channel_id=1, source_target_pairs={{1,0},{2,3},{5,4},{6,7},{9,8},{10,11},{13,12},{14,15},{17,16},{18,... | collective-permute-start | bytes 1179656 | tf_op jit(solution)/shard_map/ppermute | solution.py:547
  21.4 21.1 %collective-permute-start.7 = (bf16[64,1024]{1,0:T(8,128)(2,1)}, bf16[64,1024]{1,0:T(8,128)(2,1)S(1)}, u32[]{:S(2)}, u32[]{:S(2)}) collective-permute-start(bf16[64,1024]{1,0:T(8,128)(2,1)} %get-tuple-element.30.last), channel_id=1, source_target_pairs={{0,2},{3,1},{4,6},{7,5},{8,10},{11,9},{12,14},{15,13},{16,18},{19,... | collective-permute-start | bytes 393224 | tf_op jit(solution)/shard_map/ppermute | solution.py:547
  34.9 7.6 %collective-permute-start.5 = (bf16[64,1024]{1,0:T(8,128)(2,1)}, bf16[64,1024]{1,0:T(8,128)(2,1)S(1)}, u32[]{:S(2)}, u32[]{:S(2)}) collective-permute-start(bf16[64,1024]{1,0:T(8,128)(2,1)} %get-tuple-element.30.last), channel_id=1, source_target_pairs={{0,1},{3,2},{4,5},{7,6},{8,9},{11,10},{12,13},{15,14},{16,17},{19,... | collective-permute-start | bytes 393224 | tf_op jit(solution)/shard_map/ppermute | solution.py:547
  37.1 0.7 %copy-start = (s32[64]{0:T(128)S(1)}, s32[64]{0:T(128)}, u32[]{:S(2)}) copy-start(s32[64]{0:T(128)} %source_hbm.1) | copy-start | bytes 772
  37.7 0.7 %copy-start.1 = (s32[64]{0:T(128)S(1)}, s32[64]{0:T(128)}, u32[]{:S(2)}) copy-start(s32[64]{0:T(128)} %utt_ref.1) | copy-start | bytes 772

commit v5 on v3

--- a/solution.py
+++ b/solution.py
@@ -351,7 +351,8 @@
 
 
 def tables_kernel(
-    me_ref, source_ref, utt_ref, plan_ref, key_utt_ref, query_utt_ref, filled, ranks, key_utts
+    me_ref, source_ref, utt_ref, plan_ref, key_utt_ref, query_utt_ref, padded_ref,
+    filled, ranks, key_utts,
 ):
     me = me_ref[0]
     total = source_ref.shape[0]
@@ -412,6 +413,7 @@
         for k in range(1, per_vector):
             vector = jnp.where(lane_tile == k, tile_values[start + k], vector)
         key_utt_ref[:, start * TILE : start * TILE + 128] = vector
+    padded_ref[...] = jnp.zeros_like(padded_ref)
 
 
 def place_tiles(grouped, rows, plan, at):
@@ -470,7 +472,7 @@
 
 
 def final_kernel(
-    me_ref, plan, query_utt, key_utt, early_grouped, far, far_end, near_last,
+    me_ref, plan, query_utt, key_utt, early_grouped, zeros, far, far_end, near_last,
     early_key, early_value, second_key, second_value, middle_key, middle_value,
     key_weight, value_weight, query_weight, output_weight, half_taps, half_shift,
     out_hbm, grouped, padded, residual_rows, out, write_sems, late,
@@ -489,7 +491,6 @@
         late[: far.shape[0]] = far[...]
 
     place_tiles(grouped, late, plan, held)
-    padded[...] = jnp.zeros_like(padded)
     normed = layer_norm(late[: far.shape[0]]).astype(jnp.bfloat16)
     late_key = project(normed, key_weight)
     late_value = project(normed, value_weight)
@@ -545,17 +546,21 @@
     near = swap(low, SWAP_OUTER)
     inner = swap(high, SWAP_INNER)
     held_rows = rows_dev + 2 * TILE
-    plan, key_utt, query_utt = pl.pallas_call(
+    padded_shape = jax.ShapeDtypeStruct(
+        (width // 128, padded_rows(rows_dev // TILE), 128), jnp.float32
+    )
+    plan, key_utt, query_utt, padded = pl.pallas_call(
         tables_kernel,
         out_shape=(
             jax.ShapeDtypeStruct((plan_sizes(rows_dev // TILE)[2],), jnp.int32),
             shape(1, total * TILE, jnp.int32),
             shape(held_rows, 128, jnp.int32),
+            padded_shape,
         ),
         in_specs=[SMEM] * 3,
-        out_specs=(SMEM, VMEM, VMEM),
+        out_specs=(SMEM, VMEM, VMEM, VMEM),
         scratch_shapes=[pltpu.SMEM((n,), jnp.int32) for n in (COUNT * COUNT, total, total)],
-        compiler_params=params(4),
+        compiler_params=params(8),
         name="tables_call",
     )(me, tile_source, tile_utt)
     key_weight, value_weight, query_weight, output_weight, half_taps, half_shift = hold(
@@ -602,18 +607,18 @@
     )(near_last, inner_start, far_last, key_weight, value_weight)
     return pl.pallas_call(
         final_kernel,
-        out_shape=(shape(rows_dev), shape(held_rows)),
-        in_specs=[SMEM] * 2 + [VMEM] * 18,
-        out_specs=(HBM, VMEM),
-        input_output_aliases={4: 1},
-        scratch_shapes=block_scratch(rows_dev, width) + [pltpu.VMEM((rows_dev, width), jnp.bfloat16)],
+        out_shape=(shape(rows_dev), shape(held_rows), padded_shape),
+        in_specs=[SMEM] * 2 + [VMEM] * 19,
+        out_specs=(HBM, VMEM, VMEM),
+        input_output_aliases={4: 1, 5: 2},
+        scratch_shapes=block_scratch(rows_dev, width)[1:] + [pltpu.VMEM((rows_dev, width), jnp.bfloat16)],
         compiler_params=params(28),
         cost_estimate=pl.CostEstimate(
             flops=2 << 30, bytes_accessed=8 << 20, transcendentals=1 << 20
         ),
         name="final",
     )(
-        me, plan, query_utt, key_utt, grouped, far, far_end, near_last,
+        me, plan, query_utt, key_utt, grouped, padded, far, far_end, near_last,
         early_key, early_value, second_key, second_value, middle_key, middle_value,
         key_weight, value_weight, query_weight, output_weight, half_taps, half_shift,
     )[0]

time: 53.6 us -> 55.4 us (1.034)
  starting transfers between devices: 35 us -> 26.5 us
  waiting for transfers between devices: 0.02 us -> 7.73 us
  local copies, waits for them, and re-layouts: 0.01 us -> 1.31 us
  Pallas kernels: 18.2 us -> 19.4 us
    ppermute x8, starting transfers between devices: 35 us -> 26.5 us  [swap(): return lax.ppermute(value, 'ctx', perm)]
    ppermute x8, waiting for transfers between devices: 0.02 us -> 7.73 us  [swap(): return lax.ppermute(value, 'ctx', perm)]
    unnamed x4, local copies, waits for them, and re-layouts: 0.01 us -> 1.31 us
    pallas_call x1, Pallas kernels: 1.13 us -> 1.87 us  [line_block(): pl.pallas_call(arrange_kernel, out_shape=tuple((pltpu.VMEM((n, width), fr...]
    pallas_call x1, Pallas kernels: 2.24 us -> 2.82 us  [line_block(): pl.pallas_call(early_kernel, out_shape=(shape(early_rows, wide), shape(ea...]
  transfers between devices with their start and end apart: 8 -> 8, of which waited for: 0 -> 1; matrix products, arithmetic and copies ran while one was open for 0% -> 0% of each run, Pallas kernels for 16% -> 17%
where the time goes in v5:
time: 55.4 us; the launch traced here: 55.1 us
  starting transfers between devices  26.5 us (48%)
  Pallas kernels  19.4 us (35%)
  waiting for transfers between devices  7.73 us (14%)
  local copies, waits for them, and re-layouts  1.31 us (2%)
    ppermute x8, starting transfers between devices, swap(): return lax.ppermute(value, 'ctx', perm)  26.5 us
    pallas_call x1, Pallas kernels, line_block(): pl.pallas_call(final_kernel, out_shape=(shape(rows_dev), shape(held_rows)...  8.36 us
    ppermute x8, waiting for transfers between devices, swap(): return lax.ppermute(value, 'ctx', perm)  7.73 us
    pallas_call x1, Pallas kernels, line_block(): pl.pallas_call(early_kernel, out_shape=(shape(early_rows, wide), shape(ea...  2.82 us
    pallas_call x1, Pallas kernels, hold(): pl.pallas_call(hold_kernel, out_shape=tuple((pltpu.VMEM(a.shape, a.dtype)...  2.26 us
    pallas_call x1, Pallas kernels, line_block(): pl.pallas_call(arrange_kernel, out_shape=tuple((pltpu.VMEM((n, width), fr...  1.87 us
    pallas_call x1, Pallas kernels, line_block(): pl.pallas_call(tables_kernel, out_shape=(jax.ShapeDtypeStruct((plan_sizes...  1.84 us
    pallas_call x1, Pallas kernels, line_block(): pl.pallas_call(second_kernel, out_shape=(shape(piece, wide), shape(piece,...  1.48 us
  transfers between devices with their start and end apart: 8, of which 1 were waited for; matrix products, arithmetic and copies ran while one was open for 0% of the time, Pallas kernels for 17%

profile of v5, /device:TPU:0, one launch (start us, length us, event | category | flops | bytes accessed | tf_op | source)
XLA Modules:
  0.0 55.1 jit_solution(12901678551251118733)
XLA Ops:
  0.0 1.9 %arrange.1 = (bf16[192,1024]{1,0:T(8,128)(2,1)}, bf16[64,1024]{1,0:T(8,128)(2,1)S(1)}, bf16[192,1024]{1,0:T(8,128)(2,1)S(1)}, bf16[64,1024]{1,0:T(8,128)(2,1)S(1)}) custom-call(s32[1]{0:T(128)} %bitcast.me_ref, s32[64]{0:T(128)} %source_hbm.1, bf16[256,1024]{1,0:T(8,128)(2,1)} %rows_hbm.1), custom_call_target="tpu_custom_call" | custom-call | tf_op jit(solution)/shard_map/arrange/pallas_call | solution.py:528
  1.9 0.7 %collective-permute-start.1 = (bf16[192,1024]{1,0:T(8,128)(2,1)S(1)}, bf16[192,1024]{1,0:T(8,128)(2,1)S(1)}, u32[]{:S(2)}, u32[]{:S(2)}) collective-permute-start(bf16[192,1024]{1,0:T(8,128)(2,1)S(1)} %get-tuple-element.36), channel_id=1, source_target_pairs={{1,2},{2,1},{5,6},{6,5},{9,10},{10,9},{13,14},{14,13},{17,18},{18,... | collective-permute-start | bytes 1179656 | tf_op jit(solution)/shard_map/ppermute | solution.py:544
  2.6 7.7 %collective-permute-start.3 = (bf16[192,1024]{1,0:T(8,128)(2,1)}, bf16[192,1024]{1,0:T(8,128)(2,1)S(1)}, u32[]{:S(2)}, u32[]{:S(2)}) collective-permute-start(bf16[192,1024]{1,0:T(8,128)(2,1)} %get-tuple-element.31.low), channel_id=1, source_target_pairs={{0,2},{3,1},{4,6},{7,5},{8,10},{11,9},{12,14},{15,13},{16,18},{19,... | collective-permute-start | bytes 1179656 | tf_op jit(solution)/shard_map/ppermute | solution.py:544
  10.2 0.1 collective-permute-start
  10.3 0.0 collective-permute-done.1.inner
  10.3 1.3 %collective-permute-start.2 = (bf16[192,1024]{1,0:T(8,128)(2,1)S(1)}, bf16[192,1024]{1,0:T(8,128)(2,1)S(1)}, u32[]{:S(2)}, u32[]{:S(2)}) collective-permute-start(bf16[192,1024]{1,0:T(8,128)(2,1)S(1)} %collective-permute-done.1.inner), channel_id=1, source_target_pairs={{1,0},{2,3},{5,4},{6,7},{9,8},{10,11},{13,12},{14,15},{17,16},{18,... | collective-permute-start | bytes 1179656 | tf_op jit(solution)/shard_map/ppermute | solution.py:544
  11.6 0.7 %collective-permute-start.6 = (bf16[64,1024]{1,0:T(8,128)(2,1)S(1)}, bf16[64,1024]{1,0:T(8,128)(2,1)S(1)}, u32[]{:S(2)}, u32[]{:S(2)}) collective-permute-start(bf16[64,1024]{1,0:T(8,128)(2,1)S(1)} %get-tuple-element.43), channel_id=1, source_target_pairs={{1,2},{2,1},{5,6},{6,5},{9,10},{10,9},{13,14},{14,13},{17,18},{18,... | collective-permute-start | bytes 393224 | tf_op jit(solution)/shard_map/ppermute | solution.py:544
  12.3 7.7 %collective-permute-done.3.far = bf16[192,1024]{1,0:T(8,128)(2,1)S(1)} collective-permute-done((bf16[192,1024]{1,0:T(8,128)(2,1)}, bf16[192,1024]{1,0:T(8,128)(2,1)S(1)}, u32[]{:S(2)}, u32[]{:S(2)}) %collective-permute-start.3) | collective-permute-done | bytes 393248 | tf_op jit(solution)/shard_map/ppermute | solution.py:544
  20.0 1.3 %collective-permute-start.4 = (bf16[192,1024]{1,0:T(8,128)(2,1)S(1)}, bf16[192,1024]{1,0:T(8,128)(2,1)S(1)}, u32[]{:S(2)}, u32[]{:S(2)}) collective-permute-start(bf16[192,1024]{1,0:T(8,128)(2,1)S(1)} %collective-permute-done.3.far), channel_id=1, source_target_pairs={{1,0},{2,3},{5,4},{6,7},{9,8},{10,11},{13,12},{14,15},{17,16},{18,... | collective-permute-start | bytes 1179656 | tf_op jit(solution)/shard_map/ppermute | solution.py:544
  21.3 12.7 %collective-permute-start.7 = (bf16[64,1024]{1,0:T(8,128)(2,1)S(1)}, bf16[64,1024]{1,0:T(8,128)(2,1)S(1)}, u32[]{:S(2)}, u32[]{:S(2)}) collective-permute-start(bf16[64,1024]{1,0:T(8,128)(2,1)S(1)} %get-tuple-element.32.last), channel_id=1, source_target_pairs={{0,2},{3,1},{4,6},{7,5},{8,10},{11,9},{12,14},{15,13},{16,18},{19,... | collective-permute-start | bytes 393224 | tf_op jit(solution)/shard_map/ppermute | solution.py:544
  34.1 2.1 %collective-permute-start.5 = (bf16[64,1024]{1,0:T(8,128)(2,1)S(1)}, bf16[64,1024]{1,0:T(8,128)(2,1)S(1)}, u32[]{:S(2)}, u32[]{:S(2)}) collective-permute-start(bf16[64,1024]{1,0:T(8,128)(2,1)S(1)} %get-tuple-element.32.last), channel_id=1, source_target_pairs={{0,1},{3,2},{4,5},{7,6},{8,9},{11,10},{12,13},{15,14},{16,17},{19,... | collective-permute-start | bytes 393224 | tf_op jit(solution)/shard_map/ppermute | solution.py:544
  36.2 0.0 copy-start
  36.2 0.6 %copy-done = s32[64]{0:T(128)S(1)} copy-done((s32[64]{0:T(128)S(1)}, s32[64]{0:T(128)}, u32[]{:S(2)}) %copy-start) | copy-done | bytes 280
  36.8 0.7 %copy-done.1 = s32[64]{0:T(128)S(1)} copy-done((s32[64]{0:T(128)S(1)}, s32[64]{0:T(128)}, u32[]{:S(2)}) %copy-start.1) | copy-done | bytes 280
  37.5 1.8 %tables_call.1 = (s32[88]{0:T(128)S(1)}, s32[1,1024]{1,0:T(1,128)S(1)}, s32[288,128]{1,0:T(8,128)S(1)}, f32[8,384,128]{2,1,0:T(8,128)S(1)}) custom-call(s32[1]{0:T(128)} %bitcast.me_ref, s32[64]{0:T(128)S(1)} %copy-done, s32[64]{0:T(128)S(1)} %copy-done.1), custom_call_target="tpu_custom_call" | custom-call | tf_op jit(solution)/shard_map/tables_call/pallas_call | solution.py:552
  39.3 2.3 %hold_call.1 = (bf16[1024,512]{1,0:T(8,128)(2,1)S(1)}, bf16[1024,512]{1,0:T(8,128)(2,1)S(1)}, bf16[1024,512]{1,0:T(8,128)(2,1)S(1)}, bf16[512,1024]{1,0:T(8,128)...) custom-call(bf16[1024,512]{1,0:T(8,128)(2,1)} %refs_0_.1, bf16[1024,512]{1,0:T(8,128)(2,1)} %refs_1_.1, ...), custom_call_target="tpu_custom_call" | custom-call | bytes 8388608 | tf_op jit(solution)/shard_map/hold_call/pallas_call | solution.py:335
  41.6 0.0 collective-permute-done.7.refs_2_
  41.6 0.0 collective-permute-done.5.refs_0_.near_last
  41.6 0.8 %middle_call.1 = (bf16[192,512]{1,0:T(8,128)(2,1)S(1)}, bf16[192,512]{1,0:T(8,128)(2,1)S(1)}) custom-call(bf16[64,1024]{1,0:T(8,128)(2,1)S(1)} %collective-permute-done.5.refs_0_.near_last, bf16[64,1024]{1,0:T(8,128)(2,1)S(1)} %collective-permute-done.6.refs_1_, bf16[64,1024]{1,0:T(8,128)(2,1)S(1)} %collective-permute-done.7.refs_2_, ...), custom_call_target="tpu_custom_call" | custom-call | flops 402653184 | bytes 786432 | tf_op jit(solution)/shard_map/middle_call/pallas_call | solution.py:599
  42.4 2.8 %early_call.1 = (bf16[448,512]{1,0:T(8,128)(2,1)S(1)}, bf16[448,512]{1,0:T(8,128)(2,1)S(1)}, bf16[288,1024]{1,0:T(8,128)(2,1)S(1)}) custom-call(s32[88]{0:T(128)S(1)} %get-tuple-element.28.plan, bf16[192,1024]{1,0:T(8,128)(2,1)} %get-tuple-element.31.low, bf16[64,1024]{1,0:T(8,128)(2,1)S(1)} %get-tuple-element.32.last, ...), custom_call_target="tpu_custom_call" | custom-call | flops 939524096 | bytes 1835008 | tf_op jit(solution)/shard_map/early_call/pallas_call | solution.py:578
  45.3 0.0 collective-permute-done.2.inner_end
  45.3 1.5 %second_call.1 = (bf16[192,512]{1,0:T(8,128)(2,1)S(1)}, bf16[192,512]{1,0:T(8,128)(2,1)S(1)}, bf16[288,1024]{1,0:T(8,128)(2,1)S(1)}) custom-call(s32[1]{0:T(128)} %bitcast.me_ref, s32[88]{0:T(128)S(1)} %get-tuple-element.28.plan, bf16[288,1024]{1,0:T(8,128)(2,1)S(1)} %get-tuple-element.35.early_grouped, ...), custom_call_target="tpu_custom_call", output_to_operand_aliasing={{2}: (2, {})} | custom-call | flops 402653184 | bytes 786432 | tf_op jit(solution)/shard_map/second_call/pallas_call | solution.py:588
  46.8 0.0 collective-permute-done.4.far_end
  46.8 8.4 %final.1 = (bf16[256,1024]{1,0:T(8,128)(2,1)}, bf16[288,1024]{1,0:T(8,128)(2,1)S(1)}, f32[8,384,128]{2,1,0:T(8,128)S(1)}) custom-call(s32[1]{0:T(128)} %bitcast.me_ref, s32[88]{0:T(128)S(1)} %get-tuple-element.28.plan, s32[288,128]{1,0:T(8,128)S(1)} %get-tuple-element.29.query_utt, ...), custom_call_target="tpu_custom_call", output_to_operand_aliasing={{1}: (4, {}), {2}: (5, {})} | custom-call | flops 2147483648 | bytes 8388608 | tf_op jit(solution)/shard_map/final/pallas_call | solution.py:608
  (3 shorter events, 0.0 us)
Async XLA Ops:
  1.9 8.4 %collective-permute-start.1 = (bf16[192,1024]{1,0:T(8,128)(2,1)S(1)}, bf16[192,1024]{1,0:T(8,128)(2,1)S(1)}, u32[]{:S(2)}, u32[]{:S(2)}) collective-permute-start(bf16[192,1024]{1,0:T(8,128)(2,1)S(1)} %get-tuple-element.36), channel_id=1, source_target_pairs={{1,2},{2,1},{5,6},{6,5},{9,10},{10,9},{13,14},{14,13},{17,18},{18,... | collective-permute-start | bytes 1179656 | tf_op jit(solution)/shard_map/ppermute | solution.py:544
  2.6 17.5 %collective-permute-start.3 = (bf16[192,1024]{1,0:T(8,128)(2,1)}, bf16[192,1024]{1,0:T(8,128)(2,1)S(1)}, u32[]{:S(2)}, u32[]{:S(2)}) collective-permute-start(bf16[192,1024]{1,0:T(8,128)(2,1)} %get-tuple-element.31.low), channel_id=1, source_target_pairs={{0,2},{3,1},{4,6},{7,5},{8,10},{11,9},{12,14},{15,13},{16,18},{19,... | collective-permute-start | bytes 1179656 | tf_op jit(solution)/shard_map/ppermute | solution.py:544
  10.2 32.2 %collective-permute-start = (bf16[192,1024]{1,0:T(8,128)(2,1)}, bf16[192,1024]{1,0:T(8,128)(2,1)}, u32[]{:S(2)}, u32[]{:S(2)}) collective-permute-start(bf16[192,1024]{1,0:T(8,128)(2,1)} %get-tuple-element.31.low), channel_id=1, source_target_pairs={{0,1},{1,0},{2,3},{3,2},{4,5},{5,4},{6,7},{7,6},{8,9},{9,8},{10,11... | collective-permute-start | bytes 1179656 | tf_op jit(solution)/shard_map/ppermute | solution.py:544
  10.3 34.9 %collective-permute-start.2 = (bf16[192,1024]{1,0:T(8,128)(2,1)S(1)}, bf16[192,1024]{1,0:T(8,128)(2,1)S(1)}, u32[]{:S(2)}, u32[]{:S(2)}) collective-permute-start(bf16[192,1024]{1,0:T(8,128)(2,1)S(1)} %collective-permute-done.1.inner), channel_id=1, source_target_pairs={{1,0},{2,3},{5,4},{6,7},{9,8},{10,11},{13,12},{14,15},{17,16},{18,... | collective-permute-start | bytes 1179656 | tf_op jit(solution)/shard_map/ppermute | solution.py:544
  11.6 22.4 %collective-permute-start.6 = (bf16[64,1024]{1,0:T(8,128)(2,1)S(1)}, bf16[64,1024]{1,0:T(8,128)(2,1)S(1)}, u32[]{:S(2)}, u32[]{:S(2)}) collective-permute-start(bf16[64,1024]{1,0:T(8,128)(2,1)S(1)} %get-tuple-element.43), channel_id=1, source_target_pairs={{1,2},{2,1},{5,6},{6,5},{9,10},{10,9},{13,14},{14,13},{17,18},{18,... | collective-permute-start | bytes 393224 | tf_op jit(solution)/shard_map/ppermute | solution.py:544
  20.0 26.7 %collective-permute-start.4 = (bf16[192,1024]{1,0:T(8,128)(2,1)S(1)}, bf16[192,1024]{1,0:T(8,128)(2,1)S(1)}, u32[]{:S(2)}, u32[]{:S(2)}) collective-permute-start(bf16[192,1024]{1,0:T(8,128)(2,1)S(1)} %collective-permute-done.3.far), channel_id=1, source_target_pairs={{1,0},{2,3},{5,4},{6,7},{9,8},{10,11},{13,12},{14,15},{17,16},{18,... | collective-permute-start | bytes 1179656 | tf_op jit(solution)/shard_map/ppermute | solution.py:544
  21.3 20.3 %collective-permute-start.7 = (bf16[64,1024]{1,0:T(8,128)(2,1)S(1)}, bf16[64,1024]{1,0:T(8,128)(2,1)S(1)}, u32[]{:S(2)}, u32[]{:S(2)}) collective-permute-start(bf16[64,1024]{1,0:T(8,128)(2,1)S(1)} %get-tuple-element.32.last), channel_id=1, source_target_pairs={{0,2},{3,1},{4,6},{7,5},{8,10},{11,9},{12,14},{15,13},{16,18},{19,... | collective-permute-start | bytes 393224 | tf_op jit(solution)/shard_map/ppermute | solution.py:544
  34.1 7.6 %collective-permute-start.5 = (bf16[64,1024]{1,0:T(8,128)(2,1)S(1)}, bf16[64,1024]{1,0:T(8,128)(2,1)S(1)}, u32[]{:S(2)}, u32[]{:S(2)}) collective-permute-start(bf16[64,1024]{1,0:T(8,128)(2,1)S(1)} %get-tuple-element.32.last), channel_id=1, source_target_pairs={{0,1},{3,2},{4,5},{7,6},{8,9},{11,10},{12,13},{15,14},{16,17},{19,... | collective-permute-start | bytes 393224 | tf_op jit(solution)/shard_map/ppermute | solution.py:544
  36.2 0.7 %copy-start = (s32[64]{0:T(128)S(1)}, s32[64]{0:T(128)}, u32[]{:S(2)}) copy-start(s32[64]{0:T(128)} %source_hbm.1) | copy-start | bytes 772
  36.8 0.7 %copy-start.1 = (s32[64]{0:T(128)S(1)}, s32[64]{0:T(128)}, u32[]{:S(2)}) copy-start(s32[64]{0:T(128)} %utt_ref.1) | copy-start | bytes 772

commit v6 on v5

--- a/solution.py
+++ b/solution.py
@@ -396,8 +396,8 @@
     order = [(me, quarter, False) for quarter in (0, 1, 2, 3)]
     order += [(near, quarter, False) for quarter in (0, 1, 2)]
     order += [(second, quarter, False) for quarter in (1, 2, 3)]
+    order += [(far, quarter, False) for quarter in (0, 1, 2)]
     order += [(near, 3, True), (second, 0, True), (far, 3, True)]
-    order += [(far, quarter, False) for quarter in (0, 1, 2)]
     lane_tile = lax.broadcasted_iota(jnp.int32, (1, 128), 1) // TILE
     tile_values = []
     for shard, quarter, inner_only in order:
@@ -463,19 +463,29 @@
     value_ref[...] = project(normed, value_weight)
 
 
-def middle_kernel(*refs):
+def middle_kernel(me_ref, *refs):
+    me = me_ref[0]
+    is_end = (me == 0) | (me == COUNT - 1)
     parts, (key_weight, value_weight, key_ref, value_ref) = refs[:-4], refs[-4:]
-    rows = jnp.concatenate([part[...] for part in parts], axis=0)
-    normed = layer_norm(rows).astype(jnp.bfloat16)
-    key_ref[...] = project(normed, key_weight)
-    value_ref[...] = project(normed, value_weight)
+
+    @pl.when(is_end)
+    def _():
+        key_ref[...] = jnp.zeros_like(key_ref)
+        value_ref[...] = jnp.zeros_like(value_ref)
+
+    @pl.when(jnp.logical_not(is_end))
+    def _():
+        rows = jnp.concatenate([part[...] for part in parts], axis=0)
+        normed = layer_norm(rows).astype(jnp.bfloat16)
+        key_ref[...] = project(normed, key_weight)
+        value_ref[...] = project(normed, value_weight)
 
 
 def final_kernel(
     me_ref, plan, query_utt, key_utt, early_grouped, zeros, far, far_end, near_last,
     early_key, early_value, second_key, second_value, middle_key, middle_value,
     key_weight, value_weight, query_weight, output_weight, half_taps, half_shift,
-    out_hbm, grouped, padded, residual_rows, out, write_sems, late,
+    out_hbm, grouped, padded, residual_rows, out, write_sems, late, residual,
 ):
     me = me_ref[0]
     is_end = (me == 0) | (me == COUNT - 1)
@@ -494,14 +504,25 @@
     normed = layer_norm(late[: far.shape[0]]).astype(jnp.bfloat16)
     late_key = project(normed, key_weight)
     late_value = project(normed, value_weight)
-    residual = attend(
-        grouped, query_utt, key_utt[...],
-        [early_key, second_key, middle_key, late_key],
-        [early_value, second_value, middle_value, late_value],
-        query_weight, output_weight,
-    )
+    keys = [early_key, second_key, late_key, middle_key]
+    values = [early_value, second_value, late_value, middle_value]
+    used = key_utt.shape[1] - middle_key.shape[0]
+
+    @pl.when(is_end)
+    def _():
+        residual[...] = attend(
+            grouped, query_utt, key_utt[:, :used], keys[:-1], values[:-1],
+            query_weight, output_weight,
+        )
+
+    @pl.when(jnp.logical_not(is_end))
+    def _():
+        residual[...] = attend(
+            grouped, query_utt, key_utt[...], keys, values, query_weight, output_weight
+        )
+
     convolve(
-        residual, plan, places_at, half_taps, half_shift[...], out_hbm, padded, residual_rows,
+        residual[...], plan, places_at, half_taps, half_shift[...], out_hbm, padded, residual_rows,
         out, write_sems,
     )
 
@@ -599,19 +620,20 @@
     middle_key, middle_value = pl.pallas_call(
         middle_kernel,
         out_shape=(shape(3 * quarter, wide),) * 2,
-        in_specs=[VMEM] * 5,
+        in_specs=[SMEM] + [VMEM] * 5,
         out_specs=(VMEM,) * 2,
         compiler_params=params(8),
         cost_estimate=cost(3 * quarter),
         name="middle_call",
-    )(near_last, inner_start, far_last, key_weight, value_weight)
+    )(me, near_last, inner_start, far_last, key_weight, value_weight)
     return pl.pallas_call(
         final_kernel,
         out_shape=(shape(rows_dev), shape(held_rows), padded_shape),
         in_specs=[SMEM] * 2 + [VMEM] * 19,
         out_specs=(HBM, VMEM, VMEM),
         input_output_aliases={4: 1, 5: 2},
-        scratch_shapes=block_scratch(rows_dev, width)[1:] + [pltpu.VMEM((rows_dev, width), jnp.bfloat16)],
+        scratch_shapes=block_scratch(rows_dev, width)[1:]
+        + [pltpu.VMEM((rows, width), jnp.bfloat16) for rows in (rows_dev, held_rows)],
         compiler_params=params(28),
         cost_estimate=pl.CostEstimate(
             flops=2 << 30, bytes_accessed=8 << 20, transcendentals=1 << 20

time: 55.4 us -> 55.4 us (level)
    pallas_call x1, Pallas kernels: 0.78 us -> 0.04 us  [line_block(): pl.pallas_call(middle_kernel, out_shape=(shape(3 * quarter, wide),) * 2,...]
    pallas_call x1, Pallas kernels: 8.36 us -> 9.05 us  [line_block(): pl.pallas_call(final_kernel, out_shape=(shape(rows_dev), shape(held_rows)...]
  transfers between devices with their start and end apart: 8 -> 8, of which waited for: 1 -> 1; matrix products, arithmetic and copies ran while one was open for 0% -> 0% of each run, Pallas kernels for 17% -> 15%
where the time goes in v6:
time: 55.4 us; the launch traced here: 55.1 us
  starting transfers between devices  26.5 us (48%)
  Pallas kernels  19.4 us (35%)
  waiting for transfers between devices  7.73 us (14%)
  local copies, waits for them, and re-layouts  1.31 us (2%)
    ppermute x8, starting transfers between devices, swap(): return lax.ppermute(value, 'ctx', perm)  26.5 us
    pallas_call x1, Pallas kernels, line_block(): pl.pallas_call(final_kernel, out_shape=(shape(rows_dev), shape(held_rows)...  9.05 us
    ppermute x8, waiting for transfers between devices, swap(): return lax.ppermute(value, 'ctx', perm)  7.73 us
    pallas_call x1, Pallas kernels, line_block(): pl.pallas_call(early_kernel, out_shape=(shape(early_rows, wide), shape(ea...  2.82 us
    pallas_call x1, Pallas kernels, hold(): pl.pallas_call(hold_kernel, out_shape=tuple((pltpu.VMEM(a.shape, a.dtype)...  2.26 us
    pallas_call x1, Pallas kernels, line_block(): pl.pallas_call(arrange_kernel, out_shape=tuple((pltpu.VMEM((n, width), fr...  1.87 us
    pallas_call x1, Pallas kernels, line_block(): pl.pallas_call(tables_kernel, out_shape=(jax.ShapeDtypeStruct((plan_sizes...  1.85 us
    pallas_call x1, Pallas kernels, line_block(): pl.pallas_call(second_kernel, out_shape=(shape(piece, wide), shape(piece,...  1.48 us
  transfers between devices with their start and end apart: 8, of which 1 were waited for; matrix products, arithmetic and copies ran while one was open for 0% of the time, Pallas kernels for 15%

profile of v6, /device:TPU:0, one launch (start us, length us, event | category | flops | bytes accessed | tf_op | source)
XLA Modules:
  0.0 55.1 jit_solution(3300729062238203540)
XLA Ops:
  0.0 1.9 %arrange.1 = (bf16[192,1024]{1,0:T(8,128)(2,1)}, bf16[64,1024]{1,0:T(8,128)(2,1)S(1)}, bf16[192,1024]{1,0:T(8,128)(2,1)S(1)}, bf16[64,1024]{1,0:T(8,128)(2,1)S(1)}) custom-call(s32[1]{0:T(128)} %bitcast.me_ref, s32[64]{0:T(128)} %source_hbm.1, bf16[256,1024]{1,0:T(8,128)(2,1)} %rows_hbm.1), custom_call_target="tpu_custom_call" | custom-call | tf_op jit(solution)/shard_map/arrange/pallas_call | solution.py:549
  1.9 0.7 %collective-permute-start.1 = (bf16[192,1024]{1,0:T(8,128)(2,1)S(1)}, bf16[192,1024]{1,0:T(8,128)(2,1)S(1)}, u32[]{:S(2)}, u32[]{:S(2)}) collective-permute-start(bf16[192,1024]{1,0:T(8,128)(2,1)S(1)} %get-tuple-element.36), channel_id=1, source_target_pairs={{1,2},{2,1},{5,6},{6,5},{9,10},{10,9},{13,14},{14,13},{17,18},{18,... | collective-permute-start | bytes 1179656 | tf_op jit(solution)/shard_map/ppermute | solution.py:565
  2.6 7.7 %collective-permute-start.3 = (bf16[192,1024]{1,0:T(8,128)(2,1)}, bf16[192,1024]{1,0:T(8,128)(2,1)S(1)}, u32[]{:S(2)}, u32[]{:S(2)}) collective-permute-start(bf16[192,1024]{1,0:T(8,128)(2,1)} %get-tuple-element.31.low), channel_id=1, source_target_pairs={{0,2},{3,1},{4,6},{7,5},{8,10},{11,9},{12,14},{15,13},{16,18},{19,... | collective-permute-start | bytes 1179656 | tf_op jit(solution)/shard_map/ppermute | solution.py:565
  10.2 0.1 collective-permute-start
  10.3 0.0 collective-permute-done.1.inner
  10.3 1.3 %collective-permute-start.2 = (bf16[192,1024]{1,0:T(8,128)(2,1)S(1)}, bf16[192,1024]{1,0:T(8,128)(2,1)S(1)}, u32[]{:S(2)}, u32[]{:S(2)}) collective-permute-start(bf16[192,1024]{1,0:T(8,128)(2,1)S(1)} %collective-permute-done.1.inner), channel_id=1, source_target_pairs={{1,0},{2,3},{5,4},{6,7},{9,8},{10,11},{13,12},{14,15},{17,16},{18,... | collective-permute-start | bytes 1179656 | tf_op jit(solution)/shard_map/ppermute | solution.py:565
  11.6 0.7 %collective-permute-start.6 = (bf16[64,1024]{1,0:T(8,128)(2,1)S(1)}, bf16[64,1024]{1,0:T(8,128)(2,1)S(1)}, u32[]{:S(2)}, u32[]{:S(2)}) collective-permute-start(bf16[64,1024]{1,0:T(8,128)(2,1)S(1)} %get-tuple-element.43), channel_id=1, source_target_pairs={{1,2},{2,1},{5,6},{6,5},{9,10},{10,9},{13,14},{14,13},{17,18},{18,... | collective-permute-start | bytes 393224 | tf_op jit(solution)/shard_map/ppermute | solution.py:565
  12.3 7.7 %collective-permute-done.3.far = bf16[192,1024]{1,0:T(8,128)(2,1)S(1)} collective-permute-done((bf16[192,1024]{1,0:T(8,128)(2,1)}, bf16[192,1024]{1,0:T(8,128)(2,1)S(1)}, u32[]{:S(2)}, u32[]{:S(2)}) %collective-permute-start.3) | collective-permute-done | bytes 393248 | tf_op jit(solution)/shard_map/ppermute | solution.py:565
  20.0 1.3 %collective-permute-start.4 = (bf16[192,1024]{1,0:T(8,128)(2,1)S(1)}, bf16[192,1024]{1,0:T(8,128)(2,1)S(1)}, u32[]{:S(2)}, u32[]{:S(2)}) collective-permute-start(bf16[192,1024]{1,0:T(8,128)(2,1)S(1)} %collective-permute-done.3.far), channel_id=1, source_target_pairs={{1,0},{2,3},{5,4},{6,7},{9,8},{10,11},{13,12},{14,15},{17,16},{18,... | collective-permute-start | bytes 1179656 | tf_op jit(solution)/shard_map/ppermute | solution.py:565
  21.3 12.7 %collective-permute-start.7 = (bf16[64,1024]{1,0:T(8,128)(2,1)S(1)}, bf16[64,1024]{1,0:T(8,128)(2,1)S(1)}, u32[]{:S(2)}, u32[]{:S(2)}) collective-permute-start(bf16[64,1024]{1,0:T(8,128)(2,1)S(1)} %get-tuple-element.32.last), channel_id=1, source_target_pairs={{0,2},{3,1},{4,6},{7,5},{8,10},{11,9},{12,14},{15,13},{16,18},{19,... | collective-permute-start | bytes 393224 | tf_op jit(solution)/shard_map/ppermute | solution.py:565
  34.0 0.0 collective-permute-done.6.refs_1_
  34.1 2.1 %collective-permute-start.5 = (bf16[64,1024]{1,0:T(8,128)(2,1)S(1)}, bf16[64,1024]{1,0:T(8,128)(2,1)S(1)}, u32[]{:S(2)}, u32[]{:S(2)}) collective-permute-start(bf16[64,1024]{1,0:T(8,128)(2,1)S(1)} %get-tuple-element.32.last), channel_id=1, source_target_pairs={{0,1},{3,2},{4,5},{7,6},{8,9},{11,10},{12,13},{15,14},{16,17},{19,... | collective-permute-start | bytes 393224 | tf_op jit(solution)/shard_map/ppermute | solution.py:565
  36.2 0.0 copy-start
  36.2 0.6 %copy-done = s32[64]{0:T(128)S(1)} copy-done((s32[64]{0:T(128)S(1)}, s32[64]{0:T(128)}, u32[]{:S(2)}) %copy-start) | copy-done | bytes 280
  36.8 0.7 %copy-done.1 = s32[64]{0:T(128)S(1)} copy-done((s32[64]{0:T(128)S(1)}, s32[64]{0:T(128)}, u32[]{:S(2)}) %copy-start.1) | copy-done | bytes 280
  37.5 1.8 %tables_call.1 = (s32[88]{0:T(128)S(1)}, s32[1,1024]{1,0:T(1,128)S(1)}, s32[288,128]{1,0:T(8,128)S(1)}, f32[8,384,128]{2,1,0:T(8,128)S(1)}) custom-call(s32[1]{0:T(128)} %bitcast.me_ref, s32[64]{0:T(128)S(1)} %copy-done, s32[64]{0:T(128)S(1)} %copy-done.1), custom_call_target="tpu_custom_call" | custom-call | tf_op jit(solution)/shard_map/tables_call/pallas_call | solution.py:573
  39.4 2.3 %hold_call.1 = (bf16[1024,512]{1,0:T(8,128)(2,1)S(1)}, bf16[1024,512]{1,0:T(8,128)(2,1)S(1)}, bf16[1024,512]{1,0:T(8,128)(2,1)S(1)}, bf16[512,1024]{1,0:T(8,128)...) custom-call(bf16[1024,512]{1,0:T(8,128)(2,1)} %refs_0_.1, bf16[1024,512]{1,0:T(8,128)(2,1)} %refs_1_.1, ...), custom_call_target="tpu_custom_call" | custom-call | bytes 8388608 | tf_op jit(solution)/shard_map/hold_call/pallas_call | solution.py:335
  41.6 0.0 collective-permute-done.7.refs_2_
  41.6 0.0 collective-permute-done.5.refs_0_.near_last
  41.7 2.8 %early_call.1 = (bf16[448,512]{1,0:T(8,128)(2,1)S(1)}, bf16[448,512]{1,0:T(8,128)(2,1)S(1)}, bf16[288,1024]{1,0:T(8,128)(2,1)S(1)}) custom-call(s32[88]{0:T(128)S(1)} %get-tuple-element.28.plan, bf16[192,1024]{1,0:T(8,128)(2,1)} %get-tuple-element.31.low, bf16[64,1024]{1,0:T(8,128)(2,1)S(1)} %get-tuple-element.32.last, ...), custom_call_target="tpu_custom_call" | custom-call | flops 939524096 | bytes 1835008 | tf_op jit(solution)/shard_map/early_call/pallas_call | solution.py:599
  44.5 0.0 collective-permute-done.2.inner_end
  44.5 1.5 %second_call.1 = (bf16[192,512]{1,0:T(8,128)(2,1)S(1)}, bf16[192,512]{1,0:T(8,128)(2,1)S(1)}, bf16[288,1024]{1,0:T(8,128)(2,1)S(1)}) custom-call(s32[1]{0:T(128)} %bitcast.me_ref, s32[88]{0:T(128)S(1)} %get-tuple-element.28.plan, bf16[288,1024]{1,0:T(8,128)(2,1)S(1)} %get-tuple-element.35.early_grouped, ...), custom_call_target="tpu_custom_call", output_to_operand_aliasing={{2}: (2, {})} | custom-call | flops 402653184 | bytes 786432 | tf_op jit(solution)/shard_map/second_call/pallas_call | solution.py:609
  46.0 0.0 collective-permute-done.4.far_end
  46.0 9.0 %final.1 = (bf16[256,1024]{1,0:T(8,128)(2,1)}, bf16[288,1024]{1,0:T(8,128)(2,1)S(1)}, f32[8,384,128]{2,1,0:T(8,128)S(1)}) custom-call(s32[1]{0:T(128)} %bitcast.me_ref, s32[88]{0:T(128)S(1)} %get-tuple-element.28.plan, s32[288,128]{1,0:T(8,128)S(1)} %get-tuple-element.29.query_utt, ...), custom_call_target="tpu_custom_call", output_to_operand_aliasing={{1}: (4, {}), {2}: (5, {})} | custom-call | flops 2147483648 | bytes 8388608 | tf_op jit(solution)/shard_map/final/pallas_call | solution.py:629
  (3 shorter events, 0.0 us)
Async XLA Ops:
  1.9 8.4 %collective-permute-start.1 = (bf16[192,1024]{1,0:T(8,128)(2,1)S(1)}, bf16[192,1024]{1,0:T(8,128)(2,1)S(1)}, u32[]{:S(2)}, u32[]{:S(2)}) collective-permute-start(bf16[192,1024]{1,0:T(8,128)(2,1)S(1)} %get-tuple-element.36), channel_id=1, source_target_pairs={{1,2},{2,1},{5,6},{6,5},{9,10},{10,9},{13,14},{14,13},{17,18},{18,... | collective-permute-start | bytes 1179656 | tf_op jit(solution)/shard_map/ppermute | solution.py:565
  2.6 17.5 %collective-permute-start.3 = (bf16[192,1024]{1,0:T(8,128)(2,1)}, bf16[192,1024]{1,0:T(8,128)(2,1)S(1)}, u32[]{:S(2)}, u32[]{:S(2)}) collective-permute-start(bf16[192,1024]{1,0:T(8,128)(2,1)} %get-tuple-element.31.low), channel_id=1, source_target_pairs={{0,2},{3,1},{4,6},{7,5},{8,10},{11,9},{12,14},{15,13},{16,18},{19,... | collective-permute-start | bytes 1179656 | tf_op jit(solution)/shard_map/ppermute | solution.py:565
  10.2 31.4 %collective-permute-start = (bf16[192,1024]{1,0:T(8,128)(2,1)}, bf16[192,1024]{1,0:T(8,128)(2,1)}, u32[]{:S(2)}, u32[]{:S(2)}) collective-permute-start(bf16[192,1024]{1,0:T(8,128)(2,1)} %get-tuple-element.31.low), channel_id=1, source_target_pairs={{0,1},{1,0},{2,3},{3,2},{4,5},{5,4},{6,7},{7,6},{8,9},{9,8},{10,11... | collective-permute-start | bytes 1179656 | tf_op jit(solution)/shard_map/ppermute | solution.py:565
  10.3 34.2 %collective-permute-start.2 = (bf16[192,1024]{1,0:T(8,128)(2,1)S(1)}, bf16[192,1024]{1,0:T(8,128)(2,1)S(1)}, u32[]{:S(2)}, u32[]{:S(2)}) collective-permute-start(bf16[192,1024]{1,0:T(8,128)(2,1)S(1)} %collective-permute-done.1.inner), channel_id=1, source_target_pairs={{1,0},{2,3},{5,4},{6,7},{9,8},{10,11},{13,12},{14,15},{17,16},{18,... | collective-permute-start | bytes 1179656 | tf_op jit(solution)/shard_map/ppermute | solution.py:565
  11.6 22.4 %collective-permute-start.6 = (bf16[64,1024]{1,0:T(8,128)(2,1)S(1)}, bf16[64,1024]{1,0:T(8,128)(2,1)S(1)}, u32[]{:S(2)}, u32[]{:S(2)}) collective-permute-start(bf16[64,1024]{1,0:T(8,128)(2,1)S(1)} %get-tuple-element.43), channel_id=1, source_target_pairs={{1,2},{2,1},{5,6},{6,5},{9,10},{10,9},{13,14},{14,13},{17,18},{18,... | collective-permute-start | bytes 393224 | tf_op jit(solution)/shard_map/ppermute | solution.py:565
  20.0 26.0 %collective-permute-start.4 = (bf16[192,1024]{1,0:T(8,128)(2,1)S(1)}, bf16[192,1024]{1,0:T(8,128)(2,1)S(1)}, u32[]{:S(2)}, u32[]{:S(2)}) collective-permute-start(bf16[192,1024]{1,0:T(8,128)(2,1)S(1)} %collective-permute-done.3.far), channel_id=1, source_target_pairs={{1,0},{2,3},{5,4},{6,7},{9,8},{10,11},{13,12},{14,15},{17,16},{18,... | collective-permute-start | bytes 1179656 | tf_op jit(solution)/shard_map/ppermute | solution.py:565
  21.3 20.3 %collective-permute-start.7 = (bf16[64,1024]{1,0:T(8,128)(2,1)S(1)}, bf16[64,1024]{1,0:T(8,128)(2,1)S(1)}, u32[]{:S(2)}, u32[]{:S(2)}) collective-permute-start(bf16[64,1024]{1,0:T(8,128)(2,1)S(1)} %get-tuple-element.32.last), channel_id=1, source_target_pairs={{0,2},{3,1},{4,6},{7,5},{8,10},{11,9},{12,14},{15,13},{16,18},{19,... | collective-permute-start | bytes 393224 | tf_op jit(solution)/shard_map/ppermute | solution.py:565
  34.1 7.6 %collective-permute-start.5 = (bf16[64,1024]{1,0:T(8,128)(2,1)S(1)}, bf16[64,1024]{1,0:T(8,128)(2,1)S(1)}, u32[]{:S(2)}, u32[]{:S(2)}) collective-permute-start(bf16[64,1024]{1,0:T(8,128)(2,1)S(1)} %get-tuple-element.32.last), channel_id=1, source_target_pairs={{0,1},{3,2},{4,5},{7,6},{8,9},{11,10},{12,13},{15,14},{16,17},{19,... | collective-permute-start | bytes 393224 | tf_op jit(solution)/shard_map/ppermute | solution.py:565
  36.2 0.7 %copy-start = (s32[64]{0:T(128)S(1)}, s32[64]{0:T(128)}, u32[]{:S(2)}) copy-start(s32[64]{0:T(128)} %source_hbm.1) | copy-start | bytes 772
  36.8 0.7 %copy-start.1 = (s32[64]{0:T(128)S(1)}, s32[64]{0:T(128)}, u32[]{:S(2)}) copy-start(s32[64]{0:T(128)} %utt_ref.1) | copy-start | bytes 772

commit v7 on v5

--- a/solution.py
+++ b/solution.py
@@ -463,12 +463,22 @@
     value_ref[...] = project(normed, value_weight)
 
 
-def middle_kernel(*refs):
+def middle_kernel(me_ref, *refs):
+    me = me_ref[0]
+    is_end = (me == 0) | (me == COUNT - 1)
     parts, (key_weight, value_weight, key_ref, value_ref) = refs[:-4], refs[-4:]
-    rows = jnp.concatenate([part[...] for part in parts], axis=0)
-    normed = layer_norm(rows).astype(jnp.bfloat16)
-    key_ref[...] = project(normed, key_weight)
-    value_ref[...] = project(normed, value_weight)
+
+    @pl.when(is_end)
+    def _():
+        key_ref[...] = jnp.zeros_like(key_ref)
+        value_ref[...] = jnp.zeros_like(value_ref)
+
+    @pl.when(jnp.logical_not(is_end))
+    def _():
+        rows = jnp.concatenate([part[...] for part in parts], axis=0)
+        normed = layer_norm(rows).astype(jnp.bfloat16)
+        key_ref[...] = project(normed, key_weight)
+        value_ref[...] = project(normed, value_weight)
 
 
 def final_kernel(
@@ -599,12 +609,12 @@
     middle_key, middle_value = pl.pallas_call(
         middle_kernel,
         out_shape=(shape(3 * quarter, wide),) * 2,
-        in_specs=[VMEM] * 5,
+        in_specs=[SMEM] + [VMEM] * 5,
         out_specs=(VMEM,) * 2,
         compiler_params=params(8),
         cost_estimate=cost(3 * quarter),
         name="middle_call",
-    )(near_last, inner_start, far_last, key_weight, value_weight)
+    )(me, near_last, inner_start, far_last, key_weight, value_weight)
     return pl.pallas_call(
         final_kernel,
         out_shape=(shape(rows_dev), shape(held_rows), padded_shape),

time: 55.4 us -> 54.7 us (0.987)
  Pallas kernels: 19.4 us -> 18.7 us
    pallas_call x1, Pallas kernels: 0.78 us -> 0.04 us  [line_block(): pl.pallas_call(middle_kernel, out_shape=(shape(3 * quarter, wide),) * 2,...]
  transfers between devices with their start and end apart: 8 -> 8, of which waited for: 1 -> 1; matrix products, arithmetic and copies ran while one was open for 0% -> 0% of each run, Pallas kernels for 17% -> 15%
where the time goes in v7:
time: 54.7 us; the launch traced here: 54.4 us
  starting transfers between devices  26.5 us (48%)
  Pallas kernels  18.7 us (34%)
  waiting for transfers between devices  7.73 us (14%)
  local copies, waits for them, and re-layouts  1.31 us (2%)
    ppermute x8, starting transfers between devices, swap(): return lax.ppermute(value, 'ctx', perm)  26.5 us
    pallas_call x1, Pallas kernels, line_block(): pl.pallas_call(final_kernel, out_shape=(shape(rows_dev), shape(held_rows)...  8.36 us
    ppermute x8, waiting for transfers between devices, swap(): return lax.ppermute(value, 'ctx', perm)  7.73 us
    pallas_call x1, Pallas kernels, line_block(): pl.pallas_call(early_kernel, out_shape=(shape(early_rows, wide), shape(ea...  2.82 us
    pallas_call x1, Pallas kernels, hold(): pl.pallas_call(hold_kernel, out_shape=tuple((pltpu.VMEM(a.shape, a.dtype)...  2.26 us
    pallas_call x1, Pallas kernels, line_block(): pl.pallas_call(arrange_kernel, out_shape=tuple((pltpu.VMEM((n, width), fr...  1.87 us
    pallas_call x1, Pallas kernels, line_block(): pl.pallas_call(tables_kernel, out_shape=(jax.ShapeDtypeStruct((plan_sizes...  1.84 us
    pallas_call x1, Pallas kernels, line_block(): pl.pallas_call(second_kernel, out_shape=(shape(piece, wide), shape(piece,...  1.48 us
  transfers between devices with their start and end apart: 8, of which 1 were waited for; matrix products, arithmetic and copies ran while one was open for 0% of the time, Pallas kernels for 15%

profile of v7, /device:TPU:0, one launch (start us, length us, event | category | flops | bytes accessed | tf_op | source)
XLA Modules:
  0.0 54.4 jit_solution(707516149103545841)
XLA Ops:
  0.0 1.9 %arrange.1 = (bf16[192,1024]{1,0:T(8,128)(2,1)}, bf16[64,1024]{1,0:T(8,128)(2,1)S(1)}, bf16[192,1024]{1,0:T(8,128)(2,1)S(1)}, bf16[64,1024]{1,0:T(8,128)(2,1)S(1)}) custom-call(s32[1]{0:T(128)} %bitcast.me_ref, s32[64]{0:T(128)} %source_hbm.1, bf16[256,1024]{1,0:T(8,128)(2,1)} %rows_hbm.1), custom_call_target="tpu_custom_call" | custom-call | tf_op jit(solution)/shard_map/arrange/pallas_call | solution.py:538
  1.9 0.7 %collective-permute-start.1 = (bf16[192,1024]{1,0:T(8,128)(2,1)S(1)}, bf16[192,1024]{1,0:T(8,128)(2,1)S(1)}, u32[]{:S(2)}, u32[]{:S(2)}) collective-permute-start(bf16[192,1024]{1,0:T(8,128)(2,1)S(1)} %get-tuple-element.36), channel_id=1, source_target_pairs={{1,2},{2,1},{5,6},{6,5},{9,10},{10,9},{13,14},{14,13},{17,18},{18,... | collective-permute-start | bytes 1179656 | tf_op jit(solution)/shard_map/ppermute | solution.py:554
  2.6 7.7 %collective-permute-start.3 = (bf16[192,1024]{1,0:T(8,128)(2,1)}, bf16[192,1024]{1,0:T(8,128)(2,1)S(1)}, u32[]{:S(2)}, u32[]{:S(2)}) collective-permute-start(bf16[192,1024]{1,0:T(8,128)(2,1)} %get-tuple-element.31.low), channel_id=1, source_target_pairs={{0,2},{3,1},{4,6},{7,5},{8,10},{11,9},{12,14},{15,13},{16,18},{19,... | collective-permute-start | bytes 1179656 | tf_op jit(solution)/shard_map/ppermute | solution.py:554
  10.2 0.1 collective-permute-start
  10.3 0.0 collective-permute-done.1.inner
  10.3 1.3 %collective-permute-start.2 = (bf16[192,1024]{1,0:T(8,128)(2,1)S(1)}, bf16[192,1024]{1,0:T(8,128)(2,1)S(1)}, u32[]{:S(2)}, u32[]{:S(2)}) collective-permute-start(bf16[192,1024]{1,0:T(8,128)(2,1)S(1)} %collective-permute-done.1.inner), channel_id=1, source_target_pairs={{1,0},{2,3},{5,4},{6,7},{9,8},{10,11},{13,12},{14,15},{17,16},{18,... | collective-permute-start | bytes 1179656 | tf_op jit(solution)/shard_map/ppermute | solution.py:554
  11.6 0.7 %collective-permute-start.6 = (bf16[64,1024]{1,0:T(8,128)(2,1)S(1)}, bf16[64,1024]{1,0:T(8,128)(2,1)S(1)}, u32[]{:S(2)}, u32[]{:S(2)}) collective-permute-start(bf16[64,1024]{1,0:T(8,128)(2,1)S(1)} %get-tuple-element.43), channel_id=1, source_target_pairs={{1,2},{2,1},{5,6},{6,5},{9,10},{10,9},{13,14},{14,13},{17,18},{18,... | collective-permute-start | bytes 393224 | tf_op jit(solution)/shard_map/ppermute | solution.py:554
  12.3 7.7 %collective-permute-done.3.far = bf16[192,1024]{1,0:T(8,128)(2,1)S(1)} collective-permute-done((bf16[192,1024]{1,0:T(8,128)(2,1)}, bf16[192,1024]{1,0:T(8,128)(2,1)S(1)}, u32[]{:S(2)}, u32[]{:S(2)}) %collective-permute-start.3) | collective-permute-done | bytes 393248 | tf_op jit(solution)/shard_map/ppermute | solution.py:554
  20.0 1.3 %collective-permute-start.4 = (bf16[192,1024]{1,0:T(8,128)(2,1)S(1)}, bf16[192,1024]{1,0:T(8,128)(2,1)S(1)}, u32[]{:S(2)}, u32[]{:S(2)}) collective-permute-start(bf16[192,1024]{1,0:T(8,128)(2,1)S(1)} %collective-permute-done.3.far), channel_id=1, source_target_pairs={{1,0},{2,3},{5,4},{6,7},{9,8},{10,11},{13,12},{14,15},{17,16},{18,... | collective-permute-start | bytes 1179656 | tf_op jit(solution)/shard_map/ppermute | solution.py:554
  21.3 12.7 %collective-permute-start.7 = (bf16[64,1024]{1,0:T(8,128)(2,1)S(1)}, bf16[64,1024]{1,0:T(8,128)(2,1)S(1)}, u32[]{:S(2)}, u32[]{:S(2)}) collective-permute-start(bf16[64,1024]{1,0:T(8,128)(2,1)S(1)} %get-tuple-element.32.last), channel_id=1, source_target_pairs={{0,2},{3,1},{4,6},{7,5},{8,10},{11,9},{12,14},{15,13},{16,18},{19,... | collective-permute-start | bytes 393224 | tf_op jit(solution)/shard_map/ppermute | solution.py:554
  34.0 0.0 collective-permute-done.6.refs_1_
  34.1 2.1 %collective-permute-start.5 = (bf16[64,1024]{1,0:T(8,128)(2,1)S(1)}, bf16[64,1024]{1,0:T(8,128)(2,1)S(1)}, u32[]{:S(2)}, u32[]{:S(2)}) collective-permute-start(bf16[64,1024]{1,0:T(8,128)(2,1)S(1)} %get-tuple-element.32.last), channel_id=1, source_target_pairs={{0,1},{3,2},{4,5},{7,6},{8,9},{11,10},{12,13},{15,14},{16,17},{19,... | collective-permute-start | bytes 393224 | tf_op jit(solution)/shard_map/ppermute | solution.py:554
  36.2 0.0 copy-start
  36.2 0.6 %copy-done = s32[64]{0:T(128)S(1)} copy-done((s32[64]{0:T(128)S(1)}, s32[64]{0:T(128)}, u32[]{:S(2)}) %copy-start) | copy-done | bytes 280
  36.8 0.7 %copy-done.1 = s32[64]{0:T(128)S(1)} copy-done((s32[64]{0:T(128)S(1)}, s32[64]{0:T(128)}, u32[]{:S(2)}) %copy-start.1) | copy-done | bytes 280
  37.5 1.8 %tables_call.1 = (s32[88]{0:T(128)S(1)}, s32[1,1024]{1,0:T(1,128)S(1)}, s32[288,128]{1,0:T(8,128)S(1)}, f32[8,384,128]{2,1,0:T(8,128)S(1)}) custom-call(s32[1]{0:T(128)} %bitcast.me_ref, s32[64]{0:T(128)S(1)} %copy-done, s32[64]{0:T(128)S(1)} %copy-done.1), custom_call_target="tpu_custom_call" | custom-call | tf_op jit(solution)/shard_map/tables_call/pallas_call | solution.py:562
  39.3 2.3 %hold_call.1 = (bf16[1024,512]{1,0:T(8,128)(2,1)S(1)}, bf16[1024,512]{1,0:T(8,128)(2,1)S(1)}, bf16[1024,512]{1,0:T(8,128)(2,1)S(1)}, bf16[512,1024]{1,0:T(8,128)...) custom-call(bf16[1024,512]{1,0:T(8,128)(2,1)} %refs_0_.1, bf16[1024,512]{1,0:T(8,128)(2,1)} %refs_1_.1, ...), custom_call_target="tpu_custom_call" | custom-call | bytes 8388608 | tf_op jit(solution)/shard_map/hold_call/pallas_call | solution.py:335
  41.6 0.0 collective-permute-done.7.refs_2_
  41.6 0.0 collective-permute-done.5.refs_0_.near_last
  41.7 0.0 collective-permute-done.near
  41.7 2.8 %early_call.1 = (bf16[448,512]{1,0:T(8,128)(2,1)S(1)}, bf16[448,512]{1,0:T(8,128)(2,1)S(1)}, bf16[288,1024]{1,0:T(8,128)(2,1)S(1)}) custom-call(s32[88]{0:T(128)S(1)} %get-tuple-element.28.plan, bf16[192,1024]{1,0:T(8,128)(2,1)} %get-tuple-element.31.low, bf16[64,1024]{1,0:T(8,128)(2,1)S(1)} %get-tuple-element.32.last, ...), custom_call_target="tpu_custom_call" | custom-call | flops 939524096 | bytes 1835008 | tf_op jit(solution)/shard_map/early_call/pallas_call | solution.py:588
  44.5 0.0 collective-permute-done.2.inner_end
  44.5 1.5 %second_call.1 = (bf16[192,512]{1,0:T(8,128)(2,1)S(1)}, bf16[192,512]{1,0:T(8,128)(2,1)S(1)}, bf16[288,1024]{1,0:T(8,128)(2,1)S(1)}) custom-call(s32[1]{0:T(128)} %bitcast.me_ref, s32[88]{0:T(128)S(1)} %get-tuple-element.28.plan, bf16[288,1024]{1,0:T(8,128)(2,1)S(1)} %get-tuple-element.35.early_grouped, ...), custom_call_target="tpu_custom_call", output_to_operand_aliasing={{2}: (2, {})} | custom-call | flops 402653184 | bytes 786432 | tf_op jit(solution)/shard_map/second_call/pallas_call | solution.py:598
  46.0 8.4 %final.1 = (bf16[256,1024]{1,0:T(8,128)(2,1)}, bf16[288,1024]{1,0:T(8,128)(2,1)S(1)}, f32[8,384,128]{2,1,0:T(8,128)S(1)}) custom-call(s32[1]{0:T(128)} %bitcast.me_ref, s32[88]{0:T(128)S(1)} %get-tuple-element.28.plan, s32[288,128]{1,0:T(8,128)S(1)} %get-tuple-element.29.query_utt, ...), custom_call_target="tpu_custom_call", output_to_operand_aliasing={{1}: (4, {}), {2}: (5, {})} | custom-call | flops 2147483648 | bytes 8388608 | tf_op jit(solution)/shard_map/final/pallas_call | solution.py:618
  (3 shorter events, 0.0 us)
Async XLA Ops:
  1.9 8.4 %collective-permute-start.1 = (bf16[192,1024]{1,0:T(8,128)(2,1)S(1)}, bf16[192,1024]{1,0:T(8,128)(2,1)S(1)}, u32[]{:S(2)}, u32[]{:S(2)}) collective-permute-start(bf16[192,1024]{1,0:T(8,128)(2,1)S(1)} %get-tuple-element.36), channel_id=1, source_target_pairs={{1,2},{2,1},{5,6},{6,5},{9,10},{10,9},{13,14},{14,13},{17,18},{18,... | collective-permute-start | bytes 1179656 | tf_op jit(solution)/shard_map/ppermute | solution.py:554
  2.6 17.5 %collective-permute-start.3 = (bf16[192,1024]{1,0:T(8,128)(2,1)}, bf16[192,1024]{1,0:T(8,128)(2,1)S(1)}, u32[]{:S(2)}, u32[]{:S(2)}) collective-permute-start(bf16[192,1024]{1,0:T(8,128)(2,1)} %get-tuple-element.31.low), channel_id=1, source_target_pairs={{0,2},{3,1},{4,6},{7,5},{8,10},{11,9},{12,14},{15,13},{16,18},{19,... | collective-permute-start | bytes 1179656 | tf_op jit(solution)/shard_map/ppermute | solution.py:554
  10.2 31.4 %collective-permute-start = (bf16[192,1024]{1,0:T(8,128)(2,1)}, bf16[192,1024]{1,0:T(8,128)(2,1)}, u32[]{:S(2)}, u32[]{:S(2)}) collective-permute-start(bf16[192,1024]{1,0:T(8,128)(2,1)} %get-tuple-element.31.low), channel_id=1, source_target_pairs={{0,1},{1,0},{2,3},{3,2},{4,5},{5,4},{6,7},{7,6},{8,9},{9,8},{10,11... | collective-permute-start | bytes 1179656 | tf_op jit(solution)/shard_map/ppermute | solution.py:554
  10.3 34.2 %collective-permute-start.2 = (bf16[192,1024]{1,0:T(8,128)(2,1)S(1)}, bf16[192,1024]{1,0:T(8,128)(2,1)S(1)}, u32[]{:S(2)}, u32[]{:S(2)}) collective-permute-start(bf16[192,1024]{1,0:T(8,128)(2,1)S(1)} %collective-permute-done.1.inner), channel_id=1, source_target_pairs={{1,0},{2,3},{5,4},{6,7},{9,8},{10,11},{13,12},{14,15},{17,16},{18,... | collective-permute-start | bytes 1179656 | tf_op jit(solution)/shard_map/ppermute | solution.py:554
  11.6 22.4 %collective-permute-start.6 = (bf16[64,1024]{1,0:T(8,128)(2,1)S(1)}, bf16[64,1024]{1,0:T(8,128)(2,1)S(1)}, u32[]{:S(2)}, u32[]{:S(2)}) collective-permute-start(bf16[64,1024]{1,0:T(8,128)(2,1)S(1)} %get-tuple-element.43), channel_id=1, source_target_pairs={{1,2},{2,1},{5,6},{6,5},{9,10},{10,9},{13,14},{14,13},{17,18},{18,... | collective-permute-start | bytes 393224 | tf_op jit(solution)/shard_map/ppermute | solution.py:554
  20.0 26.0 %collective-permute-start.4 = (bf16[192,1024]{1,0:T(8,128)(2,1)S(1)}, bf16[192,1024]{1,0:T(8,128)(2,1)S(1)}, u32[]{:S(2)}, u32[]{:S(2)}) collective-permute-start(bf16[192,1024]{1,0:T(8,128)(2,1)S(1)} %collective-permute-done.3.far), channel_id=1, source_target_pairs={{1,0},{2,3},{5,4},{6,7},{9,8},{10,11},{13,12},{14,15},{17,16},{18,... | collective-permute-start | bytes 1179656 | tf_op jit(solution)/shard_map/ppermute | solution.py:554
  21.3 20.3 %collective-permute-start.7 = (bf16[64,1024]{1,0:T(8,128)(2,1)S(1)}, bf16[64,1024]{1,0:T(8,128)(2,1)S(1)}, u32[]{:S(2)}, u32[]{:S(2)}) collective-permute-start(bf16[64,1024]{1,0:T(8,128)(2,1)S(1)} %get-tuple-element.32.last), channel_id=1, source_target_pairs={{0,2},{3,1},{4,6},{7,5},{8,10},{11,9},{12,14},{15,13},{16,18},{19,... | collective-permute-start | bytes 393224 | tf_op jit(solution)/shard_map/ppermute | solution.py:554
  34.1 7.6 %collective-permute-start.5 = (bf16[64,1024]{1,0:T(8,128)(2,1)S(1)}, bf16[64,1024]{1,0:T(8,128)(2,1)S(1)}, u32[]{:S(2)}, u32[]{:S(2)}) collective-permute-start(bf16[64,1024]{1,0:T(8,128)(2,1)S(1)} %get-tuple-element.32.last), channel_id=1, source_target_pairs={{0,1},{3,2},{4,5},{7,6},{8,9},{11,10},{12,13},{15,14},{16,17},{19,... | collective-permute-start | bytes 393224 | tf_op jit(solution)/shard_map/ppermute | solution.py:554
  36.2 0.7 %copy-start = (s32[64]{0:T(128)S(1)}, s32[64]{0:T(128)}, u32[]{:S(2)}) copy-start(s32[64]{0:T(128)} %source_hbm.1) | copy-start | bytes 772
  36.8 0.7 %copy-start.1 = (s32[64]{0:T(128)S(1)}, s32[64]{0:T(128)}, u32[]{:S(2)}) copy-start(s32[64]{0:T(128)} %utt_ref.1) | copy-start | bytes 772
